TPU v7x, 128 devices: a whole 4x4x4 slice. The times are simulated.
128 devices in a mesh: seq: 32 (over y, z, core), head: 4 (over x).
Axes of the slice: x: 4, y: 4, z: 4, core: 2. Of those that a mesh axis runs over, the one named last changes fastest.
Arguments:
- image_patches: bfloat16 [32, 256, 1152], P('seq', None, 'head'), may hold values from -6 to 6
- text_embed: bfloat16 [8192, 2048], P('seq', 'head'), may hold values from -6 to 6
- image_start: int32 [32], replicated, may hold values from 0 to 126, as said below
- image_forget: float32 [32], replicated, may hold values from 0.001 to 0.3
- adapter: bfloat16 [1152, 2048], P('head'), may hold values from -0.1875 to 0.1875
- norm_gain: float32 [2048], replicated, may hold values from 0.5 to 1.5
- in_proj: bfloat16 [2048, 4, 2048], P(None, None, 'head'), may hold values from -0.125 to 0.125
- decay_proj: bfloat16 [2048, 16], P(None, 'head'), may hold values from -0.125 to 0.125
- head_decay_ceiling: float32 [16], P('head'), may hold values from 0 to 1, as said below
- out_gain: float32 [16, 128], P('head'), may hold values from 0.5 to 1.5
- out_proj: bfloat16 [2048, 2048], P('head'), may hold values from -0.125 to 0.125
Outputs:
- image_out: bfloat16 [32, 256, 2048], P('seq', None, 'head')
- text_out: bfloat16 [8192, 2048], P('seq', 'head')
Inputs may be any that keep to these rules, and one draw needn't show every extreme that they name: `image_start`: each entry is even; the images take distinct pairs of blocks. The merged piece of 512 tokens on one device of seq never holds both the image and the text that one device of seq holds in the source layout. `head_decay_ceiling`: Positive.
All inputs are finite; a program needn't handle non-finite values.
Results may differ from a plain program's by a relative error of at most 0.0095.
Values may be sent and summed in bfloat16 or wider, within the bound.
No kernel may reach another device: no remote copies, remote signals or barrier semaphores. Data moves between devices by JAX's collectives and lax.ppermute only.
A program may use at most 128 MiB of HBM per device.

v0:
```python
import jax
import jax.numpy as jnp
from jax import lax
from jax.sharding import Mesh
from jax.sharding import PartitionSpec as P

SEQ = ("seq_0", "seq_1", "seq_2")


EPSILON = 1e-06


def split_up(array, dim, length):
    shape = array.shape
    pieces = array.reshape(*shape[:dim], length, shape[dim] // length, *shape[dim + 1 :])
    return jnp.moveaxis(pieces, dim, 0)


def sent_and_summed(array, axis, dim):
    pieces = split_up(array, dim, lax.axis_size(axis))
    arrived = lax.all_to_all(pieces, axis, split_axis=0, concat_axis=0, tiled=True)
    return arrived.sum(axis=0)


def in_order(pieces, dim):
    shape = list(pieces.shape[1:])
    shape[dim] *= pieces.shape[0]
    return jnp.moveaxis(pieces, 0, dim).reshape(shape)


def copy_for_each(array, axis):
    length = lax.axis_size(axis)
    return lax.all_to_all(
        jnp.broadcast_to(array[None], (length, *array.shape)), axis, 0, 0, tiled=True
    )


def gathered_copies(array, axis, dim):
    return in_order(copy_for_each(array, axis), dim)


def neutral_like(array, identity):
    return jax.tree.map(
        lambda a, e: jnp.broadcast_to(jnp.asarray(e, a.dtype), a.shape), array, identity
    )


def entering_2(array, axes, combine, identity):
    before = start = neutral_like(array, identity)
    total = array
    for axis in reversed(axes):
        length, position = (lax.axis_size(axis), lax.axis_index(axis))
        pieces = jax.tree.map(
            lambda part, kind: lax.all_gather(part.astype(kind), axis),
            total,
            (jnp.bfloat16, jnp.bfloat16),
        )
        inside, total = (start, start)
        for k in range(length):
            passed = k < position
            total = combine(
                total, jax.tree.map(lambda part, own: part[k].astype(own.dtype), pieces, array)
            )
            inside = jax.tree.map(lambda new, old: jnp.where(passed, new, old), total, inside)
        before = combine(inside, before)
    return before


def sent_and_summed_2(array, axis, dim):
    pieces = split_up(array, dim, lax.axis_size(axis))
    arrived = lax.all_to_all(pieces, axis, split_axis=0, concat_axis=0, tiled=True)
    return arrived.astype(jnp.float32).sum(axis=0)


def rms_scale(values, gain_row):
    mean_square = jnp.mean(values * values, axis=-1, keepdims=True)
    return values * lax.rsqrt(mean_square + EPSILON) * gain_row


def shards(
    image_patches,
    text_embed,
    image_start,
    image_forget,
    adapter,
    norm_gain,
    in_proj,
    decay_proj,
    head_decay_ceiling,
    out_gain,
    out_proj,
):
    seq_count = lax.axis_size(SEQ)
    my_index = lax.axis_index(SEQ)
    patch_row_block = text_embed.shape[0]
    local_width = text_embed.shape[1]
    share_rows = patch_row_block // seq_count
    unit_count = 2 * seq_count
    token_rows = 2 * patch_row_block
    unit_ids = jnp.arange(unit_count, dtype=jnp.int32)
    device_ids = jnp.arange(seq_count, dtype=jnp.int32)
    unit_of_image = image_start // 2
    image_hits = (unit_of_image[:, None] == unit_ids[None, :]).astype(jnp.int32)
    is_image = jnp.sum(image_hits, axis=0)
    image_here = jnp.sum(image_hits * device_ids[:, None], axis=0)
    is_text = 1 - is_image
    text_here = jnp.cumsum(is_text) - is_text
    text_pick = ((is_text[None, :] == 1) & (text_here[None, :] == device_ids[:, None])).astype(
        jnp.int32
    )
    text_unit = jnp.sum(text_pick * unit_ids[None, :], axis=1)
    source = jnp.where(is_image == 1, image_here, text_here)
    my_units = 2 * my_index + jnp.arange(2, dtype=jnp.int32)
    unit_image = jnp.take(is_image, my_units)
    partial_value = jnp.dot(image_patches[0], adapter, preferred_element_type=jnp.float32)
    embedded = sent_and_summed(partial_value, "head", 1).astype(jnp.bfloat16)
    units_here = jnp.stack([embedded, text_embed]).reshape(2, seq_count, share_rows, local_width)
    spread = lax.all_to_all(units_here, SEQ, split_axis=1, concat_axis=1, tiled=True)
    table = spread.reshape(unit_count, share_rows, local_width)
    pick_index = is_text * seq_count + source
    outgoing_units = jnp.take(table, pick_index, axis=0).reshape(
        seq_count, 2, share_rows, local_width
    )
    arrived = lax.all_to_all(outgoing_units, SEQ, split_axis=0, concat_axis=2, tiled=True)
    merged = arrived.reshape(token_rows, local_width)
    full_rows = gathered_copies(merged, "head", 1)
    normed = rms_scale(full_rows.astype(jnp.float32), norm_gain).astype(jnp.bfloat16)
    model_width = in_proj.shape[0]
    head_count = head_decay_ceiling.shape[0]
    head_width = out_gain.shape[1]
    projected = jnp.dot(
        normed, in_proj.reshape(model_width, -1), preferred_element_type=jnp.float32
    )
    projected = projected.astype(jnp.bfloat16).reshape(token_rows, 4, head_count, head_width)
    gate_preactivation = jnp.dot(normed, decay_proj, preferred_element_type=jnp.float32)
    forget_element = jnp.where(
        unit_image == 1, jnp.log1p(-jnp.take(image_forget, jnp.take(image_here, my_units))), 0.0
    )
    start_offsets = jnp.arange(token_rows, dtype=jnp.int32) % patch_row_block == 0
    surge_logarithm = jnp.where(start_offsets, jnp.repeat(forget_element, patch_row_block), 0.0)
    decay_logarithm = (
        -head_decay_ceiling[None, :] * jax.nn.sigmoid(gate_preactivation) + surge_logarithm[:, None]
    )
    queries = projected[:, 0]
    key_rows = projected[:, 1]
    value_rows = projected[:, 2]
    gate_rows = projected[:, 3]
    within = jnp.cumsum(decay_logarithm, axis=0)
    span_decay = within[-1]
    scores = jnp.einsum("thd,shd->hts", queries, key_rows, preferred_element_type=jnp.float32)
    lagged = within.T[:, :, None] - within.T[:, None, :]
    row_ids = jnp.arange(token_rows, dtype=jnp.int32)
    causal = (row_ids[:, None] >= row_ids[None, :])[None]
    weights = jnp.where(causal, scores * jnp.exp(jnp.where(causal, lagged, 0.0)), 0.0).astype(
        jnp.bfloat16
    )
    inner_part = jnp.einsum("hts,shd->thd", weights, value_rows, preferred_element_type=jnp.float32)
    weighted_keys = key_rows.astype(jnp.float32) * jnp.exp(span_decay[None, :] - within)[:, :, None]
    local_state = jnp.einsum("thd,the->hde", weighted_keys, value_rows.astype(jnp.float32))

    def combine(earlier, later_part):
        return (
            earlier[0] + later_part[0],
            jnp.exp(later_part[0])[:, None, None] * earlier[1] + later_part[1],
        )

    identity = (jnp.zeros_like(span_decay), jnp.zeros_like(local_state))
    decay_before, entering = entering_2((span_decay, local_state), SEQ, combine, identity)
    carried = jnp.exp(within)[:, :, None] * jnp.einsum(
        "thd,hde->the", queries.astype(jnp.float32), entering
    )
    attended = inner_part + carried
    gated = rms_scale(attended, out_gain) * jax.nn.silu(gate_rows.astype(jnp.float32))
    gated = gated.astype(jnp.bfloat16).reshape(token_rows, -1)
    partial_out = jnp.dot(gated, out_proj, preferred_element_type=jnp.float32)
    summed = sent_and_summed_2(partial_out.astype(jnp.bfloat16), "head", 1)
    result = (merged.astype(jnp.float32) + summed).astype(jnp.bfloat16)
    result_shares = result.reshape(2, seq_count, share_rows, local_width)
    back_spread = lax.all_to_all(result_shares, SEQ, split_axis=1, concat_axis=1, tiled=True)
    back_table = back_spread.reshape(unit_count, share_rows, local_width)
    wanted = jnp.stack([unit_of_image, text_unit], axis=1).reshape(-1)
    back_index = wanted % 2 * seq_count + wanted // 2
    outgoing = jnp.take(back_table, back_index, axis=0).reshape(
        seq_count, 2, share_rows, local_width
    )
    returned = lax.all_to_all(outgoing, SEQ, split_axis=0, concat_axis=2, tiled=True)
    image_out = returned[:, 0]
    text_out = returned[0, 1]
    return (image_out, text_out)


def solution(mesh):
    split = Mesh(
        mesh.devices.reshape(4, 4, 2, mesh.shape["head"]), ("seq_0", "seq_1", "seq_2", "head")
    )
    return jax.shard_map(
        shards,
        mesh=split,
        in_specs=(
            P(SEQ, None, "head"),
            P(SEQ, "head"),
            P(),
            P(),
            P("head", None),
            P(),
            P(None, None, "head"),
            P(None, "head"),
            P("head"),
            P("head", None),
            P("head", None),
        ),
        out_specs=(P(SEQ, None, "head"), P(SEQ, "head")),
        check_vma=False,
    )
```

profile of v0, /device:TPU:1, one launch (start us, length us, event | category | flops | bytes accessed | tf_op | source)
XLA Modules:
  0.0 257.9 jit_solution(2699861484524103100)
XLA Ops:
  0.6 3.5 %convolution_bitcast_fusion = f32[4,256,512]{2,1,0:T(8,128)} fusion(bf16[36,4,8,512]{3,2,1,0:T(8,128)(2,1)} %bitcast.304, bf16[1,256,288]{1,2,0:T(8,128)(2,1)} %param.15), kind=kOutput, calls=%fused_computation.15 | convolution fusion | flops 301989888 | bytes 3424256 | tf_op jit(solution)/shard_map/dot_general | solution.py:115
  4.2 5.0 %all-to-all-start = ((f32[4,256,512]{2,1,0:T(8,128)}), f32[4,256,512]{2,1,0:T(8,128)}, u32[]{:S(2)}, u32[]{:S(2)}) async-start(f32[4,256,512]{2,1,0:T(8,128)} %convolution_bitcast_fusion), calls=%async_computation | async-start | bytes 4194304 | tf_op jit(solution)/shard_map/all_to_all | solution.py:21
  9.2 25.9 %all-to-all-done = f32[4,256,512]{2,1,0:T(8,128)} async-done(((f32[4,256,512]{2,1,0:T(8,128)}), f32[4,256,512]{2,1,0:T(8,128)}, u32[]{:S(2)}, u32[]{:S(2)}) %all-to-all-start) | async-done | bytes 2097184 | tf_op jit(solution)/shard_map/all_to_all | solution.py:21
  35.1 1.8 reduce_sum.65
  37.0 0.8 pad_maximum_fusion
  37.8 9.9 %all-to-all-start.1 = ((bf16[2,32,8,512]{3,2,0,1:T(8,128)(2,1)}), bf16[2,32,8,512]{3,2,0,1:T(8,128)(2,1)S(1)}, u32[]{:S(2)}, u32[]{:S(2)}) async-start(bf16[2,32,8,512]{3,2,0,1:T(8,128)(2,1)} %pad_maximum_fusion), calls=%async_computation.1 | async-start | bytes 1048576 | tf_op jit(solution)/shard_map/all_to_all | solution.py:118
  48.1 11.2 %all-to-all-done.1 = bf16[2,32,8,512]{3,2,0,1:T(8,128)(2,1)S(1)} async-done(((bf16[2,32,8,512]{3,2,0,1:T(8,128)(2,1)}), bf16[2,32,8,512]{3,2,0,1:T(8,128)(2,1)S(1)}, u32[]{:S(2)}, u32[]{:S(2)}) %all-to-all-start.1) | async-done | bytes 524320 | tf_op jit(solution)/shard_map/all_to_all | solution.py:118
  59.3 0.6 gather_fusion.1
  60.1 15.0 %all_to_all.58 = bf16[32,2,8,512]{3,2,1,0:T(8,128)(2,1)S(1)} all-to-all(bf16[32,2,8,512]{3,2,1,0:T(8,128)(2,1)S(1)} %bitcast.299), channel_id=1, replica_groups=mesh['seq_0'=4,'seq_1'=4,'seq_2'=2,'head'=4] {'seq_0','seq_1','seq_2'}, dimensions={0} | all-to-all | bytes 1048576 | tf_op jit(solution)/shard_map/all_to_all | solution.py:124
  75.1 0.8 copy.136
  75.9 1.3 copy.137
  77.2 1.5 broadcast_in_dim.53
  78.7 4.8 %all-to-all-start.3 = ((bf16[4,512,512]{1,2,0:T(8,128)(2,1)}), bf16[4,512,512]{1,2,0:T(8,128)(2,1)}, u32[]{:S(2)}, u32[]{:S(2)}) async-start(bf16[4,512,512]{1,2,0:T(8,128)(2,1)} %broadcast_in_dim.53), calls=%async_computation.3 | async-start | bytes 4194304 | tf_op jit(solution)/shard_map/all_to_all | solution.py:33
  83.5 0.6 gather_fusion.3
  84.2 0.6 gather_fusion.2
  84.8 0.6 gather_fusion
  85.6 10.2 %copy.158 = bf16[256,8,4,512]{3,1,2,0:T(8,128)(2,1)} copy(bf16[256,8,4,512]{3,2,1,0:T(4,128)(2,1)} %bitcast.292) | data formatting | bytes 16777216
  95.8 0.8 iota_compare_fusion
  96.6 13.5 %all-to-all-done.3 = bf16[4,512,512]{1,2,0:T(8,128)(2,1)} async-done(((bf16[4,512,512]{1,2,0:T(8,128)(2,1)}), bf16[4,512,512]{1,2,0:T(8,128)(2,1)}, u32[]{:S(2)}, u32[]{:S(2)}) %all-to-all-start.3) | async-done | bytes 2097184 | tf_op jit(solution)/shard_map/all_to_all | solution.py:33
  110.1 2.1 multiply_reduce_fusion
  112.2 2.1 fusion.1
  114.8 1.2 reduce-window.18
  116.8 2.2 multiply_convert_fusion
  119.0 9.1 %convolution_convert_fusion.1 = bf16[512,2048]{1,0:T(8,128)(2,1)} fusion(bf16[512,2048]{0,1:T(8,128)(2,1)S(1)} %bitcast.303, bf16[2048,2048]{1,0:T(8,128)(2,1)} %bitcast.293), kind=kOutput, calls=%fused_computation.13 | convolution fusion | flops 4296015872 | bytes 12582912 | tf_op jit(solution)/shard_map/dot_general | solution.py:131
  128.1 4.4 %reshape.369 = bf16[512,4,4,128]{3,2,1,0:T(4,128)(2,1)} reshape(bf16[512,2048]{1,0:T(8,128)(2,1)} %convolution_convert_fusion.1) | data formatting | bytes 4194304 | tf_op jit(solution)/shard_map/reshape | solution.py:134
  132.6 3.2 %fusion.128 = (bf16[512,1,4,128]{3,2,1,0:T(4,128)(2,1)}, bf16[512,1,4,128]{3,2,1,0:T(4,128)(2,1)}, bf16[512,1,4,128]{3,2,1,0:T(4,128)(2,1)S(1)}, bf16[512,1,4,128]{3,2,1,0:T(4,128)(2,1)}) fusion(bf16[512,4,4,128]{3,2,1,0:T(4,128)(2,1)} %reshape.369), kind=kLoop, calls=%fused_computation.240 | loop fusion | bytes 4194304 | tf_op jit(solution)/shard_map/slice | solution.py:147
  135.8 1.1 copy.152
  136.9 1.9 convolution_convert_fusion.2
  138.8 2.2 all-gather
  141.0 1.8 all-gather.1
  143.0 9.9 %all_gather.31 = bf16[4,4,128,128]{3,2,1,0:T(8,128)(2,1)S(1)} all-gather(bf16[1,4,128,128]{3,2,1,0:T(8,128)(2,1)S(1)} %fusion.52), channel_id=1, replica_groups=mesh['seq_0'=4,'seq_1'=4,'seq_2'=2,'head'=4] {'seq_1'}, dimensions={0}, use_global_device_ids=true | all-gather | bytes 655360 | tf_op jit(solution)/shard_map/all_gather | solution.py:54
  152.9 6.5 %all-gather.2 = bf16[4,1,4]{2,1,0:T(2,128)(2,1)S(1)} all-gather(bf16[1,1,4]{2,1,0:T(2,128)(2,1)S(1)} %get-tuple-element.32), channel_id=1, replica_groups=mesh['seq_0'=4,'seq_1'=4,'seq_2'=2,'head'=4] {'seq_1'}, dimensions={0}, use_global_device_ids=true | all-gather | bytes 40 | tf_op jit(solution)/shard_map/all_gather | solution.py:54
  159.6 11.5 %all_gather.32 = bf16[4,4,128,128]{3,2,1,0:T(8,128)(2,1)} all-gather(bf16[1,4,128,128]{3,2,1,0:T(8,128)(2,1)S(1)} %fusion.46), channel_id=1, replica_groups=mesh['seq_0'=4,'seq_1'=4,'seq_2'=2,'head'=4] {'seq_0'}, dimensions={0}, use_global_device_ids=true | all-gather | bytes 655360 | tf_op jit(solution)/shard_map/all_gather | solution.py:54
  171.1 6.6 %all-gather.3 = bf16[4,1,4]{2,1,0:T(2,128)(2,1)S(1)} all-gather(bf16[1,1,4]{2,1,0:T(2,128)(2,1)S(1)} %get-tuple-element.26), channel_id=1, replica_groups=mesh['seq_0'=4,'seq_1'=4,'seq_2'=2,'head'=4] {'seq_0'}, dimensions={0}, use_global_device_ids=true | all-gather | bytes 40 | tf_op jit(solution)/shard_map/all_gather | solution.py:54
  177.7 4.4 %fusion.3 = f32[512,4,128]{0,2,1:T(8,128)} fusion(f32[4,512]{1,0:T(4,128)S(1)} %bitcast.310, pred[512,512]{1,0:T(8,128)(4,1)} %iota_compare_fusion, bf16[512,1,4,128]{0,3,2,1:T(8,128)(2,1)} %copy.152, bf16[512,1,4,128]{3,2,1,0:T(4,128)(2,1)} %get-tuple-element.13, bf16[512,1,4,128]{3,2,1,0:T(4,128)(2,1)} %get-tuple-element.15), kind=kOutput, calls=%fused_computation.17 | convolution fusion | flops 542113792 | bytes 2891776 | tf_op jit(solution)/shard_map/hts,shd->thd/dot_general | solution.py:157
  182.1 3.4 %multiply_reduce_fusion.1 = (f32[512,4]{0,1:T(4,128)S(1)}, f32[512,4,128]{0,2,1:T(8,128)}) fusion(f32[512,4,128]{0,2,1:T(8,128)} %fusion.3, bf16[512,1,4,128]{3,2,1,0:T(4,128)(2,1)} %get-tuple-element.13, bf16[4,4,128,128]{3,2,1,0:T(8,128)(2,1)} %all_gather.32, f32[4]{0:T(128)S(1)} %get-tuple-element.33, f32[4]{0:T(128)S(1)} %get-tuple-element.31, ...), kind=kOutput, calls=%fused_computation.39 | convolution fusion | flops 70842368 | bytes 3948746 | tf_op jit(solution)/shard_map/thd,hde->the/dot_general | solution.py:169
  185.5 1.3 copy.155
  186.8 1.6 fusion.21
  188.4 1.3 convolution_convert_fusion
  189.7 1.5 copy.187
  191.2 4.4 %all-to-all-start.4 = ((bf16[4,512,512]{2,1,0:T(8,128)(2,1)}), bf16[4,512,512]{2,1,0:T(8,128)(2,1)}, u32[]{:S(2)}, u32[]{:S(2)}) async-start(bf16[4,512,512]{2,1,0:T(8,128)(2,1)} %bitcast.294), calls=%async_computation.4 | async-start | bytes 4194304 | tf_op jit(solution)/shard_map/all_to_all | solution.py:71
  195.7 16.7 %all-to-all-done.4 = bf16[4,512,512]{2,1,0:T(8,128)(2,1)} async-done(((bf16[4,512,512]{2,1,0:T(8,128)(2,1)}), bf16[4,512,512]{2,1,0:T(8,128)(2,1)}, u32[]{:S(2)}, u32[]{:S(2)}) %all-to-all-start.4) | async-done | bytes 2097184 | tf_op jit(solution)/shard_map/all_to_all | solution.py:71
  212.4 2.0 convert_reduce_fusion
  214.5 1.0 fusion.18
  215.4 14.1 %all-to-all-start.5 = ((bf16[2,32,8,512]{3,2,0,1:T(8,128)(2,1)}), bf16[2,32,8,512]{3,2,0,1:T(8,128)(2,1)S(1)}, u32[]{:S(2)}, u32[]{:S(2)}) async-start(bf16[2,32,8,512]{3,2,0,1:T(8,128)(2,1)} %fusion.18), calls=%async_computation.5 | async-start | bytes 1048576 | tf_op jit(solution)/shard_map/all_to_all | solution.py:179
  229.9 11.3 %all-to-all-done.5 = bf16[2,32,8,512]{3,2,0,1:T(8,128)(2,1)S(1)} async-done(((bf16[2,32,8,512]{3,2,0,1:T(8,128)(2,1)}), bf16[2,32,8,512]{3,2,0,1:T(8,128)(2,1)S(1)}, u32[]{:S(2)}, u32[]{:S(2)}) %all-to-all-start.5) | async-done | bytes 524320 | tf_op jit(solution)/shard_map/all_to_all | solution.py:179
  242.0 15.0 %all_to_all.59 = bf16[32,2,8,512]{3,2,1,0:T(8,128)(2,1)S(1)} all-to-all(bf16[32,2,8,512]{3,2,1,0:T(8,128)(2,1)S(1)} %bitcast.301), channel_id=1, replica_groups=mesh['seq_0'=4,'seq_1'=4,'seq_2'=2,'head'=4] {'seq_0','seq_1','seq_2'}, dimensions={0} | all-to-all | bytes 1048576 | tf_op jit(solution)/shard_map/all_to_all | solution.py:186
  257.1 0.8 slice_bitcast_fusion
  (66 shorter events, 3.6 us)
Async XLA Ops:
  0.6 187.8 %copy-start = (bf16[512,2048]{1,0:T(8,128)(2,1)S(1)}, bf16[512,2048]{1,0:T(8,128)(2,1)}, u32[]{:S(2)}) copy-start(bf16[512,2048]{1,0:T(8,128)(2,1)} %param.25) | copy-start | bytes 6291460
  4.2 5.0 %copy-start.7 = (s32[32]{0:T(128)S(1)}, s32[32]{0:T(128)}, u32[]{:S(2)}) copy-start(s32[32]{0:T(128)} %param.17) | copy-start | bytes 388
  4.2 30.9 %all-to-all-start = ((f32[4,256,512]{2,1,0:T(8,128)}), f32[4,256,512]{2,1,0:T(8,128)}, u32[]{:S(2)}, u32[]{:S(2)}) async-start(f32[4,256,512]{2,1,0:T(8,128)} %convolution_bitcast_fusion), calls=%async_computation | async-start | bytes 4194304 | tf_op jit(solution)/shard_map/all_to_all | solution.py:21
  9.1 27.8 %copy-start.2 = (bf16[256,512]{1,0:T(8,128)(2,1)S(1)}, bf16[256,512]{1,0:T(8,128)(2,1)}, u32[]{:S(2)}) copy-start(bf16[256,512]{1,0:T(8,128)(2,1)} %param.16) | copy-start | bytes 786436
  37.8 21.5 %all-to-all-start.1 = ((bf16[2,32,8,512]{3,2,0,1:T(8,128)(2,1)}), bf16[2,32,8,512]{3,2,0,1:T(8,128)(2,1)S(1)}, u32[]{:S(2)}, u32[]{:S(2)}) async-start(bf16[2,32,8,512]{3,2,0,1:T(8,128)(2,1)} %pad_maximum_fusion), calls=%async_computation.1 | async-start | bytes 1048576 | tf_op jit(solution)/shard_map/all_to_all | solution.py:118
  78.7 6.2 %copy-start.1 = (f32[32]{0:T(128)S(1)}, f32[32]{0:T(128)}, u32[]{:S(2)}) copy-start(f32[32]{0:T(128)} %param.18) | copy-start | bytes 388
  78.7 6.9 %copy-start.6 = (f32[4]{0:T(128)S(1)}, f32[4]{0:T(128)}, u32[]{:S(2)}) copy-start(f32[4]{0:T(128)} %param.23) | copy-start | bytes 52
  78.7 6.9 %copy-start.3 = (f32[2048]{0:T(1024)S(1)}, f32[2048]{0:T(1024)}, u32[]{:S(2)}) copy-start(f32[2048]{0:T(1024)} %param.20) | copy-start | bytes 24580
  78.7 31.4 %all-to-all-start.3 = ((bf16[4,512,512]{1,2,0:T(8,128)(2,1)}), bf16[4,512,512]{1,2,0:T(8,128)(2,1)}, u32[]{:S(2)}, u32[]{:S(2)}) async-start(bf16[4,512,512]{1,2,0:T(8,128)(2,1)} %broadcast_in_dim.53), calls=%async_computation.3 | async-start | bytes 4194304 | tf_op jit(solution)/shard_map/all_to_all | solution.py:33
  112.2 2.2 copy-start.4
  182.1 4.7 %copy-start.5 = (f32[4,128]{1,0:T(4,128)S(1)}, f32[4,128]{1,0:T(4,128)}, u32[]{:S(2)}) copy-start(f32[4,128]{1,0:T(4,128)} %param.24) | copy-start | bytes 6148
  191.2 21.2 %all-to-all-start.4 = ((bf16[4,512,512]{2,1,0:T(8,128)(2,1)}), bf16[4,512,512]{2,1,0:T(8,128)(2,1)}, u32[]{:S(2)}, u32[]{:S(2)}) async-start(bf16[4,512,512]{2,1,0:T(8,128)(2,1)} %bitcast.294), calls=%async_computation.4 | async-start | bytes 4194304 | tf_op jit(solution)/shard_map/all_to_all | solution.py:71
  215.4 25.8 %all-to-all-start.5 = ((bf16[2,32,8,512]{3,2,0,1:T(8,128)(2,1)}), bf16[2,32,8,512]{3,2,0,1:T(8,128)(2,1)S(1)}, u32[]{:S(2)}, u32[]{:S(2)}) async-start(bf16[2,32,8,512]{3,2,0,1:T(8,128)(2,1)} %fusion.18), calls=%async_computation.5 | async-start | bytes 1048576 | tf_op jit(solution)/shard_map/all_to_all | solution.py:179
where the time goes:
time: 259 us; the launch traced here: 258 us
  waiting for transfers between devices  78.7 us (30%)
  blocking collectives  68.5 us (26%)
  starting transfers between devices  38.2 us (15%)
  local copies, waits for them, and re-layouts  30.4 us (12%)
  matrix products  24 us (9%)
  other arithmetic  17.2 us (7%)
    all_gather x6, blocking collectives, entering_2(): lax.all_gather(part.astype(kind), axis)  38.5 us
    all_to_all x1, waiting for transfers between devices, sent_and_summed(): lax.all_to_all(pieces, axis, split_axis=0, concat_axis=0, tiled=True)  25.9 us
    all_to_all x1, waiting for transfers between devices, sent_and_summed_2(): lax.all_to_all(pieces, axis, split_axis=0, concat_axis=0, tiled=True)  16.7 us
    all_to_all x1, blocking collectives, shards(): lax.all_to_all(outgoing_units, SEQ, split_axis=0, concat_axis=2, tiled=True)  15 us
    all_to_all x1, blocking collectives, shards(): lax.all_to_all(outgoing, SEQ, split_axis=0, concat_axis=2, tiled=True)  15 us
    all_to_all x1, starting transfers between devices, shards(): lax.all_to_all(result_shares, SEQ, split_axis=1, concat_axis=1, tiled=True)  14.1 us
    all_to_all x1, waiting for transfers between devices, copy_for_each(): lax.all_to_all(jnp.broadcast_to(array[None], (length, *array.shape)), axi...  13.5 us
    unnamed x22, local copies, waits for them, and re-layouts  12.8 us
  transfers between devices with their start and end apart: 5, of which 5 were waited for; matrix products, arithmetic and copies ran while one was open for 5% of the time, Pallas kernels for 0%

commit v1 on v0

v1 whole, which is shorter than its diff:
```python
import jax
import jax.numpy as jnp
from jax import lax
from jax.experimental import pallas as pl
from jax.experimental.pallas import tpu as pltpu
from jax.sharding import Mesh
from jax.sharding import PartitionSpec as P

SEQ = ("seq_0", "seq_1", "seq_2")
EPSILON = 1e-06
F32 = jnp.float32
BF16 = jnp.bfloat16
HEAD_WIDTH = 128


VMEM = pl.BlockSpec(memory_space=pltpu.VMEM)
SMEM = pl.BlockSpec(memory_space=pltpu.SMEM)


def shape_of(*dims, dtype=BF16):
    return jax.ShapeDtypeStruct(dims, dtype)


def hbm_of(*dims, dtype=BF16):
    return pltpu.HBM(dims, dtype)


def in_hbm(*arrays):
    return [pltpu.with_memory_space_constraint(a, pltpu.HBM) for a in arrays]


def limit(mebibytes, *semantics):
    return pltpu.CompilerParams(
        dimension_semantics=semantics or None, vmem_limit_bytes=mebibytes << 20
    )


def fixed(*dims):
    return pl.BlockSpec(dims, lambda *_: (0,) * len(dims))


def columns_of(place, step, count, width):
    return pl.ds(pl.multiple_of(lax.rem(place + step, count) * width, width), width)


def adapter_kernel(place_ref, patches_ref, adapter_ref, to_next, to_last, near_next, near_last, own):
    step = pl.program_id(0)
    half = near_next.shape[0]
    block = lax.dot_general(
        patches_ref[0], adapter_ref[...], (((0,), (0,)), ((), ())), preferred_element_type=F32
    )
    small = block.astype(BF16)

    @pl.when(step == 0)
    def _():
        to_next[:half] = small[:half]
        to_last[half:] = small[half:]

    @pl.when(step == 1)
    def _():
        near_next[...] = small[:half]
        to_next[half:] = small[half:]

    @pl.when(step == 2)
    def _():
        to_last[:half] = small[:half]
        near_last[...] = small[half:]

    @pl.when(step == 3)
    def _():
        own[...] = block


def adapter_sums(place, patches, adapter):
    depth, rows = patches.shape[1:]
    width = adapter.shape[1] // 4
    outs = (
        shape_of(rows, width),
        shape_of(rows, width),
        shape_of(rows // 2, width),
        shape_of(rows // 2, width),
        shape_of(rows, width, dtype=F32),
    )

    def block_of(step, place_ref):
        ahead = jnp.where(step == 0, 2, jnp.where(step == 2, 3, jnp.where(step == 1, 1, 0)))
        return (0, lax.rem(place_ref[0] + ahead, 4))

    return pl.pallas_call(
        adapter_kernel,
        out_shape=outs,
        grid_spec=pltpu.PrefetchScalarGridSpec(
            num_scalar_prefetch=1,
            grid=(4,),
            in_specs=[fixed(*patches.shape), pl.BlockSpec((depth, width), block_of)],
            out_specs=tuple(fixed(*o.shape) for o in outs),
        ),
        compiler_params=limit(8, "arbitrary"),
        name="adapter_sums",
    )(place, patches, adapter)


def pass_kernel(from_left, from_right, near_next, near_last, next_out, last_out):
    half = near_next.shape[0]
    next_out[...] = (near_next[...].astype(F32) + from_left[:half].astype(F32)).astype(BF16)
    last_out[...] = (near_last[...].astype(F32) + from_right[half:].astype(F32)).astype(BF16)


def pass_call(*arrays):
    half = shape_of(*arrays[2].shape)
    return pl.pallas_call(
        pass_kernel,
        out_shape=(half, half),
        in_specs=[VMEM] * 4,
        out_specs=(VMEM, VMEM),
        compiler_params=limit(4),
        name="pass_on",
    )(*arrays)


def embed_kernel(own, from_left, from_right, left, right, out):
    half = left.shape[0]
    first = own[:half] + left[...].astype(F32) + from_right[:half].astype(F32)
    second = own[half:] + from_left[half:].astype(F32) + right[...].astype(F32)
    out[:half] = first.astype(BF16)
    out[half:] = second.astype(BF16)


def embed_call(own, *arrays):
    return pl.pallas_call(
        embed_kernel,
        out_shape=shape_of(*own.shape),
        in_specs=[VMEM] * 5,
        out_specs=VMEM,
        compiler_params=limit(4),
        name="embed",
    )(own, *arrays)


def normalize(place, chunks, gain_ref, normed):
    own, left, right, far_a, far_b = chunks
    rows, width = own.shape
    half = rows // 2
    for at, far in ((0, far_a), (half, far_b)):
        span = slice(at, at + half)
        values = ((0, own[span]), (3, left[span]), (1, right[span]), (2, far[...]))
        total = 0.0
        for _, value in values:
            value = value.astype(F32)
            total += jnp.sum(value * value, axis=-1, keepdims=True)
        scale = lax.rsqrt(total / (4 * width) + EPSILON)
        for step, value in values:
            columns = columns_of(place, step, 4, width)
            normed[span, columns] = (value.astype(F32) * scale * gain_ref[:, columns]).astype(BF16)


def product(normed, weight):
    return jnp.dot(normed[...], weight[...], preferred_element_type=F32)


def decay_sums(normed, decay_ref, columns, lanes):
    rows = normed.shape[0]
    values = normed[...]
    decay = decay_ref[...]
    by_row = lax.dot_general(values, decay, (((1,), (1,)), ((), ())), preferred_element_type=F32)
    by_lane = lax.dot_general(decay, values, (((1,), (1,)), ((), ())), preferred_element_type=F32)
    row_ids = lax.broadcasted_iota(jnp.int32, (rows, rows), 0)
    column_ids = lax.broadcasted_iota(jnp.int32, (rows, rows), 1)
    exact = dict(precision=lax.Precision.HIGHEST, preferred_element_type=F32)
    columns[...] = jnp.dot((row_ids >= column_ids).astype(F32), jax.nn.sigmoid(by_row), **exact)
    lanes[...] = jnp.dot(jax.nn.sigmoid(by_lane), (row_ids <= column_ids).astype(F32), **exact)


def chunk_state(head, key, value, columns, ceiling, burst):
    rows = columns.shape[0]
    lanes = slice(head * HEAD_WIDTH, (head + 1) * HEAD_WIDTH)
    column = columns[:, head : head + 1]
    last = columns[rows - 1 :, head : head + 1]
    weighted = key[:, lanes].astype(F32) * jnp.exp(ceiling * (column - last))
    state = lax.dot_general(
        weighted.astype(BF16), value[:, lanes], (((0,), (0,)), ((), ())), preferred_element_type=F32
    )
    return state.astype(BF16).reshape(8, 16, HEAD_WIDTH), burst - ceiling * last


def attend(head, query, key, value, columns, lanes_ref, ceiling, burst, query_out, inner_out):
    rows = columns.shape[0]
    lanes = slice(head * HEAD_WIDTH, (head + 1) * HEAD_WIDTH)
    column = columns[:, head : head + 1]
    lagged = ceiling * (lanes_ref[head : head + 1, :] - column)
    row_ids = lax.broadcasted_iota(jnp.int32, (rows, rows), 0)
    column_ids = lax.broadcasted_iota(jnp.int32, (rows, rows), 1)
    scores = lax.dot_general(
        query[:, lanes], key[:, lanes], (((1,), (1,)), ((), ())), preferred_element_type=F32
    )
    weights = jnp.where(row_ids >= column_ids, scores * jnp.exp(jnp.minimum(lagged, 0.0)), 0.0)
    inner_out[:, lanes] = jnp.dot(weights.astype(BF16), value[:, lanes], preferred_element_type=F32)
    entry = jnp.exp(burst - ceiling * column)
    query_out[:, lanes] = (query[:, lanes].astype(F32) * entry).astype(BF16)


def text_kernel(
    place_ref,
    ceiling_ref,
    own,
    left,
    right,
    far_a,
    far_b,
    gain_ref,
    weight,
    decay_ref,
    query_out,
    gate_out,
    inner_out,
    state_out,
    span_out,
    normed,
    parts,
    columns,
    lanes,
):
    part = pl.program_id(0)

    @pl.when(part == 0)
    def _():
        normalize(place_ref[0], (own, left, right, far_a, far_b), gain_ref, normed)

    parts[part] = product(normed, weight).astype(BF16)

    @pl.when(part == 3)
    def _():
        decay_sums(normed, decay_ref, columns, lanes)
        gate_out[...] = parts[3]
        for head in range(4):
            ceiling = ceiling_ref[head]
            state, span = chunk_state(head, parts.at[1], parts.at[2], columns, ceiling, 0.0)
            state_out[head * 8 : (head + 1) * 8] = state
            span_out[head : head + 1] = jnp.broadcast_to(span, (1, HEAD_WIDTH))
            attend(
                head,
                parts.at[0],
                parts.at[1],
                parts.at[2],
                columns,
                lanes,
                ceiling,
                0.0,
                query_out,
                inner_out,
            )


def image_state_kernel(
    place_ref,
    ceiling_ref,
    forget_ref,
    own,
    left,
    right,
    far_a,
    far_b,
    gain_ref,
    weight,
    decay_ref,
    other_state,
    other_span,
    normed,
    key_value,
    columns,
    lanes,
    state_out,
):
    part = pl.program_id(0)

    @pl.when(part == 0)
    def _():
        normalize(place_ref[0], (own, left, right, far_a, far_b), gain_ref, normed)
        state_out[:, 0:16, :] = other_state[...]

    key_value[part] = product(normed, weight).astype(BF16)

    @pl.when(part == 1)
    def _():
        decay_sums(normed, decay_ref, columns, lanes)
        burst = jnp.log1p(jnp.full((1, 1), -forget_ref[place_ref[1]], F32))
        ids = lax.broadcasted_iota(jnp.int32, (8, HEAD_WIDTH), 0)
        for head in range(4):
            state, span = chunk_state(
                head, key_value.at[0], key_value.at[1], columns, ceiling_ref[head], burst
            )
            targets = slice(head * 8, (head + 1) * 8)
            state_out[targets, 16:32, :] = state
            tile = jnp.zeros((8, HEAD_WIDTH), F32)
            for kind, value in enumerate((other_span[head : head + 1, 0:1], span)):
                upper = value.astype(BF16).astype(F32)
                tile = jnp.where(ids == 2 * kind, upper, tile)
                tile = jnp.where(ids == 2 * kind + 1, value - upper, tile)
            state_out[targets, 32:40, :] = jnp.broadcast_to(
                tile.astype(BF16)[None], (8, 8, HEAD_WIDTH)
            )


def image_attend_kernel(
    place_ref,
    ceiling_ref,
    forget_ref,
    normed,
    key_value,
    columns,
    lanes,
    weight,
    query_out,
    gate_out,
    inner_out,
    query,
):
    part = pl.program_id(0)
    block = product(normed, weight).astype(BF16)

    @pl.when(part == 0)
    def _():
        query[...] = block

    @pl.when(part == 1)
    def _():
        gate_out[...] = block
        burst = jnp.log1p(jnp.full((1, 1), -forget_ref[place_ref[1]], F32))
        for head in range(4):
            attend(
                head,
                query,
                key_value.at[0],
                key_value.at[1],
                columns,
                lanes,
                ceiling_ref[head],
                burst,
                query_out,
                inner_out,
            )


def cost_of(rows, depth, width):
    return pl.CostEstimate(
        flops=2 * rows * depth * width, bytes_accessed=depth * width * 2, transcendentals=0
    )


def weight_spec(weight, column):
    return [pl.BlockSpec((weight.shape[0], weight.shape[1] // 4), lambda p: (0, column(p)))]


def relay_kernel(source, out):
    width = source.shape[2]
    moved_rows = jnp.swapaxes(source[...], 0, 1)
    for part in range(4):
        out[:, part * width : (part + 1) * width] = moved_rows[part]


def relay_call(in_proj):
    depth, parts, width = in_proj.shape
    rows = 256
    return pl.pallas_call(
        relay_kernel,
        grid=(depth // rows,),
        out_shape=hbm_of(depth, parts * width),
        in_specs=[pl.BlockSpec((rows, parts, width), lambda b: (b, 0, 0))],
        out_specs=pl.BlockSpec((rows, parts * width), lambda b: (b, 0)),
        compiler_params=limit(8, "arbitrary"),
        name="relay",
    )(*in_hbm(in_proj))


def text_call(place, ceiling, chunks, gain, weights, decay):
    rows, width = chunks[0].shape
    depth = gain.shape[1]
    outs = (
        hbm_of(rows, width),
        hbm_of(rows, width),
        hbm_of(rows, width, dtype=F32),
        shape_of(32, 16, HEAD_WIDTH),
        shape_of(4, HEAD_WIDTH, dtype=F32),
    )
    return pl.pallas_call(
        text_kernel,
        grid=(4,),
        out_shape=outs,
        in_specs=[SMEM, SMEM]
        + [fixed(*c.shape) for c in chunks]
        + [fixed(1, depth)]
        + weight_spec(weights, lambda p: p)
        + [fixed(*decay.shape)],
        out_specs=tuple(fixed(*o.shape) for o in outs),
        scratch_shapes=[
            pltpu.VMEM((rows, depth), BF16),
            pltpu.VMEM((4, rows, width), BF16),
            pltpu.VMEM((rows, 4), F32),
            pltpu.VMEM((4, rows), F32),
        ],
        compiler_params=limit(20, "arbitrary"),
        cost_estimate=cost_of(rows, depth, 4 * width),
        name="text_unit",
    )(place, ceiling, *chunks, gain, *in_hbm(weights), decay)


def image_state_call(place, ceiling, forget, chunks, gain, weights, decay, state, span):
    rows, width = chunks[0].shape
    depth = gain.shape[1]
    outs = (
        hbm_of(rows, depth),
        hbm_of(2, rows, width),
        shape_of(rows, 4, dtype=F32),
        shape_of(4, rows, dtype=F32),
        shape_of(32, 40, HEAD_WIDTH),
    )
    return pl.pallas_call(
        image_state_kernel,
        grid=(2,),
        out_shape=outs,
        in_specs=[SMEM] * 3
        + [fixed(*c.shape) for c in chunks]
        + [fixed(1, depth)]
        + weight_spec(weights, lambda p: p + 1)
        + [fixed(*decay.shape), fixed(*state.shape), fixed(*span.shape)],
        out_specs=tuple(fixed(*o.shape) for o in outs),
        compiler_params=limit(20, "arbitrary"),
        cost_estimate=cost_of(rows, depth, 2 * width),
        name="image_state",
    )(place, ceiling, forget, *chunks, gain, *in_hbm(weights), decay, state, span)


def image_attend_call(place, ceiling, forget, weights, normed, key_value, columns, lanes):
    rows, depth = normed.shape
    width = key_value.shape[2]
    outs = (
        hbm_of(rows, width),
        hbm_of(rows, width),
        hbm_of(rows, width, dtype=F32),
    )
    held = (*in_hbm(normed, key_value), columns, lanes)
    return pl.pallas_call(
        image_attend_kernel,
        grid=(2,),
        out_shape=outs,
        in_specs=[SMEM] * 3
        + [fixed(*h.shape) for h in held]
        + weight_spec(weights, lambda p: 3 * p),
        out_specs=tuple(fixed(*o.shape) for o in outs),
        scratch_shapes=[pltpu.VMEM((rows, width), BF16)],
        compiler_params=limit(20, "arbitrary"),
        cost_estimate=cost_of(rows, depth, 2 * width),
        name="image_attend",
    )(place, ceiling, forget, *held, *in_hbm(weights))


def scan_kernel(start_ref, states, out, decay, image_at):
    count = start_ref.shape[0]
    for kind in range(2):
        spans = states[:, 32:40, :].astype(F32)
        span = spans[:, 2 * kind : 2 * kind + 1, :] + spans[:, 2 * kind + 1 : 2 * kind + 2, :]
        decay[:, kind] = jnp.broadcast_to(jnp.exp(span), (count, 16, HEAD_WIDTH))
    for position in range(2 * count):
        image_at[position] = -1
    for image in range(count):
        image_at[lax.shift_right_logical(start_ref[image], 1)] = image
    carry = jnp.zeros((16, HEAD_WIDTH), F32)
    texts = jnp.int32(0)
    for position in range(2 * count):
        found = image_at[position]
        kind = (found >= 0).astype(jnp.int32)
        source = jnp.where(found >= 0, found, jnp.minimum(texts, count - 1))
        texts += 1 - kind
        rows = pl.ds(pl.multiple_of(kind * 16, 16), 16)
        out[source, rows, :] = carry.astype(BF16)
        carry = decay[source, kind] * carry + states[source, rows, :].astype(F32)


def scan_call(starts, states):
    count = states.shape[0]
    return pl.pallas_call(
        scan_kernel,
        out_shape=shape_of(count, 32, HEAD_WIDTH),
        in_specs=[SMEM, VMEM],
        out_specs=VMEM,
        scratch_shapes=[
            pltpu.VMEM((count, 2, 16, HEAD_WIDTH), F32),
            pltpu.SMEM((2 * count,), jnp.int32),
        ],
        compiler_params=limit(6),
        name="state_scan",
    )(starts, states)


def output_kernel(
    place_ref,
    entering,
    out_gain,
    out_proj,
    query_t,
    gate_t,
    inner_t,
    query_i,
    gate_i,
    inner_i,
    *outs,
):
    gated_refs = outs[8:]
    outs = outs[:8]
    _, width = query_t.shape
    refs = ((query_t, gate_t, inner_t), (query_i, gate_i, inner_i))
    for kind, (query, gate, inner) in enumerate(refs):
        for head in range(width // HEAD_WIDTH):
            lanes = slice(head * HEAD_WIDTH, (head + 1) * HEAD_WIDTH)
            state = entering[head * 8 : (head + 1) * 8, kind * 16 : (kind + 1) * 16, :]
            attended = inner[:, lanes] + jnp.dot(
                query[:, lanes], state.reshape(HEAD_WIDTH, HEAD_WIDTH), preferred_element_type=F32
            )
            scale = lax.rsqrt(jnp.mean(attended * attended, axis=-1, keepdims=True) + EPSILON)
            gates = gate[:, lanes].astype(F32)
            value = attended * scale * out_gain[head : head + 1, :] * (gates * jax.nn.sigmoid(gates))
            gated_refs[kind][:, lanes] = value.astype(BF16)
    for slot, step in enumerate((2, 1, 3, 0)):
        weight = out_proj[:, columns_of(place_ref[0], step, 4, width)]
        for kind in range(2):
            block = jnp.dot(gated_refs[kind][...], weight, preferred_element_type=F32)
            ref = outs[2 * slot + kind]
            ref[...] = block.astype(ref.dtype)


def output_call(place, entering, out_gain, out_proj, text_parts, image_parts):
    rows, width = text_parts[0].shape
    outs = (shape_of(rows, width),) * 6 + (shape_of(rows, width, dtype=F32),) * 2
    arrays = (entering, out_gain, out_proj, *in_hbm(*text_parts, *image_parts))
    return pl.pallas_call(
        output_kernel,
        grid=(1,),
        out_shape=outs,
        in_specs=[SMEM] + [fixed(*a.shape) for a in arrays],
        out_specs=tuple(fixed(*o.shape) for o in outs),
        scratch_shapes=[pltpu.VMEM((rows, width), BF16)] * 2,
        compiler_params=limit(20, "arbitrary"),
        name="output_blocks",
    )(place, *arrays)


def moved(array, step):
    return lax.ppermute(array, "head", [(i, (i + step) % 4) for i in range(4)])


def gathered(rows):
    half = rows.shape[0] // 2
    left = moved(rows, 1)
    right = moved(rows, 3)
    far_a = moved(left[:half], 1)
    far_b = moved(right[half:], 3)
    return (rows, left, right, far_a, far_b)


def added(one, two):
    return (one.astype(F32) + two.astype(F32)).astype(BF16)


def steps(
    image_patches,
    text_embed,
    image_start,
    image_forget,
    adapter,
    norm_gain,
    in_proj,
    decay_proj,
    head_decay_ceiling,
    out_gain,
    out_proj,
):
    place = jnp.stack([lax.axis_index("head"), lax.axis_index(SEQ)]).astype(jnp.int32)
    decay = decay_proj.T
    gain = norm_gain[None]
    ceiling = head_decay_ceiling

    text_chunks = gathered(text_embed)
    to_next, to_last, near_next, near_last, own = adapter_sums(
        place, image_patches.transpose(0, 2, 1), adapter
    )
    weights = relay_call(in_proj)
    from_left = moved(to_next, 1)
    from_right = moved(to_last, 3)
    next_sum, last_sum = pass_call(from_left, from_right, near_next, near_last)
    left = moved(next_sum, 1)
    right = moved(last_sum, 3)
    embed = embed_call(own, from_left, from_right, left, right)
    image_chunks = gathered(embed)

    *text_parts, text_state, text_span = text_call(
        place, ceiling, text_chunks, gain, weights, decay
    )
    *held, states = image_state_call(
        place, ceiling, image_forget, image_chunks, gain, weights, decay, text_state, text_span
    )
    slices = lax.all_to_all(states, SEQ, 0, 0, tiled=True)
    image_parts = image_attend_call(place, ceiling, image_forget, weights, *held)
    entering = lax.all_to_all(scan_call(image_start, slices), SEQ, 0, 0, tiled=True)

    far_t, far_i, next_t, next_i, last_t, last_i, own_t, own_i = output_call(
        place, entering, out_gain, out_proj, text_parts, image_parts
    )
    far_from_left = moved(far_t, 1)
    far_from_right = moved(far_i, 3)
    left_i = moved(next_i, 1)
    right_t = moved(last_t, 3)
    left_t = moved(added(next_t, far_from_left), 1)
    right_i = moved(added(last_i, far_from_right), 3)
    text_out = text_embed.astype(F32) + (own_t + left_t.astype(F32) + right_t.astype(F32))
    image_out = embed.astype(F32) + (own_i + left_i.astype(F32) + right_i.astype(F32))
    return (image_out.astype(BF16)[None], text_out.astype(BF16))


def solution(mesh):
    split = Mesh(
        mesh.devices.reshape(4, 4, 2, mesh.shape["head"]), ("seq_0", "seq_1", "seq_2", "head")
    )
    return jax.shard_map(
        steps,
        mesh=split,
        in_specs=(
            P(SEQ, None, "head"),
            P(SEQ, "head"),
            P(),
            P(),
            P("head", None),
            P(),
            P(None, None, "head"),
            P(None, "head"),
            P("head"),
            P("head", None),
            P("head", None),
        ),
        out_specs=(P(SEQ, None, "head"), P(SEQ, "head")),
        check_vma=False,
    )
```

time: 259 us -> 120 us (0.46)
  waiting for transfers between devices: 78.7 us -> 27 us
  blocking collectives: 68.5 us -> 22.9 us
  Pallas kernels: 0 us -> 37.7 us
  local copies, waits for them, and re-layouts: 30.4 us -> 2.27 us
  matrix products: 24 us -> 0 us
  other arithmetic: 17.2 us -> 1.89 us
  starting transfers between devices: 38.2 us -> 25.8 us
    all_to_all x5 -> x1, waiting for transfers between devices: 78.7 us -> 3.68 us  [steps(): lax.all_to_all(scan_call(image_start, slices), SEQ, 0, 0, tiled=True)]
    all_gather x6 -> x0, blocking collectives: 38.5 us -> none  [entering_2(): lax.all_gather(part.astype(kind), axis)]
    pallas_call x0 -> x9, Pallas kernels: none -> 37.7 us  [the longest x1 9.61 us: relay_call(): pl.pallas_call(relay_kernel, grid=(depth // rows,), out_shape=hbm_of(dept...]
    all_to_all x5 -> x1, starting transfers between devices: 38.2 us -> 3.84 us  [steps(): lax.all_to_all(scan_call(image_start, slices), SEQ, 0, 0, tiled=True)]
    dot_general x7 -> x0, matrix products: 24 us -> none  [the longest x1 9.12 us: shards(): jnp.dot(normed, in_proj.reshape(model_width, -1), preferred_element_type=...]
    ppermute x0 -> x18, waiting for transfers between devices: none -> 23.3 us  [moved(): return lax.ppermute(array, 'head', [(i, (i + step) % 4) for i in range(4)])]
    ppermute x0 -> x18, starting transfers between devices: none -> 22 us  [moved(): return lax.ppermute(array, 'head', [(i, (i + step) % 4) for i in range(4)])]
    unnamed x22 -> x20, local copies, waits for them, and re-layouts: 12.8 us -> 2.23 us
  transfers between devices with their start and end apart: 5 -> 19, of which waited for: 5 -> 7; matrix products, arithmetic and copies ran while one was open for 5% -> 1% of each run, Pallas kernels for 0% -> 20%
where the time goes in v1:
time: 120 us; the launch traced here: 118 us
  Pallas kernels  37.7 us (31%)
  waiting for transfers between devices  27 us (22%)
  starting transfers between devices  25.8 us (22%)
  blocking collectives  22.9 us (19%)
  local copies, waits for them, and re-layouts  2.27 us (2%)
  other arithmetic  1.89 us (2%)
    ppermute x18, waiting for transfers between devices, moved(): return lax.ppermute(array, 'head', [(i, (i + step) % 4) for i in range(4)])  23.3 us
    all_to_all x1, blocking collectives, steps(): slices = lax.all_to_all(states, SEQ, 0, 0, tiled=True)  22.9 us
    ppermute x18, starting transfers between devices, moved(): return lax.ppermute(array, 'head', [(i, (i + step) % 4) for i in range(4)])  22 us
    pallas_call x1, Pallas kernels, relay_call(): pl.pallas_call(relay_kernel, grid=(depth // rows,), out_shape=hbm_of(dept...  9.61 us
    pallas_call x1, Pallas kernels, text_call(): pl.pallas_call(text_kernel, grid=(4,), out_shape=outs, in_specs=[SMEM, SM...  9.12 us
    pallas_call x1, Pallas kernels, image_state_call(): pl.pallas_call(image_state_kernel, grid=(2,), out_shape=outs, in_specs=[S...  6.5 us
    pallas_call x1, Pallas kernels, image_attend_call(): pl.pallas_call(image_attend_kernel, grid=(2,), out_shape=outs, in_specs=[...  5.18 us
    all_to_all x1, starting transfers between devices, steps(): lax.all_to_all(scan_call(image_start, slices), SEQ, 0, 0, tiled=True)  3.84 us
  transfers between devices with their start and end apart: 19, of which 7 were waited for; matrix products, arithmetic and copies ran while one was open for 1% of the time, Pallas kernels for 20%

profile of v1, /device:TPU:1, one launch (start us, length us, event | category | flops | bytes accessed | tf_op | source)
XLA Modules:
  0.0 118.4 jit_solution(9415442612187219048)
XLA Ops:
  0.6 0.1 pad_add_fusion.place_ref
  0.7 1.3 %copy-done.1 = bf16[288,2048]{1,0:T(8,128)(2,1)S(1)} copy-done((bf16[288,2048]{1,0:T(8,128)(2,1)S(1)}, bf16[288,2048]{1,0:T(8,128)(2,1)}, u32[]{:S(2)}) %copy-start.1) | copy-done | bytes 1179672
  2.0 0.9 copy-done.3
  2.9 2.2 %adapter_sums.1 = (bf16[256,512]{1,0:T(8,128)(2,1)S(1)}, bf16[256,512]{1,0:T(8,128)(2,1)S(1)}, bf16[128,512]{1,0:T(8,128)(2,1)S(1)}, bf16[128,512]{1,0:T(8,128)(2,1)S(1)}, f32[256,512]{1,0:T(8,128)S(1)}) custom-call(s32[2]{0:T(128)S(1)} %pad_add_fusion.place_ref, bf16[1,288,256]{2,1,0:T(8,128)(2,1)S(1)} %bitcast.7, bf16[288,2048]{1,0:T(8,128)(2,1)S(1)} %copy-done.1), custom_call_target="tpu_custom_call" | custom-call | tf_op jit(solution)/shard_map/adapter_sums/pallas_call | solution.py:89
  5.1 2.1 %collective-permute-start = (bf16[256,512]{1,0:T(8,128)(2,1)S(1)}, bf16[256,512]{1,0:T(8,128)(2,1)S(1)}, u32[]{:S(2)}, u32[]{:S(2)}) collective-permute-start(bf16[256,512]{1,0:T(8,128)(2,1)S(1)} %get-tuple-element.31), channel_id=1, source_target_pairs={{0,1},{1,2},{2,3},{3,0},{4,5},{5,6},{6,7},{7,4},{8,9},{9,10},{10,1... | collective-permute-start | bytes 786440 | tf_op jit(solution)/shard_map/ppermute | solution.py:548
  7.2 1.4 %collective-permute-start.1 = (bf16[256,512]{1,0:T(8,128)(2,1)S(1)}, bf16[256,512]{1,0:T(8,128)(2,1)S(1)}, u32[]{:S(2)}, u32[]{:S(2)}) collective-permute-start(bf16[256,512]{1,0:T(8,128)(2,1)S(1)} %get-tuple-element.32), channel_id=1, source_target_pairs={{0,3},{1,0},{2,1},{3,2},{4,7},{5,4},{6,5},{7,6},{8,11},{9,8},{10,9... | collective-permute-start | bytes 786440 | tf_op jit(solution)/shard_map/ppermute | solution.py:548
  8.5 5.6 %collective-permute-done.from_left = bf16[256,512]{1,0:T(8,128)(2,1)S(1)} collective-permute-done((bf16[256,512]{1,0:T(8,128)(2,1)S(1)}, bf16[256,512]{1,0:T(8,128)(2,1)S(1)}, u32[]{:S(2)}, u32[]{:S(2)}) %collective-permute-start) | collective-permute-done | bytes 262176 | tf_op jit(solution)/shard_map/ppermute | solution.py:548
  14.1 0.1 pass_on.1
  14.2 1.3 %collective-permute-start.2 = (bf16[128,512]{1,0:T(8,128)(2,1)S(1)}, bf16[128,512]{1,0:T(8,128)(2,1)S(1)}, u32[]{:S(2)}, u32[]{:S(2)}) collective-permute-start(bf16[128,512]{1,0:T(8,128)(2,1)S(1)} %get-tuple-element.35), channel_id=1, source_target_pairs={{0,1},{1,2},{2,3},{3,0},{4,5},{5,6},{6,7},{7,4},{8,9},{9,10},{10,1... | collective-permute-start | bytes 393224 | tf_op jit(solution)/shard_map/ppermute | solution.py:548
  15.4 1.5 %collective-permute-start.3 = (bf16[128,512]{1,0:T(8,128)(2,1)S(1)}, bf16[128,512]{1,0:T(8,128)(2,1)S(1)}, u32[]{:S(2)}, u32[]{:S(2)}) collective-permute-start(bf16[128,512]{1,0:T(8,128)(2,1)S(1)} %get-tuple-element.36), channel_id=1, source_target_pairs={{0,3},{1,0},{2,1},{3,2},{4,7},{5,4},{6,5},{7,6},{8,11},{9,8},{10,9... | collective-permute-start | bytes 393224 | tf_op jit(solution)/shard_map/ppermute | solution.py:548
  16.9 2.7 %collective-permute-start.9 = (bf16[256,512]{1,0:T(8,128)(2,1)}, bf16[256,512]{1,0:T(8,128)(2,1)S(1)}, u32[]{:S(2)}, u32[]{:S(2)}) collective-permute-start(bf16[256,512]{1,0:T(8,128)(2,1)} %own.1), channel_id=1, source_target_pairs={{0,3},{1,0},{2,1},{3,2},{4,7},{5,4},{6,5},{7,6},{8,11},{9,8},{10,9... | collective-permute-start | bytes 786440 | tf_op jit(solution)/shard_map/ppermute | solution.py:548
  19.6 0.1 embed.1.own
  19.7 0.9 collective-permute-start.4
  20.6 1.8 %collective-permute-start.5 = (bf16[256,512]{1,0:T(8,128)(2,1)S(1)}, bf16[256,512]{1,0:T(8,128)(2,1)S(1)}, u32[]{:S(2)}, u32[]{:S(2)}) collective-permute-start(bf16[256,512]{1,0:T(8,128)(2,1)S(1)} %embed.1.own), channel_id=1, source_target_pairs={{0,3},{1,0},{2,1},{3,2},{4,7},{5,4},{6,5},{7,6},{8,11},{9,8},{10,9... | collective-permute-start | bytes 786440 | tf_op jit(solution)/shard_map/ppermute | solution.py:548
  22.4 3.0 %collective-permute-done.8.left = bf16[256,512]{1,0:T(8,128)(2,1)S(1)} collective-permute-done((bf16[256,512]{1,0:T(8,128)(2,1)}, bf16[256,512]{1,0:T(8,128)(2,1)S(1)}, u32[]{:S(2)}, u32[]{:S(2)}) %collective-permute-start.8) | collective-permute-done | bytes 262176 | tf_op jit(solution)/shard_map/ppermute | solution.py:548
  25.4 0.1 collective-permute-start.10
  25.5 0.0 copy-start.2
  25.5 0.0 copy-start.4
  25.5 0.0 copy-start.5
  25.5 0.0 copy-start.6
  25.6 2.9 %collective-permute-start.11 = (bf16[128,512]{1,0:T(8,128)(2,1)S(1)}, bf16[128,512]{1,0:T(8,128)(2,1)S(1)}, u32[]{:S(2)}, u32[]{:S(2)}) collective-permute-start(bf16[128,512]{1,0:T(8,128)(2,1)S(1)} %slice.19), channel_id=1, source_target_pairs={{0,3},{1,0},{2,1},{3,2},{4,7},{5,4},{6,5},{7,6},{8,11},{9,8},{10,9... | collective-permute-start | bytes 393224 | tf_op jit(solution)/shard_map/ppermute | solution.py:548
  28.5 9.6 %relay.1.weight = bf16[2048,2048]{1,0:T(8,128)(2,1)} custom-call(bf16[2048,4,512]{2,1,0:T(4,128)(2,1)} %source.1), custom_call_target="tpu_custom_call" | custom-call | tf_op jit(solution)/shard_map/relay/pallas_call | solution.py:364
  38.1 0.1 collective-permute-start.6
  38.2 2.7 %collective-permute-start.7 = (bf16[128,512]{1,0:T(8,128)(2,1)S(1)}, bf16[128,512]{1,0:T(8,128)(2,1)S(1)}, u32[]{:S(2)}, u32[]{:S(2)}) collective-permute-start(bf16[128,512]{1,0:T(8,128)(2,1)S(1)} %slice.17), channel_id=1, source_target_pairs={{0,3},{1,0},{2,1},{3,2},{4,7},{5,4},{6,5},{7,6},{8,11},{9,8},{10,9... | collective-permute-start | bytes 393224 | tf_op jit(solution)/shard_map/ppermute | solution.py:548
  41.0 0.0 copy-start.9
  41.0 9.1 %text_unit.1 = (bf16[256,512]{1,0:T(8,128)(2,1)}, bf16[256,512]{1,0:T(8,128)(2,1)}, f32[256,512]{1,0:T(8,128)}, bf16[32,16,128]{2,1,0:T(8,128)(2,1)S(1)}, f32[4,128]{1,0:T(4,128)S(1)}) custom-call(s32[2]{0:T(128)S(1)} %pad_add_fusion.place_ref, f32[4]{0:T(128)S(1)} %copy-done.6, bf16[256,512]{1,0:T(8,128)(2,1)S(1)} %copy-done.2, ...), custom_call_target="tpu_custom_call" | custom-call | flops 2147483648 | bytes 8388608 | tf_op jit(solution)/shard_map/text_unit/pallas_call | solution.py:385
  50.1 0.0 copy-start
  50.1 6.5 %image_state.1 = (bf16[256,2048]{1,0:T(8,128)(2,1)}, bf16[2,256,512]{2,1,0:T(8,128)(2,1)}, f32[256,4]{1,0:T(8,128)S(1)}, f32[4,256]{1,0:T(4,128)S(1)}, bf16[32,40,128]{2,1,0:T(8,128)(2,1)S(1)}) custom-call(s32[2]{0:T(128)S(1)} %pad_add_fusion.place_ref, f32[4]{0:T(128)S(1)} %copy-done.6, f32[32]{0:T(128)S(1)} %copy-done.8, bf16[256,512]{1,0:T(8,128)(2,1)S(1)} %embed.1.own, ...), custom_call_target="tpu_custom_call" | custom-call | flops 1073741824 | bytes 4194304 | tf_op jit(solution)/shard_map/image_state/pallas_call | solution.py:417
  56.7 22.9 %all_to_all.10.states = bf16[32,40,128]{2,1,0:T(8,128)(2,1)S(1)} all-to-all(bf16[32,40,128]{2,1,0:T(8,128)(2,1)S(1)} %get-tuple-element.39), channel_id=1, replica_groups=mesh['seq_0'=4,'seq_1'=4,'seq_2'=2,'head'=4] {'seq_0','seq_1','seq_2'}, dimensions={0} | all-to-all | bytes 655360 | tf_op jit(solution)/shard_map/all_to_all | solution.py:601
  79.6 1.7 %state_scan.1 = bf16[32,32,128]{2,1,0:T(8,128)(2,1)} custom-call(s32[32]{0:T(128)S(1)} %copy-done.9, bf16[32,40,128]{2,1,0:T(8,128)(2,1)S(1)} %all_to_all.10.states), custom_call_target="tpu_custom_call" | custom-call | tf_op jit(solution)/shard_map/state_scan/pallas_call | solution.py:481
  81.2 3.8 %all-to-all-start.1 = ((bf16[32,32,128]{2,1,0:T(8,128)(2,1)}), bf16[32,32,128]{2,1,0:T(8,128)(2,1)S(1)}, u32[]{:S(2)}, u32[]{:S(2)}) async-start(bf16[32,32,128]{2,1,0:T(8,128)(2,1)} %state_scan.1), calls=%async_computation.1 | async-start | bytes 524288 | tf_op jit(solution)/shard_map/all_to_all | solution.py:603
  85.1 5.2 %image_attend.1 = (bf16[256,512]{1,0:T(8,128)(2,1)}, bf16[256,512]{1,0:T(8,128)(2,1)}, f32[256,512]{1,0:T(8,128)}) custom-call(s32[2]{0:T(128)S(1)} %pad_add_fusion.place_ref, f32[4]{0:T(128)S(1)} %copy-done.6, f32[32]{0:T(128)S(1)} %copy-done.8, bf16[256,2048]{1,0:T(8,128)(2,1)} %get-tuple-element.43.normed, ...), custom_call_target="tpu_custom_call" | custom-call | flops 1073741824 | bytes 4194304 | tf_op jit(solution)/shard_map/image_attend/pallas_call | solution.py:442
  90.3 3.7 %all-to-all-done.1.entering = bf16[32,32,128]{2,1,0:T(8,128)(2,1)S(1)} async-done(((bf16[32,32,128]{2,1,0:T(8,128)(2,1)}), bf16[32,32,128]{2,1,0:T(8,128)(2,1)S(1)}, u32[]{:S(2)}, u32[]{:S(2)}) %all-to-all-start.1) | async-done | bytes 262176 | tf_op jit(solution)/shard_map/all_to_all | solution.py:603
  94.0 3.3 %output_blocks.1 = (bf16[256,512]{1,0:T(8,128)(2,1)S(1)}, bf16[256,512]{1,0:T(8,128)(2,1)S(1)}, bf16[256,512]{1,0:T(8,128)(2,1)S(1)}, bf16[256,512]{1,0:T(8,128)...) custom-call(s32[2]{0:T(128)S(1)} %pad_add_fusion.place_ref, ...), custom_call_target="tpu_custom_call" | custom-call | tf_op jit(solution)/shard_map/output_blocks/pallas_call | solution.py:535
  97.2 0.1 collective-permute-start.13
  97.3 1.5 %collective-permute-start.15 = (bf16[256,512]{1,0:T(8,128)(2,1)S(1)}, bf16[256,512]{1,0:T(8,128)(2,1)S(1)}, u32[]{:S(2)}, u32[]{:S(2)}) collective-permute-start(bf16[256,512]{1,0:T(8,128)(2,1)S(1)} %get-tuple-element.56), channel_id=1, source_target_pairs={{0,1},{1,2},{2,3},{3,0},{4,5},{5,6},{6,7},{7,4},{8,9},{9,10},{10,1... | collective-permute-start | bytes 786440 | tf_op jit(solution)/shard_map/ppermute | solution.py:548
  98.8 0.0 collective-permute-start.12
  98.8 6.2 %collective-permute-done.13 = bf16[256,512]{1,0:T(8,128)(2,1)S(1)} collective-permute-done((bf16[256,512]{1,0:T(8,128)(2,1)S(1)}, bf16[256,512]{1,0:T(8,128)(2,1)S(1)}, u32[]{:S(2)}, u32[]{:S(2)}) %collective-permute-start.13) | collective-permute-done | bytes 262176 | tf_op jit(solution)/shard_map/ppermute | solution.py:548
  105.0 0.1 add_convert_fusion.3
  105.1 1.5 %collective-permute-start.14 = (bf16[256,512]{1,0:T(8,128)(2,1)S(1)}, bf16[256,512]{1,0:T(8,128)(2,1)S(1)}, u32[]{:S(2)}, u32[]{:S(2)}) collective-permute-start(bf16[256,512]{1,0:T(8,128)(2,1)S(1)} %add_convert_fusion.3), channel_id=1, source_target_pairs={{0,3},{1,0},{2,1},{3,2},{4,7},{5,4},{6,5},{7,6},{8,11},{9,8},{10,9... | collective-permute-start | bytes 786440 | tf_op jit(solution)/shard_map/ppermute | solution.py:548
  106.6 0.1 collective-permute-start.17
  106.7 0.1 add_convert_fusion.1
  106.7 1.5 %collective-permute-start.16 = (bf16[256,512]{1,0:T(8,128)(2,1)S(1)}, bf16[256,512]{1,0:T(8,128)(2,1)S(1)}, u32[]{:S(2)}, u32[]{:S(2)}) collective-permute-start(bf16[256,512]{1,0:T(8,128)(2,1)S(1)} %add_convert_fusion.1), channel_id=1, source_target_pairs={{0,1},{1,2},{2,3},{3,0},{4,5},{5,6},{6,7},{7,4},{8,9},{9,10},{10,1... | collective-permute-start | bytes 786440 | tf_op jit(solution)/shard_map/ppermute | solution.py:548
  108.2 3.7 %collective-permute-done.12 = bf16[256,512]{1,0:T(8,128)(2,1)S(1)} collective-permute-done((bf16[256,512]{1,0:T(8,128)(2,1)S(1)}, bf16[256,512]{1,0:T(8,128)(2,1)S(1)}, u32[]{:S(2)}, u32[]{:S(2)}) %collective-permute-start.12) | collective-permute-done | bytes 262176 | tf_op jit(solution)/shard_map/ppermute | solution.py:548
  111.9 0.1 collective-permute-done.14
  112.0 0.8 fusion
  112.8 4.8 %collective-permute-done.17 = bf16[256,512]{1,0:T(8,128)(2,1)S(1)} collective-permute-done((bf16[256,512]{1,0:T(8,128)(2,1)S(1)}, bf16[256,512]{1,0:T(8,128)(2,1)S(1)}, u32[]{:S(2)}, u32[]{:S(2)}) %collective-permute-start.17) | collective-permute-done | bytes 262176 | tf_op jit(solution)/shard_map/ppermute | solution.py:548
  117.6 0.8 add_convert_fusion
  (29 shorter events, 0.1 us)
Async XLA Ops:
  0.7 1.3 %copy-start.1 = (bf16[288,2048]{1,0:T(8,128)(2,1)S(1)}, bf16[288,2048]{1,0:T(8,128)(2,1)}, u32[]{:S(2)}) copy-start(bf16[288,2048]{1,0:T(8,128)(2,1)} %adapter_ref.1) | copy-start | bytes 3538948
  2.0 0.9 copy-start.3
  5.1 9.0 %collective-permute-start = (bf16[256,512]{1,0:T(8,128)(2,1)S(1)}, bf16[256,512]{1,0:T(8,128)(2,1)S(1)}, u32[]{:S(2)}, u32[]{:S(2)}) collective-permute-start(bf16[256,512]{1,0:T(8,128)(2,1)S(1)} %get-tuple-element.31), channel_id=1, source_target_pairs={{0,1},{1,2},{2,3},{3,0},{4,5},{5,6},{6,7},{7,4},{8,9},{9,10},{10,1... | collective-permute-start | bytes 786440 | tf_op jit(solution)/shard_map/ppermute | solution.py:548
  7.2 6.9 %collective-permute-start.1 = (bf16[256,512]{1,0:T(8,128)(2,1)S(1)}, bf16[256,512]{1,0:T(8,128)(2,1)S(1)}, u32[]{:S(2)}, u32[]{:S(2)}) collective-permute-start(bf16[256,512]{1,0:T(8,128)(2,1)S(1)} %get-tuple-element.32), channel_id=1, source_target_pairs={{0,3},{1,0},{2,1},{3,2},{4,7},{5,4},{6,5},{7,6},{8,11},{9,8},{10,9... | collective-permute-start | bytes 786440 | tf_op jit(solution)/shard_map/ppermute | solution.py:548
  14.2 5.4 %collective-permute-start.2 = (bf16[128,512]{1,0:T(8,128)(2,1)S(1)}, bf16[128,512]{1,0:T(8,128)(2,1)S(1)}, u32[]{:S(2)}, u32[]{:S(2)}) collective-permute-start(bf16[128,512]{1,0:T(8,128)(2,1)S(1)} %get-tuple-element.35), channel_id=1, source_target_pairs={{0,1},{1,2},{2,3},{3,0},{4,5},{5,6},{6,7},{7,4},{8,9},{9,10},{10,1... | collective-permute-start | bytes 393224 | tf_op jit(solution)/shard_map/ppermute | solution.py:548
  15.4 4.2 %collective-permute-start.3 = (bf16[128,512]{1,0:T(8,128)(2,1)S(1)}, bf16[128,512]{1,0:T(8,128)(2,1)S(1)}, u32[]{:S(2)}, u32[]{:S(2)}) collective-permute-start(bf16[128,512]{1,0:T(8,128)(2,1)S(1)} %get-tuple-element.36), channel_id=1, source_target_pairs={{0,3},{1,0},{2,1},{3,2},{4,7},{5,4},{6,5},{7,6},{8,11},{9,8},{10,9... | collective-permute-start | bytes 393224 | tf_op jit(solution)/shard_map/ppermute | solution.py:548
  16.9 8.5 %collective-permute-start.8 = (bf16[256,512]{1,0:T(8,128)(2,1)}, bf16[256,512]{1,0:T(8,128)(2,1)S(1)}, u32[]{:S(2)}, u32[]{:S(2)}) collective-permute-start(bf16[256,512]{1,0:T(8,128)(2,1)} %own.1), channel_id=1, source_target_pairs={{0,1},{1,2},{2,3},{3,0},{4,5},{5,6},{6,7},{7,4},{8,9},{9,10},{10,1... | collective-permute-start | bytes 786440 | tf_op jit(solution)/shard_map/ppermute | solution.py:548
  16.9 8.6 %collective-permute-start.9 = (bf16[256,512]{1,0:T(8,128)(2,1)}, bf16[256,512]{1,0:T(8,128)(2,1)S(1)}, u32[]{:S(2)}, u32[]{:S(2)}) collective-permute-start(bf16[256,512]{1,0:T(8,128)(2,1)} %own.1), channel_id=1, source_target_pairs={{0,3},{1,0},{2,1},{3,2},{4,7},{5,4},{6,5},{7,6},{8,11},{9,8},{10,9... | collective-permute-start | bytes 786440 | tf_op jit(solution)/shard_map/ppermute | solution.py:548
  19.7 18.4 %collective-permute-start.4 = (bf16[256,512]{1,0:T(8,128)(2,1)S(1)}, bf16[256,512]{1,0:T(8,128)(2,1)S(1)}, u32[]{:S(2)}, u32[]{:S(2)}) collective-permute-start(bf16[256,512]{1,0:T(8,128)(2,1)S(1)} %embed.1.own), channel_id=1, source_target_pairs={{0,1},{1,2},{2,3},{3,0},{4,5},{5,6},{6,7},{7,4},{8,9},{9,10},{10,1... | collective-permute-start | bytes 786440 | tf_op jit(solution)/shard_map/ppermute | solution.py:548
  20.6 17.6 %collective-permute-start.5 = (bf16[256,512]{1,0:T(8,128)(2,1)S(1)}, bf16[256,512]{1,0:T(8,128)(2,1)S(1)}, u32[]{:S(2)}, u32[]{:S(2)}) collective-permute-start(bf16[256,512]{1,0:T(8,128)(2,1)S(1)} %embed.1.own), channel_id=1, source_target_pairs={{0,3},{1,0},{2,1},{3,2},{4,7},{5,4},{6,5},{7,6},{8,11},{9,8},{10,9... | collective-permute-start | bytes 786440 | tf_op jit(solution)/shard_map/ppermute | solution.py:548
  25.4 15.5 %collective-permute-start.10 = (bf16[128,512]{1,0:T(8,128)(2,1)S(1)}, bf16[128,512]{1,0:T(8,128)(2,1)S(1)}, u32[]{:S(2)}, u32[]{:S(2)}) collective-permute-start(bf16[128,512]{1,0:T(8,128)(2,1)S(1)} %slice.18), channel_id=1, source_target_pairs={{0,1},{1,2},{2,3},{3,0},{4,5},{5,6},{6,7},{7,4},{8,9},{9,10},{10,1... | collective-permute-start | bytes 393224 | tf_op jit(solution)/shard_map/ppermute | solution.py:548
  25.5 15.4 %copy-start.2 = (bf16[256,512]{1,0:T(8,128)(2,1)S(1)}, bf16[256,512]{1,0:T(8,128)(2,1)}, u32[]{:S(2)}) copy-start(bf16[256,512]{1,0:T(8,128)(2,1)} %own.1) | copy-start | bytes 786436
  25.5 15.4 %copy-start.4 = (bf16[2048,4]{0,1:T(4,128)(2,1)S(1)}, bf16[2048,4]{0,1:T(4,128)(2,1)}, u32[]{:S(2)}) copy-start(bf16[2048,4]{0,1:T(4,128)(2,1)} %param.18) | copy-start | bytes 49156
  25.5 15.4 %copy-start.5 = (f32[2048]{0:T(1024)S(1)}, f32[2048]{0:T(1024)}, u32[]{:S(2)}) copy-start(f32[2048]{0:T(1024)} %param.16) | copy-start | bytes 24580
  25.5 15.4 %copy-start.6 = (f32[4]{0:T(128)S(1)}, f32[4]{0:T(128)}, u32[]{:S(2)}) copy-start(f32[4]{0:T(128)} %ceiling_ref.5) | copy-start | bytes 52
  25.6 15.4 %collective-permute-start.11 = (bf16[128,512]{1,0:T(8,128)(2,1)S(1)}, bf16[128,512]{1,0:T(8,128)(2,1)S(1)}, u32[]{:S(2)}, u32[]{:S(2)}) collective-permute-start(bf16[128,512]{1,0:T(8,128)(2,1)S(1)} %slice.19), channel_id=1, source_target_pairs={{0,3},{1,0},{2,1},{3,2},{4,7},{5,4},{6,5},{7,6},{8,11},{9,8},{10,9... | collective-permute-start | bytes 393224 | tf_op jit(solution)/shard_map/ppermute | solution.py:548
  38.1 12.0 %copy-start.8 = (f32[32]{0:T(128)S(1)}, f32[32]{0:T(128)}, u32[]{:S(2)}) copy-start(f32[32]{0:T(128)} %forget_ref.3) | copy-start | bytes 388
  38.1 12.0 %collective-permute-start.6 = (bf16[128,512]{1,0:T(8,128)(2,1)S(1)}, bf16[128,512]{1,0:T(8,128)(2,1)S(1)}, u32[]{:S(2)}, u32[]{:S(2)}) collective-permute-start(bf16[128,512]{1,0:T(8,128)(2,1)S(1)} %slice.16), channel_id=1, source_target_pairs={{0,1},{1,2},{2,3},{3,0},{4,5},{5,6},{6,7},{7,4},{8,9},{9,10},{10,1... | collective-permute-start | bytes 393224 | tf_op jit(solution)/shard_map/ppermute | solution.py:548
  38.2 11.9 %collective-permute-start.7 = (bf16[128,512]{1,0:T(8,128)(2,1)S(1)}, bf16[128,512]{1,0:T(8,128)(2,1)S(1)}, u32[]{:S(2)}, u32[]{:S(2)}) collective-permute-start(bf16[128,512]{1,0:T(8,128)(2,1)S(1)} %slice.17), channel_id=1, source_target_pairs={{0,3},{1,0},{2,1},{3,2},{4,7},{5,4},{6,5},{7,6},{8,11},{9,8},{10,9... | collective-permute-start | bytes 393224 | tf_op jit(solution)/shard_map/ppermute | solution.py:548
  41.0 38.6 %copy-start.9 = (s32[32]{0:T(128)S(1)}, s32[32]{0:T(128)}, u32[]{:S(2)}) copy-start(s32[32]{0:T(128)} %start_ref.1) | copy-start | bytes 388
  50.1 43.8 %copy-start = (bf16[512,2048]{1,0:T(8,128)(2,1)S(1)}, bf16[512,2048]{1,0:T(8,128)(2,1)}, u32[]{:S(2)}) copy-start(bf16[512,2048]{1,0:T(8,128)(2,1)} %out_proj.1) | copy-start | bytes 6291460
  50.1 43.8 %copy-start.7 = (f32[4,128]{1,0:T(4,128)S(1)}, f32[4,128]{1,0:T(4,128)}, u32[]{:S(2)}) copy-start(f32[4,128]{1,0:T(4,128)} %out_gain.1) | copy-start | bytes 6148
  81.2 12.7 %all-to-all-start.1 = ((bf16[32,32,128]{2,1,0:T(8,128)(2,1)}), bf16[32,32,128]{2,1,0:T(8,128)(2,1)S(1)}, u32[]{:S(2)}, u32[]{:S(2)}) async-start(bf16[32,32,128]{2,1,0:T(8,128)(2,1)} %state_scan.1), calls=%async_computation.1 | async-start | bytes 524288 | tf_op jit(solution)/shard_map/all_to_all | solution.py:603
  97.2 7.7 %collective-permute-start.13 = (bf16[256,512]{1,0:T(8,128)(2,1)S(1)}, bf16[256,512]{1,0:T(8,128)(2,1)S(1)}, u32[]{:S(2)}, u32[]{:S(2)}) collective-permute-start(bf16[256,512]{1,0:T(8,128)(2,1)S(1)} %get-tuple-element.53), channel_id=1, source_target_pairs={{0,3},{1,0},{2,1},{3,2},{4,7},{5,4},{6,5},{7,6},{8,11},{9,8},{10,9... | collective-permute-start | bytes 786440 | tf_op jit(solution)/shard_map/ppermute | solution.py:548
  97.3 9.3 %collective-permute-start.15 = (bf16[256,512]{1,0:T(8,128)(2,1)S(1)}, bf16[256,512]{1,0:T(8,128)(2,1)S(1)}, u32[]{:S(2)}, u32[]{:S(2)}) collective-permute-start(bf16[256,512]{1,0:T(8,128)(2,1)S(1)} %get-tuple-element.56), channel_id=1, source_target_pairs={{0,1},{1,2},{2,3},{3,0},{4,5},{5,6},{6,7},{7,4},{8,9},{9,10},{10,1... | collective-permute-start | bytes 786440 | tf_op jit(solution)/shard_map/ppermute | solution.py:548
  98.8 13.1 %collective-permute-start.12 = (bf16[256,512]{1,0:T(8,128)(2,1)S(1)}, bf16[256,512]{1,0:T(8,128)(2,1)S(1)}, u32[]{:S(2)}, u32[]{:S(2)}) collective-permute-start(bf16[256,512]{1,0:T(8,128)(2,1)S(1)} %get-tuple-element.51), channel_id=1, source_target_pairs={{0,1},{1,2},{2,3},{3,0},{4,5},{5,6},{6,7},{7,4},{8,9},{9,10},{10,1... | collective-permute-start | bytes 786440 | tf_op jit(solution)/shard_map/ppermute | solution.py:548
  105.1 6.9 %collective-permute-start.14 = (bf16[256,512]{1,0:T(8,128)(2,1)S(1)}, bf16[256,512]{1,0:T(8,128)(2,1)S(1)}, u32[]{:S(2)}, u32[]{:S(2)}) collective-permute-start(bf16[256,512]{1,0:T(8,128)(2,1)S(1)} %add_convert_fusion.3), channel_id=1, source_target_pairs={{0,3},{1,0},{2,1},{3,2},{4,7},{5,4},{6,5},{7,6},{8,11},{9,8},{10,9... | collective-permute-start | bytes 786440 | tf_op jit(solution)/shard_map/ppermute | solution.py:548
  106.6 11.0 %collective-permute-start.17 = (bf16[256,512]{1,0:T(8,128)(2,1)S(1)}, bf16[256,512]{1,0:T(8,128)(2,1)S(1)}, u32[]{:S(2)}, u32[]{:S(2)}) collective-permute-start(bf16[256,512]{1,0:T(8,128)(2,1)S(1)} %get-tuple-element.57), channel_id=1, source_target_pairs={{0,3},{1,0},{2,1},{3,2},{4,7},{5,4},{6,5},{7,6},{8,11},{9,8},{10,9... | collective-permute-start | bytes 786440 | tf_op jit(solution)/shard_map/ppermute | solution.py:548
  106.7 10.8 %collective-permute-start.16 = (bf16[256,512]{1,0:T(8,128)(2,1)S(1)}, bf16[256,512]{1,0:T(8,128)(2,1)S(1)}, u32[]{:S(2)}, u32[]{:S(2)}) collective-permute-start(bf16[256,512]{1,0:T(8,128)(2,1)S(1)} %add_convert_fusion.1), channel_id=1, source_target_pairs={{0,1},{1,2},{2,3},{3,0},{4,5},{5,6},{6,7},{7,4},{8,9},{9,10},{10,1... | collective-permute-start | bytes 786440 | tf_op jit(solution)/shard_map/ppermute | solution.py:548

commit v2 on v1

--- a/solution.py
+++ b/solution.py
@@ -15,6 +15,7 @@
 
 VMEM = pl.BlockSpec(memory_space=pltpu.VMEM)
 SMEM = pl.BlockSpec(memory_space=pltpu.SMEM)
+HBM = pl.BlockSpec(memory_space=pltpu.HBM)
 
 
 def shape_of(*dims, dtype=BF16):
@@ -97,7 +98,7 @@
         ),
         compiler_params=limit(8, "arbitrary"),
         name="adapter_sums",
-    )(place, patches, adapter)
+    )(place, *in_hbm(patches, adapter))
 
 
 def pass_kernel(from_left, from_right, near_next, near_last, next_out, last_out):
@@ -155,20 +156,34 @@
 
 
 def product(normed, weight):
-    return jnp.dot(normed[...], weight[...], preferred_element_type=F32)
+    return jnp.dot(normed[...], weight, preferred_element_type=F32)
 
 
 def decay_sums(normed, decay_ref, columns, lanes):
     rows = normed.shape[0]
-    values = normed[...]
-    decay = decay_ref[...]
-    by_row = lax.dot_general(values, decay, (((1,), (1,)), ((), ())), preferred_element_type=F32)
-    by_lane = lax.dot_general(decay, values, (((1,), (1,)), ((), ())), preferred_element_type=F32)
+    decay = decay_ref[...].astype(F32)
+    decay = jnp.concatenate([decay] * 4, axis=0).astype(BF16)
+    decay = jnp.concatenate([decay, jnp.zeros((HEAD_WIDTH - 16, decay.shape[1]), BF16)], axis=0)
+    gates = jax.nn.sigmoid(
+        lax.dot_general(normed[...], decay, (((1,), (1,)), ((), ())), preferred_element_type=F32)
+    )
+    ids = lax.broadcasted_iota(jnp.int32, gates.shape, 1)
+    upper = gates.astype(BF16).astype(F32)
+    middle = (gates - upper).astype(BF16).astype(F32)
+    terms = jnp.where(ids < 4, upper, jnp.where(ids < 8, middle, gates - upper - middle))
     row_ids = lax.broadcasted_iota(jnp.int32, (rows, rows), 0)
     column_ids = lax.broadcasted_iota(jnp.int32, (rows, rows), 1)
-    exact = dict(precision=lax.Precision.HIGHEST, preferred_element_type=F32)
-    columns[...] = jnp.dot((row_ids >= column_ids).astype(F32), jax.nn.sigmoid(by_row), **exact)
-    lanes[...] = jnp.dot(jax.nn.sigmoid(by_lane), (row_ids <= column_ids).astype(F32), **exact)
+    sums = jnp.dot(
+        (row_ids >= column_ids).astype(BF16), terms.astype(BF16), preferred_element_type=F32
+    )
+    columns[...] = sums[:, 0:4] + sums[:, 4:8] + sums[:, 8:12]
+    by_row = sums.T
+    lanes[...] = by_row[0:4] + by_row[4:8] + by_row[8:12]
+
+
+def silu_of(gates):
+    gates = gates.astype(BF16).astype(F32)
+    return (gates * jax.nn.sigmoid(gates)).astype(BF16)
 
 
 def chunk_state(head, key, value, columns, ceiling, burst):
@@ -220,35 +235,28 @@
     columns,
     lanes,
 ):
-    part = pl.program_id(0)
-
-    @pl.when(part == 0)
-    def _():
-        normalize(place_ref[0], (own, left, right, far_a, far_b), gain_ref, normed)
-
-    parts[part] = product(normed, weight).astype(BF16)
-
-    @pl.when(part == 3)
-    def _():
-        decay_sums(normed, decay_ref, columns, lanes)
-        gate_out[...] = parts[3]
-        for head in range(4):
-            ceiling = ceiling_ref[head]
-            state, span = chunk_state(head, parts.at[1], parts.at[2], columns, ceiling, 0.0)
-            state_out[head * 8 : (head + 1) * 8] = state
-            span_out[head : head + 1] = jnp.broadcast_to(span, (1, HEAD_WIDTH))
-            attend(
-                head,
-                parts.at[0],
-                parts.at[1],
-                parts.at[2],
-                columns,
-                lanes,
-                ceiling,
-                0.0,
-                query_out,
-                inner_out,
-            )
+    normalize(place_ref[0], (own, left, right, far_a, far_b), gain_ref, normed)
+    decay_sums(normed, decay_ref, columns, lanes)
+    for part in range(3):
+        parts[part] = product(normed, weight[part]).astype(BF16)
+    gate_out[...] = silu_of(product(normed, weight[3]))
+    for head in range(4):
+        ceiling = ceiling_ref[head]
+        state, span = chunk_state(head, parts.at[1], parts.at[2], columns, ceiling, 0.0)
+        state_out[head * 8 : (head + 1) * 8] = state
+        span_out[head : head + 1] = jnp.broadcast_to(span, (1, HEAD_WIDTH))
+        attend(
+            head,
+            parts.at[0],
+            parts.at[1],
+            parts.at[2],
+            columns,
+            lanes,
+            ceiling,
+            0.0,
+            query_out,
+            inner_out,
+        )
 
 
 def image_state_kernel(
@@ -265,40 +273,42 @@
     decay_ref,
     other_state,
     other_span,
-    normed,
-    key_value,
+    normed_out,
+    key_value_out,
     columns,
     lanes,
     state_out,
+    normed,
+    key_value,
+    sems,
 ):
-    part = pl.program_id(0)
-
-    @pl.when(part == 0)
-    def _():
-        normalize(place_ref[0], (own, left, right, far_a, far_b), gain_ref, normed)
-        state_out[:, 0:16, :] = other_state[...]
-
-    key_value[part] = product(normed, weight).astype(BF16)
-
-    @pl.when(part == 1)
-    def _():
-        decay_sums(normed, decay_ref, columns, lanes)
-        burst = jnp.log1p(jnp.full((1, 1), -forget_ref[place_ref[1]], F32))
-        ids = lax.broadcasted_iota(jnp.int32, (8, HEAD_WIDTH), 0)
-        for head in range(4):
-            state, span = chunk_state(
-                head, key_value.at[0], key_value.at[1], columns, ceiling_ref[head], burst
-            )
-            targets = slice(head * 8, (head + 1) * 8)
-            state_out[targets, 16:32, :] = state
-            tile = jnp.zeros((8, HEAD_WIDTH), F32)
-            for kind, value in enumerate((other_span[head : head + 1, 0:1], span)):
-                upper = value.astype(BF16).astype(F32)
-                tile = jnp.where(ids == 2 * kind, upper, tile)
-                tile = jnp.where(ids == 2 * kind + 1, value - upper, tile)
-            state_out[targets, 32:40, :] = jnp.broadcast_to(
-                tile.astype(BF16)[None], (8, 8, HEAD_WIDTH)
-            )
+    normalize(place_ref[0], (own, left, right, far_a, far_b), gain_ref, normed)
+    key_value[0] = product(normed, weight[1]).astype(BF16)
+    normed_copy = pltpu.make_async_copy(normed, normed_out, sems.at[0])
+    normed_copy.start()
+    key_value[1] = product(normed, weight[2]).astype(BF16)
+    decay_sums(normed, decay_ref, columns, lanes)
+    key_value_copy = pltpu.make_async_copy(key_value, key_value_out, sems.at[1])
+    key_value_copy.start()
+    state_out[:, 0:16, :] = other_state[...]
+    burst = jnp.log1p(jnp.full((1, 1), -forget_ref[place_ref[1]], F32))
+    ids = lax.broadcasted_iota(jnp.int32, (8, HEAD_WIDTH), 0)
+    for head in range(4):
+        state, span = chunk_state(
+            head, key_value.at[0], key_value.at[1], columns, ceiling_ref[head], burst
+        )
+        targets = slice(head * 8, (head + 1) * 8)
+        state_out[targets, 16:32, :] = state
+        tile = jnp.zeros((8, HEAD_WIDTH), F32)
+        for kind, value in enumerate((other_span[head : head + 1, 0:1], span)):
+            upper = value.astype(BF16).astype(F32)
+            tile = jnp.where(ids == 2 * kind, upper, tile)
+            tile = jnp.where(ids == 2 * kind + 1, value - upper, tile)
+        state_out[targets, 32:40, :] = jnp.broadcast_to(
+            tile.astype(BF16)[None], (8, 8, HEAD_WIDTH)
+        )
+    normed_copy.wait()
+    key_value_copy.wait()
 
 
 def image_attend_kernel(
@@ -316,15 +326,15 @@
     query,
 ):
     part = pl.program_id(0)
-    block = product(normed, weight).astype(BF16)
+    block = product(normed, weight[0])
 
     @pl.when(part == 0)
     def _():
-        query[...] = block
+        query[...] = block.astype(BF16)
 
     @pl.when(part == 1)
     def _():
-        gate_out[...] = block
+        gate_out[...] = silu_of(block)
         burst = jnp.log1p(jnp.full((1, 1), -forget_ref[place_ref[1]], F32))
         for head in range(4):
             attend(
@@ -347,15 +357,12 @@
     )
 
 
-def weight_spec(weight, column):
-    return [pl.BlockSpec((weight.shape[0], weight.shape[1] // 4), lambda p: (0, column(p)))]
-
-
-def relay_kernel(source, out):
-    width = source.shape[2]
+def relay_kernel(source, out, late):
+    rows = source.shape[0]
     moved_rows = jnp.swapaxes(source[...], 0, 1)
-    for part in range(4):
-        out[:, part * width : (part + 1) * width] = moved_rows[part]
+    out[:, pl.ds(pl.multiple_of(pl.program_id(0) * rows, rows), rows), :] = moved_rows
+    late[0] = moved_rows[0]
+    late[1] = moved_rows[3]
 
 
 def relay_call(in_proj):
@@ -364,10 +371,10 @@
     return pl.pallas_call(
         relay_kernel,
         grid=(depth // rows,),
-        out_shape=hbm_of(depth, parts * width),
+        out_shape=(pltpu.VMEM((parts, depth, width), BF16), hbm_of(2, depth, width)),
         in_specs=[pl.BlockSpec((rows, parts, width), lambda b: (b, 0, 0))],
-        out_specs=pl.BlockSpec((rows, parts * width), lambda b: (b, 0)),
-        compiler_params=limit(8, "arbitrary"),
+        out_specs=(VMEM, pl.BlockSpec((2, rows, width), lambda b: (0, b, 0))),
+        compiler_params=limit(18, "arbitrary"),
         name="relay",
     )(*in_hbm(in_proj))
 
@@ -382,26 +389,23 @@
         shape_of(32, 16, HEAD_WIDTH),
         shape_of(4, HEAD_WIDTH, dtype=F32),
     )
+    arrays = (*chunks, gain, weights, decay)
     return pl.pallas_call(
         text_kernel,
-        grid=(4,),
+        grid=(1,),
         out_shape=outs,
-        in_specs=[SMEM, SMEM]
-        + [fixed(*c.shape) for c in chunks]
-        + [fixed(1, depth)]
-        + weight_spec(weights, lambda p: p)
-        + [fixed(*decay.shape)],
+        in_specs=[SMEM, SMEM] + [VMEM] * len(arrays),
         out_specs=tuple(fixed(*o.shape) for o in outs),
         scratch_shapes=[
             pltpu.VMEM((rows, depth), BF16),
-            pltpu.VMEM((4, rows, width), BF16),
+            pltpu.VMEM((3, rows, width), BF16),
             pltpu.VMEM((rows, 4), F32),
             pltpu.VMEM((4, rows), F32),
         ],
-        compiler_params=limit(20, "arbitrary"),
+        compiler_params=limit(24, "arbitrary"),
         cost_estimate=cost_of(rows, depth, 4 * width),
         name="text_unit",
-    )(place, ceiling, *chunks, gain, *in_hbm(weights), decay)
+    )(place, ceiling, *arrays)
 
 
 def image_state_call(place, ceiling, forget, chunks, gain, weights, decay, state, span):
@@ -414,20 +418,21 @@
         shape_of(4, rows, dtype=F32),
         shape_of(32, 40, HEAD_WIDTH),
     )
+    arrays = (*chunks, gain, weights, decay, state, span)
     return pl.pallas_call(
         image_state_kernel,
-        grid=(2,),
         out_shape=outs,
-        in_specs=[SMEM] * 3
-        + [fixed(*c.shape) for c in chunks]
-        + [fixed(1, depth)]
-        + weight_spec(weights, lambda p: p + 1)
-        + [fixed(*decay.shape), fixed(*state.shape), fixed(*span.shape)],
-        out_specs=tuple(fixed(*o.shape) for o in outs),
-        compiler_params=limit(20, "arbitrary"),
+        in_specs=[SMEM] * 3 + [VMEM] * len(arrays),
+        out_specs=(HBM, HBM, VMEM, VMEM, VMEM),
+        scratch_shapes=[
+            pltpu.VMEM((rows, depth), BF16),
+            pltpu.VMEM((2, rows, width), BF16),
+            pltpu.SemaphoreType.DMA((2,)),
+        ],
+        compiler_params=limit(24),
         cost_estimate=cost_of(rows, depth, 2 * width),
         name="image_state",
-    )(place, ceiling, forget, *chunks, gain, *in_hbm(weights), decay, state, span)
+    )(place, ceiling, forget, *arrays)
 
 
 def image_attend_call(place, ceiling, forget, weights, normed, key_value, columns, lanes):
@@ -445,7 +450,7 @@
         out_shape=outs,
         in_specs=[SMEM] * 3
         + [fixed(*h.shape) for h in held]
-        + weight_spec(weights, lambda p: 3 * p),
+        + [pl.BlockSpec((1, depth, width), lambda p: (p, 0, 0))],
         out_specs=tuple(fixed(*o.shape) for o in outs),
         scratch_shapes=[pltpu.VMEM((rows, width), BF16)],
         compiler_params=limit(20, "arbitrary"),
@@ -492,24 +497,19 @@
     )(starts, states)
 
 
-def output_kernel(
-    place_ref,
-    entering,
-    out_gain,
-    out_proj,
-    query_t,
-    gate_t,
-    inner_t,
-    query_i,
-    gate_i,
-    inner_i,
-    *outs,
-):
-    gated_refs = outs[8:]
-    outs = outs[:8]
-    _, width = query_t.shape
-    refs = ((query_t, gate_t, inner_t), (query_i, gate_i, inner_i))
-    for kind, (query, gate, inner) in enumerate(refs):
+def gate_kernel(place_ref, entering, out_gain, out_proj, *refs):
+    sources, (far_text, far_image, gated), buffers, sems = refs[:6], refs[6:9], refs[9:15], refs[15]
+    copies = [
+        pltpu.make_async_copy(source, buffer, sems.at[at])
+        for at, (source, buffer) in enumerate(zip(sources, buffers))
+    ]
+    for copy in copies:
+        copy.start()
+    rows, width = far_text.shape
+    for kind in range(2):
+        for copy in copies[3 * kind : 3 * kind + 3]:
+            copy.wait()
+        query, gate, inner = buffers[3 * kind : 3 * kind + 3]
         for head in range(width // HEAD_WIDTH):
             lanes = slice(head * HEAD_WIDTH, (head + 1) * HEAD_WIDTH)
             state = entering[head * 8 : (head + 1) * 8, kind * 16 : (kind + 1) * 16, :]
@@ -517,31 +517,51 @@
                 query[:, lanes], state.reshape(HEAD_WIDTH, HEAD_WIDTH), preferred_element_type=F32
             )
             scale = lax.rsqrt(jnp.mean(attended * attended, axis=-1, keepdims=True) + EPSILON)
-            gates = gate[:, lanes].astype(F32)
-            value = attended * scale * out_gain[head : head + 1, :] * (gates * jax.nn.sigmoid(gates))
-            gated_refs[kind][:, lanes] = value.astype(BF16)
-    for slot, step in enumerate((2, 1, 3, 0)):
+            value = attended * scale * out_gain[head : head + 1, :] * gate[:, lanes].astype(F32)
+            gated[kind * rows : (kind + 1) * rows, lanes] = value.astype(BF16)
+    weight = out_proj[:, columns_of(place_ref[0], 2, 4, width)]
+    block = jnp.dot(gated[...], weight, preferred_element_type=F32).astype(BF16)
+    far_text[...] = block[:rows]
+    far_image[...] = block[rows:]
+
+
+def gate_call(place, entering, out_gain, out_proj, text_parts, image_parts):
+    rows, width = text_parts[0].shape
+    outs = (shape_of(rows, width), shape_of(rows, width), shape_of(2 * rows, width))
+    parts = in_hbm(*text_parts, *image_parts)
+    return pl.pallas_call(
+        gate_kernel,
+        out_shape=outs,
+        in_specs=[SMEM] + [VMEM] * 3 + [HBM] * 6,
+        out_specs=(VMEM,) * 3,
+        scratch_shapes=[pltpu.VMEM(p.shape, p.dtype) for p in parts]
+        + [pltpu.SemaphoreType.DMA((6,))],
+        compiler_params=limit(16),
+        name="gate_far",
+    )(place, entering, out_gain, out_proj, *parts)
+
+
+def near_kernel(place_ref, gated, out_proj, next_t, next_i, last_t, last_i, own_t, own_i):
+    rows, width = next_t.shape
+    for step, text, image in ((1, next_t, next_i), (3, last_t, last_i), (0, own_t, own_i)):
         weight = out_proj[:, columns_of(place_ref[0], step, 4, width)]
-        for kind in range(2):
-            block = jnp.dot(gated_refs[kind][...], weight, preferred_element_type=F32)
-            ref = outs[2 * slot + kind]
-            ref[...] = block.astype(ref.dtype)
-
-
-def output_call(place, entering, out_gain, out_proj, text_parts, image_parts):
-    rows, width = text_parts[0].shape
-    outs = (shape_of(rows, width),) * 6 + (shape_of(rows, width, dtype=F32),) * 2
-    arrays = (entering, out_gain, out_proj, *in_hbm(*text_parts, *image_parts))
-    return pl.pallas_call(
-        output_kernel,
-        grid=(1,),
+        block = jnp.dot(gated[...], weight, preferred_element_type=F32)
+        text[...] = block[:rows].astype(text.dtype)
+        image[...] = block[rows:].astype(image.dtype)
+
+
+def near_call(place, gated, out_proj):
+    rows, width = gated.shape[0] // 2, gated.shape[1]
+    outs = (shape_of(rows, width),) * 4 + (shape_of(rows, width, dtype=F32),) * 2
+    return pl.pallas_call(
+        near_kernel,
         out_shape=outs,
-        in_specs=[SMEM] + [fixed(*a.shape) for a in arrays],
-        out_specs=tuple(fixed(*o.shape) for o in outs),
-        scratch_shapes=[pltpu.VMEM((rows, width), BF16)] * 2,
-        compiler_params=limit(20, "arbitrary"),
-        name="output_blocks",
-    )(place, *arrays)
+        in_specs=[SMEM, VMEM, VMEM],
+        out_specs=(VMEM,) * 6,
+        compiler_params=limit(16),
+        cost_estimate=cost_of(2 * rows, width, 3 * width),
+        name="near_blocks",
+    )(place, gated, out_proj)
 
 
 def moved(array, step):
@@ -583,7 +603,7 @@
     to_next, to_last, near_next, near_last, own = adapter_sums(
         place, image_patches.transpose(0, 2, 1), adapter
     )
-    weights = relay_call(in_proj)
+    weights, late_weights = relay_call(in_proj)
     from_left = moved(to_next, 1)
     from_right = moved(to_last, 3)
     next_sum, last_sum = pass_call(from_left, from_right, near_next, near_last)
@@ -599,12 +619,15 @@
         place, ceiling, image_forget, image_chunks, gain, weights, decay, text_state, text_span
     )
     slices = lax.all_to_all(states, SEQ, 0, 0, tiled=True)
-    image_parts = image_attend_call(place, ceiling, image_forget, weights, *held)
+    image_parts = image_attend_call(
+        place, ceiling, image_forget, late_weights, *held
+    )
     entering = lax.all_to_all(scan_call(image_start, slices), SEQ, 0, 0, tiled=True)
 
-    far_t, far_i, next_t, next_i, last_t, last_i, own_t, own_i = output_call(
+    far_t, far_i, gated = gate_call(
         place, entering, out_gain, out_proj, text_parts, image_parts
     )
+    next_t, next_i, last_t, last_i, own_t, own_i = near_call(place, gated, out_proj)
     far_from_left = moved(far_t, 1)
     far_from_right = moved(far_i, 3)
     left_i = moved(next_i, 1)

time: 120 us -> 114 us (0.950)
  Pallas kernels: 37.7 us -> 33.3 us
  local copies, waits for them, and re-layouts: 2.27 us -> 0.09 us
  waiting for transfers between devices: 27 us -> 25 us
  starting transfers between devices: 25.8 us -> 27.1 us
  blocking collectives: 22.9 us -> 24.1 us
    pallas_call x4 -> x5, Pallas kernels: 28.5 us -> 22.6 us  [the longest x1 8.46 us: relay_call(): pl.pallas_call(relay_kernel, grid=(depth // rows,), out_shape=(pltpu.VMEM...]
    unnamed x20 -> x16, local copies, waits for them, and re-layouts: 2.23 us -> 0.05 us
    ppermute x18, waiting for transfers between devices: 23.3 us -> 21.2 us  [moved(): return lax.ppermute(array, 'head', [(i, (i + step) % 4) for i in range(4)])]
    pallas_call x1, Pallas kernels: 2.17 us -> 3.69 us  [adapter_sums(): pl.pallas_call(adapter_kernel, out_shape=outs, grid_spec=pltpu.PrefetchSc...]
    ppermute x18, starting transfers between devices: 22 us -> 23.4 us  [moved(): return lax.ppermute(array, 'head', [(i, (i + step) % 4) for i in range(4)])]
  transfers between devices with their start and end apart: 19 -> 19, of which waited for: 7 -> 8; matrix products, arithmetic and copies ran while one was open for 1% -> 1% of each run, Pallas kernels for 20% -> 19%
where the time goes in v2:
time: 114 us; the launch traced here: 112 us
  Pallas kernels  33.3 us (29%)
  starting transfers between devices  27.1 us (24%)
  waiting for transfers between devices  25 us (22%)
  blocking collectives  24.1 us (21%)
  other arithmetic  1.91 us (2%)
    all_to_all x1, blocking collectives, steps(): slices = lax.all_to_all(states, SEQ, 0, 0, tiled=True)  24.1 us
    ppermute x18, starting transfers between devices, moved(): return lax.ppermute(array, 'head', [(i, (i + step) % 4) for i in range(4)])  23.4 us
    ppermute x18, waiting for transfers between devices, moved(): return lax.ppermute(array, 'head', [(i, (i + step) % 4) for i in range(4)])  21.2 us
    pallas_call x1, Pallas kernels, relay_call(): pl.pallas_call(relay_kernel, grid=(depth // rows,), out_shape=(pltpu.VMEM...  8.46 us
    pallas_call x1, Pallas kernels, text_call(): pl.pallas_call(text_kernel, grid=(1,), out_shape=outs, in_specs=[SMEM, SM...  5.65 us
    pallas_call x1, Pallas kernels, image_attend_call(): pl.pallas_call(image_attend_kernel, grid=(2,), out_shape=outs, in_specs=[...  5.19 us
    pallas_call x1, Pallas kernels, image_state_call(): pl.pallas_call(image_state_kernel, out_shape=outs, in_specs=[SMEM] * 3 +...  4.15 us
    all_to_all x1, waiting for transfers between devices, steps(): lax.all_to_all(scan_call(image_start, slices), SEQ, 0, 0, tiled=True)  3.85 us
  transfers between devices with their start and end apart: 19, of which 8 were waited for; matrix products, arithmetic and copies ran while one was open for 1% of the time, Pallas kernels for 19%

profile of v2, /device:TPU:1, one launch (start us, length us, event | category | flops | bytes accessed | tf_op | source)
XLA Modules:
  0.0 112.4 jit_solution(14284753483919033291)
XLA Ops:
  0.6 0.1 pad_add_fusion.place_ref
  0.7 3.7 %adapter_sums.1 = (bf16[256,512]{1,0:T(8,128)(2,1)S(1)}, bf16[256,512]{1,0:T(8,128)(2,1)S(1)}, bf16[128,512]{1,0:T(8,128)(2,1)S(1)}, bf16[128,512]{1,0:T(8,128)(2,1)S(1)}, f32[256,512]{1,0:T(8,128)S(1)}) custom-call(s32[2]{0:T(128)S(1)} %pad_add_fusion.place_ref, bf16[1,288,256]{2,1,0:T(8,128)(2,1)} %bitcast.11, bf16[288,2048]{1,0:T(8,128)(2,1)} %adapter_ref.1), custom_call_target="tpu_custom_call" | custom-call | tf_op jit(solution)/shard_map/adapter_sums/pallas_call | solution.py:90
  4.4 2.1 %collective-permute-start = (bf16[256,512]{1,0:T(8,128)(2,1)S(1)}, bf16[256,512]{1,0:T(8,128)(2,1)S(1)}, u32[]{:S(2)}, u32[]{:S(2)}) collective-permute-start(bf16[256,512]{1,0:T(8,128)(2,1)S(1)} %get-tuple-element.34), channel_id=1, source_target_pairs={{0,1},{1,2},{2,3},{3,0},{4,5},{5,6},{6,7},{7,4},{8,9},{9,10},{10,1... | collective-permute-start | bytes 786440 | tf_op jit(solution)/shard_map/ppermute | solution.py:568
  6.5 1.4 %collective-permute-start.1 = (bf16[256,512]{1,0:T(8,128)(2,1)S(1)}, bf16[256,512]{1,0:T(8,128)(2,1)S(1)}, u32[]{:S(2)}, u32[]{:S(2)}) collective-permute-start(bf16[256,512]{1,0:T(8,128)(2,1)S(1)} %get-tuple-element.35), channel_id=1, source_target_pairs={{0,3},{1,0},{2,1},{3,2},{4,7},{5,4},{6,5},{7,6},{8,11},{9,8},{10,9... | collective-permute-start | bytes 786440 | tf_op jit(solution)/shard_map/ppermute | solution.py:568
  7.9 5.6 %collective-permute-done.from_left = bf16[256,512]{1,0:T(8,128)(2,1)S(1)} collective-permute-done((bf16[256,512]{1,0:T(8,128)(2,1)S(1)}, bf16[256,512]{1,0:T(8,128)(2,1)S(1)}, u32[]{:S(2)}, u32[]{:S(2)}) %collective-permute-start) | collective-permute-done | bytes 262176 | tf_op jit(solution)/shard_map/ppermute | solution.py:568
  13.4 0.1 pass_on.1
  13.5 1.3 %collective-permute-start.2 = (bf16[128,512]{1,0:T(8,128)(2,1)S(1)}, bf16[128,512]{1,0:T(8,128)(2,1)S(1)}, u32[]{:S(2)}, u32[]{:S(2)}) collective-permute-start(bf16[128,512]{1,0:T(8,128)(2,1)S(1)} %get-tuple-element.38), channel_id=1, source_target_pairs={{0,1},{1,2},{2,3},{3,0},{4,5},{5,6},{6,7},{7,4},{8,9},{9,10},{10,1... | collective-permute-start | bytes 393224 | tf_op jit(solution)/shard_map/ppermute | solution.py:568
  14.8 1.5 %collective-permute-start.3 = (bf16[128,512]{1,0:T(8,128)(2,1)S(1)}, bf16[128,512]{1,0:T(8,128)(2,1)S(1)}, u32[]{:S(2)}, u32[]{:S(2)}) collective-permute-start(bf16[128,512]{1,0:T(8,128)(2,1)S(1)} %get-tuple-element.39), channel_id=1, source_target_pairs={{0,3},{1,0},{2,1},{3,2},{4,7},{5,4},{6,5},{7,6},{8,11},{9,8},{10,9... | collective-permute-start | bytes 393224 | tf_op jit(solution)/shard_map/ppermute | solution.py:568
  16.2 1.3 %collective-permute-start.9 = (bf16[256,512]{1,0:T(8,128)(2,1)}, bf16[256,512]{1,0:T(8,128)(2,1)S(1)}, u32[]{:S(2)}, u32[]{:S(2)}) collective-permute-start(bf16[256,512]{1,0:T(8,128)(2,1)} %own.1), channel_id=1, source_target_pairs={{0,3},{1,0},{2,1},{3,2},{4,7},{5,4},{6,5},{7,6},{8,11},{9,8},{10,9... | collective-permute-start | bytes 786440 | tf_op jit(solution)/shard_map/ppermute | solution.py:568
  17.6 0.1 collective-permute-start.8
  17.7 0.9 collective-permute-done.2.left
  18.6 0.1 embed.1.own
  18.7 2.7 %collective-permute-start.5 = (bf16[256,512]{1,0:T(8,128)(2,1)S(1)}, bf16[256,512]{1,0:T(8,128)(2,1)S(1)}, u32[]{:S(2)}, u32[]{:S(2)}) collective-permute-start(bf16[256,512]{1,0:T(8,128)(2,1)S(1)} %embed.1.own), channel_id=1, source_target_pairs={{0,3},{1,0},{2,1},{3,2},{4,7},{5,4},{6,5},{7,6},{8,11},{9,8},{10,9... | collective-permute-start | bytes 786440 | tf_op jit(solution)/shard_map/ppermute | solution.py:568
  21.4 2.5 %collective-permute-done.9.right = bf16[256,512]{1,0:T(8,128)(2,1)S(1)} collective-permute-done((bf16[256,512]{1,0:T(8,128)(2,1)}, bf16[256,512]{1,0:T(8,128)(2,1)S(1)}, u32[]{:S(2)}, u32[]{:S(2)}) %collective-permute-start.9) | collective-permute-done | bytes 262176 | tf_op jit(solution)/shard_map/ppermute | solution.py:568
  23.9 2.5 %collective-permute-start.11 = (bf16[128,512]{1,0:T(8,128)(2,1)S(1)}, bf16[128,512]{1,0:T(8,128)(2,1)S(1)}, u32[]{:S(2)}, u32[]{:S(2)}) collective-permute-start(bf16[128,512]{1,0:T(8,128)(2,1)S(1)} %slice.19), channel_id=1, source_target_pairs={{0,3},{1,0},{2,1},{3,2},{4,7},{5,4},{6,5},{7,6},{8,11},{9,8},{10,9... | collective-permute-start | bytes 393224 | tf_op jit(solution)/shard_map/ppermute | solution.py:568
  26.4 0.0 copy-start.1
  26.4 0.0 copy-start.2
  26.5 0.0 copy-start.3
  26.5 0.0 copy-start.4
  26.5 0.1 collective-permute-start.10
  26.6 8.5 %relay.1 = (bf16[4,2048,512]{2,1,0:T(8,128)(2,1)S(1)}, bf16[2,2048,512]{2,1,0:T(8,128)(2,1)}) custom-call(bf16[2048,4,512]{2,1,0:T(4,128)(2,1)} %source.1), custom_call_target="tpu_custom_call" | custom-call | tf_op jit(solution)/shard_map/relay/pallas_call | solution.py:371
  35.0 2.7 %collective-permute-start.7 = (bf16[128,512]{1,0:T(8,128)(2,1)S(1)}, bf16[128,512]{1,0:T(8,128)(2,1)S(1)}, u32[]{:S(2)}, u32[]{:S(2)}) collective-permute-start(bf16[128,512]{1,0:T(8,128)(2,1)S(1)} %slice.17), channel_id=1, source_target_pairs={{0,3},{1,0},{2,1},{3,2},{4,7},{5,4},{6,5},{7,6},{8,11},{9,8},{10,9... | collective-permute-start | bytes 393224 | tf_op jit(solution)/shard_map/ppermute | solution.py:568
  37.8 0.1 collective-permute-start.6
  37.9 0.0 copy-start.6
  37.9 5.6 %text_unit.1 = (bf16[256,512]{1,0:T(8,128)(2,1)}, bf16[256,512]{1,0:T(8,128)(2,1)}, f32[256,512]{1,0:T(8,128)}, bf16[32,16,128]{2,1,0:T(8,128)(2,1)S(1)}, f32[4,128]{1,0:T(4,128)S(1)}) custom-call(s32[2]{0:T(128)S(1)} %pad_add_fusion.place_ref, f32[4]{0:T(128)S(1)} %copy-done.4, bf16[256,512]{1,0:T(8,128)(2,1)S(1)} %copy-done.1, ...), custom_call_target="tpu_custom_call" | custom-call | flops 2147483648 | bytes 8388608 | tf_op jit(solution)/shard_map/text_unit/pallas_call | solution.py:393
  43.6 4.2 %image_state.1 = (bf16[256,2048]{1,0:T(8,128)(2,1)}, bf16[2,256,512]{2,1,0:T(8,128)(2,1)}, f32[256,4]{1,0:T(8,128)S(1)}, f32[4,256]{1,0:T(4,128)S(1)}, bf16[32,40,128]{2,1,0:T(8,128)(2,1)S(1)}) custom-call(s32[2]{0:T(128)S(1)} %pad_add_fusion.place_ref, f32[4]{0:T(128)S(1)} %copy-done.4, f32[32]{0:T(128)S(1)} %copy-done.6, bf16[256,512]{1,0:T(8,128)(2,1)S(1)} %embed.1.own, ...), custom_call_target="tpu_custom_call" | custom-call | flops 1073741824 | bytes 4194304 | tf_op jit(solution)/shard_map/image_state/pallas_call | solution.py:422
  47.8 0.0 copy-start
  47.8 0.0 copy-start.5
  47.8 24.1 %all_to_all.10.states = bf16[32,40,128]{2,1,0:T(8,128)(2,1)S(1)} all-to-all(bf16[32,40,128]{2,1,0:T(8,128)(2,1)S(1)} %get-tuple-element.43), channel_id=1, replica_groups=mesh['seq_0'=4,'seq_1'=4,'seq_2'=2,'head'=4] {'seq_0','seq_1','seq_2'}, dimensions={0} | all-to-all | bytes 655360 | tf_op jit(solution)/shard_map/all_to_all | solution.py:621
  71.9 1.7 %state_scan.1 = bf16[32,32,128]{2,1,0:T(8,128)(2,1)} custom-call(s32[32]{0:T(128)S(1)} %copy-done.7, bf16[32,40,128]{2,1,0:T(8,128)(2,1)S(1)} %all_to_all.10.states), custom_call_target="tpu_custom_call" | custom-call | tf_op jit(solution)/shard_map/state_scan/pallas_call | solution.py:486
  73.6 3.7 %all-to-all-start.1 = ((bf16[32,32,128]{2,1,0:T(8,128)(2,1)}), bf16[32,32,128]{2,1,0:T(8,128)(2,1)S(1)}, u32[]{:S(2)}, u32[]{:S(2)}) async-start(bf16[32,32,128]{2,1,0:T(8,128)(2,1)} %state_scan.1), calls=%async_computation.1 | async-start | bytes 524288 | tf_op jit(solution)/shard_map/all_to_all | solution.py:625
  77.2 5.2 %image_attend.1 = (bf16[256,512]{1,0:T(8,128)(2,1)}, bf16[256,512]{1,0:T(8,128)(2,1)}, f32[256,512]{1,0:T(8,128)}) custom-call(s32[2]{0:T(128)S(1)} %pad_add_fusion.place_ref, f32[4]{0:T(128)S(1)} %copy-done.4, f32[32]{0:T(128)S(1)} %copy-done.6, bf16[256,2048]{1,0:T(8,128)(2,1)} %get-tuple-element.47.normed, ...), custom_call_target="tpu_custom_call" | custom-call | flops 1073741824 | bytes 4194304 | tf_op jit(solution)/shard_map/image_attend/pallas_call | solution.py:447
  82.4 3.9 %all-to-all-done.1.entering = bf16[32,32,128]{2,1,0:T(8,128)(2,1)S(1)} async-done(((bf16[32,32,128]{2,1,0:T(8,128)(2,1)}), bf16[32,32,128]{2,1,0:T(8,128)(2,1)S(1)}, u32[]{:S(2)}, u32[]{:S(2)}) %all-to-all-start.1) | async-done | bytes 262176 | tf_op jit(solution)/shard_map/all_to_all | solution.py:625
  86.3 2.8 %gate_far.1 = (bf16[256,512]{1,0:T(8,128)(2,1)S(1)}, bf16[256,512]{1,0:T(8,128)(2,1)S(1)}, bf16[512,512]{1,0:T(8,128)(2,1)S(1)}) custom-call(s32[2]{0:T(128)S(1)} %pad_add_fusion.place_ref, bf16[32,32,128]{2,1,0:T(8,128)(2,1)S(1)} %all-to-all-done.1.entering, f32[4,128]{1,0:T(4,128)S(1)} %copy-done.5, bf16[512,2048]{1,0:T(8,128)(2,1)S(1)} %copy-done, ...), custom_call_target="tpu_custom_call" | custom-call | tf_op jit(solution)/shard_map/gate_far/pallas_call | solution.py:532
  89.1 2.6 %collective-permute-start.13 = (bf16[256,512]{1,0:T(8,128)(2,1)S(1)}, bf16[256,512]{1,0:T(8,128)(2,1)S(1)}, u32[]{:S(2)}, u32[]{:S(2)}) collective-permute-start(bf16[256,512]{1,0:T(8,128)(2,1)S(1)} %get-tuple-element.59), channel_id=1, source_target_pairs={{0,3},{1,0},{2,1},{3,2},{4,7},{5,4},{6,5},{7,6},{8,11},{9,8},{10,9... | collective-permute-start | bytes 786440 | tf_op jit(solution)/shard_map/ppermute | solution.py:568
  91.7 1.5 %near_blocks.1 = (bf16[256,512]{1,0:T(8,128)(2,1)S(1)}, bf16[256,512]{1,0:T(8,128)(2,1)S(1)}, bf16[256,512]{1,0:T(8,128)(2,1)S(1)}, bf16[256,512]{1,0:T(8,128)(2...) custom-call(s32[2]{0:T(128)S(1)} %pad_add_fusion.place_ref, bf16[512,512]{1,0:T(8,128)(2,1)S(1)} %get-tuple-element.55.gated, ...), custom_call_target="tpu_custom_call" | custom-call | flops 805306368 | bytes 1572864 | tf_op jit(solution)/shard_map/near_blocks/pallas_call | solution.py:556
  93.2 0.1 collective-permute-start.12
  93.3 3.9 %collective-permute-done.13 = bf16[256,512]{1,0:T(8,128)(2,1)S(1)} collective-permute-done((bf16[256,512]{1,0:T(8,128)(2,1)S(1)}, bf16[256,512]{1,0:T(8,128)(2,1)S(1)}, u32[]{:S(2)}, u32[]{:S(2)}) %collective-permute-start.13) | collective-permute-done | bytes 262176 | tf_op jit(solution)/shard_map/ppermute | solution.py:568
  97.1 0.1 add_convert_fusion.3
  97.2 3.5 %collective-permute-start.14 = (bf16[256,512]{1,0:T(8,128)(2,1)S(1)}, bf16[256,512]{1,0:T(8,128)(2,1)S(1)}, u32[]{:S(2)}, u32[]{:S(2)}) collective-permute-start(bf16[256,512]{1,0:T(8,128)(2,1)S(1)} %add_convert_fusion.3), channel_id=1, source_target_pairs={{0,3},{1,0},{2,1},{3,2},{4,7},{5,4},{6,5},{7,6},{8,11},{9,8},{10,9... | collective-permute-start | bytes 786440 | tf_op jit(solution)/shard_map/ppermute | solution.py:568
  100.7 0.1 collective-permute-start.17
  100.8 0.1 add_convert_fusion.1
  100.8 1.5 %collective-permute-start.16 = (bf16[256,512]{1,0:T(8,128)(2,1)S(1)}, bf16[256,512]{1,0:T(8,128)(2,1)S(1)}, u32[]{:S(2)}, u32[]{:S(2)}) collective-permute-start(bf16[256,512]{1,0:T(8,128)(2,1)S(1)} %add_convert_fusion.1), channel_id=1, source_target_pairs={{0,1},{1,2},{2,3},{3,0},{4,5},{5,6},{6,7},{7,4},{8,9},{9,10},{10,1... | collective-permute-start | bytes 786440 | tf_op jit(solution)/shard_map/ppermute | solution.py:568
  102.3 3.6 %collective-permute-done.12 = bf16[256,512]{1,0:T(8,128)(2,1)S(1)} collective-permute-done((bf16[256,512]{1,0:T(8,128)(2,1)S(1)}, bf16[256,512]{1,0:T(8,128)(2,1)S(1)}, u32[]{:S(2)}, u32[]{:S(2)}) %collective-permute-start.12) | collective-permute-done | bytes 262176 | tf_op jit(solution)/shard_map/ppermute | solution.py:568
  105.9 0.9 fusion
  106.7 4.2 %collective-permute-done.17 = bf16[256,512]{1,0:T(8,128)(2,1)S(1)} collective-permute-done((bf16[256,512]{1,0:T(8,128)(2,1)S(1)}, bf16[256,512]{1,0:T(8,128)(2,1)S(1)}, u32[]{:S(2)}, u32[]{:S(2)}) %collective-permute-start.17) | collective-permute-done | bytes 262176 | tf_op jit(solution)/shard_map/ppermute | solution.py:568
  110.9 0.6 collective-permute-done.16
  111.5 0.9 add_convert_fusion
  (26 shorter events, 0.1 us)
Async XLA Ops:
  4.4 9.0 %collective-permute-start = (bf16[256,512]{1,0:T(8,128)(2,1)S(1)}, bf16[256,512]{1,0:T(8,128)(2,1)S(1)}, u32[]{:S(2)}, u32[]{:S(2)}) collective-permute-start(bf16[256,512]{1,0:T(8,128)(2,1)S(1)} %get-tuple-element.34), channel_id=1, source_target_pairs={{0,1},{1,2},{2,3},{3,0},{4,5},{5,6},{6,7},{7,4},{8,9},{9,10},{10,1... | collective-permute-start | bytes 786440 | tf_op jit(solution)/shard_map/ppermute | solution.py:568
  6.5 6.9 %collective-permute-start.1 = (bf16[256,512]{1,0:T(8,128)(2,1)S(1)}, bf16[256,512]{1,0:T(8,128)(2,1)S(1)}, u32[]{:S(2)}, u32[]{:S(2)}) collective-permute-start(bf16[256,512]{1,0:T(8,128)(2,1)S(1)} %get-tuple-element.35), channel_id=1, source_target_pairs={{0,3},{1,0},{2,1},{3,2},{4,7},{5,4},{6,5},{7,6},{8,11},{9,8},{10,9... | collective-permute-start | bytes 786440 | tf_op jit(solution)/shard_map/ppermute | solution.py:568
  13.5 5.1 %collective-permute-start.2 = (bf16[128,512]{1,0:T(8,128)(2,1)S(1)}, bf16[128,512]{1,0:T(8,128)(2,1)S(1)}, u32[]{:S(2)}, u32[]{:S(2)}) collective-permute-start(bf16[128,512]{1,0:T(8,128)(2,1)S(1)} %get-tuple-element.38), channel_id=1, source_target_pairs={{0,1},{1,2},{2,3},{3,0},{4,5},{5,6},{6,7},{7,4},{8,9},{9,10},{10,1... | collective-permute-start | bytes 393224 | tf_op jit(solution)/shard_map/ppermute | solution.py:568
  14.8 3.8 %collective-permute-start.3 = (bf16[128,512]{1,0:T(8,128)(2,1)S(1)}, bf16[128,512]{1,0:T(8,128)(2,1)S(1)}, u32[]{:S(2)}, u32[]{:S(2)}) collective-permute-start(bf16[128,512]{1,0:T(8,128)(2,1)S(1)} %get-tuple-element.39), channel_id=1, source_target_pairs={{0,3},{1,0},{2,1},{3,2},{4,7},{5,4},{6,5},{7,6},{8,11},{9,8},{10,9... | collective-permute-start | bytes 393224 | tf_op jit(solution)/shard_map/ppermute | solution.py:568
  16.2 7.7 %collective-permute-start.9 = (bf16[256,512]{1,0:T(8,128)(2,1)}, bf16[256,512]{1,0:T(8,128)(2,1)S(1)}, u32[]{:S(2)}, u32[]{:S(2)}) collective-permute-start(bf16[256,512]{1,0:T(8,128)(2,1)} %own.1), channel_id=1, source_target_pairs={{0,3},{1,0},{2,1},{3,2},{4,7},{5,4},{6,5},{7,6},{8,11},{9,8},{10,9... | collective-permute-start | bytes 786440 | tf_op jit(solution)/shard_map/ppermute | solution.py:568
  17.6 8.8 %collective-permute-start.8 = (bf16[256,512]{1,0:T(8,128)(2,1)}, bf16[256,512]{1,0:T(8,128)(2,1)S(1)}, u32[]{:S(2)}, u32[]{:S(2)}) collective-permute-start(bf16[256,512]{1,0:T(8,128)(2,1)} %own.1), channel_id=1, source_target_pairs={{0,1},{1,2},{2,3},{3,0},{4,5},{5,6},{6,7},{7,4},{8,9},{9,10},{10,1... | collective-permute-start | bytes 786440 | tf_op jit(solution)/shard_map/ppermute | solution.py:568
  18.7 16.3 %collective-permute-start.5 = (bf16[256,512]{1,0:T(8,128)(2,1)S(1)}, bf16[256,512]{1,0:T(8,128)(2,1)S(1)}, u32[]{:S(2)}, u32[]{:S(2)}) collective-permute-start(bf16[256,512]{1,0:T(8,128)(2,1)S(1)} %embed.1.own), channel_id=1, source_target_pairs={{0,3},{1,0},{2,1},{3,2},{4,7},{5,4},{6,5},{7,6},{8,11},{9,8},{10,9... | collective-permute-start | bytes 786440 | tf_op jit(solution)/shard_map/ppermute | solution.py:568
  21.4 16.3 %collective-permute-start.4 = (bf16[256,512]{1,0:T(8,128)(2,1)S(1)}, bf16[256,512]{1,0:T(8,128)(2,1)S(1)}, u32[]{:S(2)}, u32[]{:S(2)}) collective-permute-start(bf16[256,512]{1,0:T(8,128)(2,1)S(1)} %embed.1.own), channel_id=1, source_target_pairs={{0,1},{1,2},{2,3},{3,0},{4,5},{5,6},{6,7},{7,4},{8,9},{9,10},{10,1... | collective-permute-start | bytes 786440 | tf_op jit(solution)/shard_map/ppermute | solution.py:568
  23.9 13.9 %collective-permute-start.11 = (bf16[128,512]{1,0:T(8,128)(2,1)S(1)}, bf16[128,512]{1,0:T(8,128)(2,1)S(1)}, u32[]{:S(2)}, u32[]{:S(2)}) collective-permute-start(bf16[128,512]{1,0:T(8,128)(2,1)S(1)} %slice.19), channel_id=1, source_target_pairs={{0,3},{1,0},{2,1},{3,2},{4,7},{5,4},{6,5},{7,6},{8,11},{9,8},{10,9... | collective-permute-start | bytes 393224 | tf_op jit(solution)/shard_map/ppermute | solution.py:568
  26.4 11.5 %copy-start.1 = (bf16[256,512]{1,0:T(8,128)(2,1)S(1)}, bf16[256,512]{1,0:T(8,128)(2,1)}, u32[]{:S(2)}) copy-start(bf16[256,512]{1,0:T(8,128)(2,1)} %own.1) | copy-start | bytes 786436
  26.4 11.5 %copy-start.2 = (bf16[2048,4]{0,1:T(4,128)(2,1)S(1)}, bf16[2048,4]{0,1:T(4,128)(2,1)}, u32[]{:S(2)}) copy-start(bf16[2048,4]{0,1:T(4,128)(2,1)} %param.18) | copy-start | bytes 49156
  26.5 11.5 %copy-start.3 = (f32[2048]{0:T(1024)S(1)}, f32[2048]{0:T(1024)}, u32[]{:S(2)}) copy-start(f32[2048]{0:T(1024)} %param.16) | copy-start | bytes 24580
  26.5 11.4 %copy-start.4 = (f32[4]{0:T(128)S(1)}, f32[4]{0:T(128)}, u32[]{:S(2)}) copy-start(f32[4]{0:T(128)} %ceiling_ref.5) | copy-start | bytes 52
  26.5 11.4 %collective-permute-start.10 = (bf16[128,512]{1,0:T(8,128)(2,1)S(1)}, bf16[128,512]{1,0:T(8,128)(2,1)S(1)}, u32[]{:S(2)}, u32[]{:S(2)}) collective-permute-start(bf16[128,512]{1,0:T(8,128)(2,1)S(1)} %slice.18), channel_id=1, source_target_pairs={{0,1},{1,2},{2,3},{3,0},{4,5},{5,6},{6,7},{7,4},{8,9},{9,10},{10,1... | collective-permute-start | bytes 393224 | tf_op jit(solution)/shard_map/ppermute | solution.py:568
  35.0 8.5 %collective-permute-start.7 = (bf16[128,512]{1,0:T(8,128)(2,1)S(1)}, bf16[128,512]{1,0:T(8,128)(2,1)S(1)}, u32[]{:S(2)}, u32[]{:S(2)}) collective-permute-start(bf16[128,512]{1,0:T(8,128)(2,1)S(1)} %slice.17), channel_id=1, source_target_pairs={{0,3},{1,0},{2,1},{3,2},{4,7},{5,4},{6,5},{7,6},{8,11},{9,8},{10,9... | collective-permute-start | bytes 393224 | tf_op jit(solution)/shard_map/ppermute | solution.py:568
  37.8 5.8 %collective-permute-start.6 = (bf16[128,512]{1,0:T(8,128)(2,1)S(1)}, bf16[128,512]{1,0:T(8,128)(2,1)S(1)}, u32[]{:S(2)}, u32[]{:S(2)}) collective-permute-start(bf16[128,512]{1,0:T(8,128)(2,1)S(1)} %slice.16), channel_id=1, source_target_pairs={{0,1},{1,2},{2,3},{3,0},{4,5},{5,6},{6,7},{7,4},{8,9},{9,10},{10,1... | collective-permute-start | bytes 393224 | tf_op jit(solution)/shard_map/ppermute | solution.py:568
  37.9 5.7 %copy-start.6 = (f32[32]{0:T(128)S(1)}, f32[32]{0:T(128)}, u32[]{:S(2)}) copy-start(f32[32]{0:T(128)} %forget_ref.3) | copy-start | bytes 388
  43.6 28.3 %copy-start.7 = (s32[32]{0:T(128)S(1)}, s32[32]{0:T(128)}, u32[]{:S(2)}) copy-start(s32[32]{0:T(128)} %start_ref.1) | copy-start | bytes 388
  47.8 38.5 %copy-start = (bf16[512,2048]{1,0:T(8,128)(2,1)S(1)}, bf16[512,2048]{1,0:T(8,128)(2,1)}, u32[]{:S(2)}) copy-start(bf16[512,2048]{1,0:T(8,128)(2,1)} %out_proj.3) | copy-start | bytes 6291460
  47.8 38.5 %copy-start.5 = (f32[4,128]{1,0:T(4,128)S(1)}, f32[4,128]{1,0:T(4,128)}, u32[]{:S(2)}) copy-start(f32[4,128]{1,0:T(4,128)} %out_gain.1) | copy-start | bytes 6148
  73.6 12.7 %all-to-all-start.1 = ((bf16[32,32,128]{2,1,0:T(8,128)(2,1)}), bf16[32,32,128]{2,1,0:T(8,128)(2,1)S(1)}, u32[]{:S(2)}, u32[]{:S(2)}) async-start(bf16[32,32,128]{2,1,0:T(8,128)(2,1)} %state_scan.1), calls=%async_computation.1 | async-start | bytes 524288 | tf_op jit(solution)/shard_map/all_to_all | solution.py:625
  89.1 8.0 %collective-permute-start.13 = (bf16[256,512]{1,0:T(8,128)(2,1)S(1)}, bf16[256,512]{1,0:T(8,128)(2,1)S(1)}, u32[]{:S(2)}, u32[]{:S(2)}) collective-permute-start(bf16[256,512]{1,0:T(8,128)(2,1)S(1)} %get-tuple-element.59), channel_id=1, source_target_pairs={{0,3},{1,0},{2,1},{3,2},{4,7},{5,4},{6,5},{7,6},{8,11},{9,8},{10,9... | collective-permute-start | bytes 786440 | tf_op jit(solution)/shard_map/ppermute | solution.py:568
  91.7 9.1 %collective-permute-start.15 = (bf16[256,512]{1,0:T(8,128)(2,1)S(1)}, bf16[256,512]{1,0:T(8,128)(2,1)S(1)}, u32[]{:S(2)}, u32[]{:S(2)}) collective-permute-start(bf16[256,512]{1,0:T(8,128)(2,1)S(1)} %get-tuple-element.62), channel_id=1, source_target_pairs={{0,1},{1,2},{2,3},{3,0},{4,5},{5,6},{6,7},{7,4},{8,9},{9,10},{10,1... | collective-permute-start | bytes 786440 | tf_op jit(solution)/shard_map/ppermute | solution.py:568
  93.2 12.7 %collective-permute-start.12 = (bf16[256,512]{1,0:T(8,128)(2,1)S(1)}, bf16[256,512]{1,0:T(8,128)(2,1)S(1)}, u32[]{:S(2)}, u32[]{:S(2)}) collective-permute-start(bf16[256,512]{1,0:T(8,128)(2,1)S(1)} %get-tuple-element.57), channel_id=1, source_target_pairs={{0,1},{1,2},{2,3},{3,0},{4,5},{5,6},{6,7},{7,4},{8,9},{9,10},{10,1... | collective-permute-start | bytes 786440 | tf_op jit(solution)/shard_map/ppermute | solution.py:568
  97.2 8.7 %collective-permute-start.14 = (bf16[256,512]{1,0:T(8,128)(2,1)S(1)}, bf16[256,512]{1,0:T(8,128)(2,1)S(1)}, u32[]{:S(2)}, u32[]{:S(2)}) collective-permute-start(bf16[256,512]{1,0:T(8,128)(2,1)S(1)} %add_convert_fusion.3), channel_id=1, source_target_pairs={{0,3},{1,0},{2,1},{3,2},{4,7},{5,4},{6,5},{7,6},{8,11},{9,8},{10,9... | collective-permute-start | bytes 786440 | tf_op jit(solution)/shard_map/ppermute | solution.py:568
  100.7 10.2 %collective-permute-start.17 = (bf16[256,512]{1,0:T(8,128)(2,1)S(1)}, bf16[256,512]{1,0:T(8,128)(2,1)S(1)}, u32[]{:S(2)}, u32[]{:S(2)}) collective-permute-start(bf16[256,512]{1,0:T(8,128)(2,1)S(1)} %get-tuple-element.63), channel_id=1, source_target_pairs={{0,3},{1,0},{2,1},{3,2},{4,7},{5,4},{6,5},{7,6},{8,11},{9,8},{10,9... | collective-permute-start | bytes 786440 | tf_op jit(solution)/shard_map/ppermute | solution.py:568
  100.8 10.7 %collective-permute-start.16 = (bf16[256,512]{1,0:T(8,128)(2,1)S(1)}, bf16[256,512]{1,0:T(8,128)(2,1)S(1)}, u32[]{:S(2)}, u32[]{:S(2)}) collective-permute-start(bf16[256,512]{1,0:T(8,128)(2,1)S(1)} %add_convert_fusion.1), channel_id=1, source_target_pairs={{0,1},{1,2},{2,3},{3,0},{4,5},{5,6},{6,7},{7,4},{8,9},{9,10},{10,1... | collective-permute-start | bytes 786440 | tf_op jit(solution)/shard_map/ppermute | solution.py:568

commit v3 on v2

--- a/solution.py
+++ b/solution.py
@@ -44,32 +44,47 @@
     return pl.ds(pl.multiple_of(lax.rem(place + step, count) * width, width), width)
 
 
-def adapter_kernel(place_ref, patches_ref, adapter_ref, to_next, to_last, near_next, near_last, own):
-    step = pl.program_id(0)
+def adapter_kernel(
+    place_ref,
+    patches_ref,
+    adapter_ref,
+    to_next,
+    to_last,
+    near_next,
+    near_last,
+    own,
+    patches,
+    blocks,
+    sems,
+):
     half = near_next.shape[0]
-    block = lax.dot_general(
-        patches_ref[0], adapter_ref[...], (((0,), (0,)), ((), ())), preferred_element_type=F32
-    )
-    small = block.astype(BF16)
-
-    @pl.when(step == 0)
-    def _():
-        to_next[:half] = small[:half]
-        to_last[half:] = small[half:]
-
-    @pl.when(step == 1)
-    def _():
-        near_next[...] = small[:half]
-        to_next[half:] = small[half:]
-
-    @pl.when(step == 2)
-    def _():
-        to_last[:half] = small[:half]
-        near_last[...] = small[half:]
-
-    @pl.when(step == 3)
-    def _():
-        own[...] = block
+    width = own.shape[1]
+    patches_copy = pltpu.make_async_copy(patches_ref.at[0], patches, sems.at[0])
+    patches_copy.start()
+    copies = []
+    for at, step in enumerate((2, 1, 3, 0)):
+        columns = columns_of(place_ref[0], step, 4, width)
+        copies.append(
+            pltpu.make_async_copy(adapter_ref.at[:, columns], blocks.at[at], sems.at[at + 1])
+        )
+        copies[at].start()
+    patches_copy.wait()
+    rows = patches[...].T
+    for at in range(4):
+        copies[at].wait()
+        block = jnp.dot(rows, blocks[at], preferred_element_type=F32)
+        small = block.astype(BF16)
+        if at == 0:
+            to_next[:half] = small[:half]
+            to_last[half:] = small[half:]
+        elif at == 1:
+            near_next[...] = small[:half]
+            to_next[half:] = small[half:]
+        elif at == 2:
+            to_last[:half] = small[:half]
+            near_last[...] = small[half:]
+        else:
+            own[...] = block
 
 
 def adapter_sums(place, patches, adapter):
@@ -82,21 +97,17 @@
         shape_of(rows // 2, width),
         shape_of(rows, width, dtype=F32),
     )
-
-    def block_of(step, place_ref):
-        ahead = jnp.where(step == 0, 2, jnp.where(step == 2, 3, jnp.where(step == 1, 1, 0)))
-        return (0, lax.rem(place_ref[0] + ahead, 4))
-
     return pl.pallas_call(
         adapter_kernel,
         out_shape=outs,
-        grid_spec=pltpu.PrefetchScalarGridSpec(
-            num_scalar_prefetch=1,
-            grid=(4,),
-            in_specs=[fixed(*patches.shape), pl.BlockSpec((depth, width), block_of)],
-            out_specs=tuple(fixed(*o.shape) for o in outs),
-        ),
-        compiler_params=limit(8, "arbitrary"),
+        in_specs=[SMEM, HBM, HBM],
+        out_specs=(VMEM,) * 5,
+        scratch_shapes=[
+            pltpu.VMEM((depth, rows), BF16),
+            pltpu.VMEM((4, depth, width), BF16),
+            pltpu.SemaphoreType.DMA((5,)),
+        ],
+        compiler_params=limit(8),
         name="adapter_sums",
     )(place, *in_hbm(patches, adapter))
 
@@ -230,11 +241,18 @@
     inner_out,
     state_out,
     span_out,
+    late_out,
     normed,
     parts,
     columns,
     lanes,
+    sems,
 ):
+    copies = [
+        pltpu.make_async_copy(weight.at[3 * at], late_out.at[at], sems.at[at]) for at in range(2)
+    ]
+    for copy in copies:
+        copy.start()
     normalize(place_ref[0], (own, left, right, far_a, far_b), gain_ref, normed)
     decay_sums(normed, decay_ref, columns, lanes)
     for part in range(3):
@@ -257,6 +275,8 @@
             query_out,
             inner_out,
         )
+    for copy in copies:
+        copy.wait()
 
 
 def image_state_kernel(
@@ -357,24 +377,35 @@
     )
 
 
-def relay_kernel(source, out, late):
-    rows = source.shape[0]
-    moved_rows = jnp.swapaxes(source[...], 0, 1)
-    out[:, pl.ds(pl.multiple_of(pl.program_id(0) * rows, rows), rows), :] = moved_rows
-    late[0] = moved_rows[0]
-    late[1] = moved_rows[3]
+def relay_kernel(source, out, blocks, sems):
+    count, rows = blocks.shape[:2]
+    copies = [
+        pltpu.make_async_copy(source.at[pl.ds(at * rows, rows)], blocks.at[at], sems.at[at])
+        for at in range(count)
+    ]
+    for copy in copies:
+        copy.start()
+    for at in range(count):
+        copies[at].wait()
+        out[:, at * rows : (at + 1) * rows, :] = jnp.swapaxes(blocks[at], 0, 1)
 
 
 def relay_call(in_proj):
     depth, parts, width = in_proj.shape
-    rows = 256
+    count = 8
     return pl.pallas_call(
         relay_kernel,
-        grid=(depth // rows,),
-        out_shape=(pltpu.VMEM((parts, depth, width), BF16), hbm_of(2, depth, width)),
-        in_specs=[pl.BlockSpec((rows, parts, width), lambda b: (b, 0, 0))],
-        out_specs=(VMEM, pl.BlockSpec((2, rows, width), lambda b: (0, b, 0))),
-        compiler_params=limit(18, "arbitrary"),
+        out_shape=pltpu.VMEM((parts, depth, width), BF16),
+        in_specs=[HBM],
+        out_specs=VMEM,
+        scratch_shapes=[
+            pltpu.VMEM((count, depth // count, parts, width), BF16),
+            pltpu.SemaphoreType.DMA((count,)),
+        ],
+        compiler_params=limit(20),
+        cost_estimate=pl.CostEstimate(
+            flops=0, bytes_accessed=2 * depth * parts * width, transcendentals=0
+        ),
         name="relay",
     )(*in_hbm(in_proj))
 
@@ -388,6 +419,7 @@
         hbm_of(rows, width, dtype=F32),
         shape_of(32, 16, HEAD_WIDTH),
         shape_of(4, HEAD_WIDTH, dtype=F32),
+        hbm_of(2, depth, width),
     )
     arrays = (*chunks, gain, weights, decay)
     return pl.pallas_call(
@@ -395,12 +427,13 @@
         grid=(1,),
         out_shape=outs,
         in_specs=[SMEM, SMEM] + [VMEM] * len(arrays),
-        out_specs=tuple(fixed(*o.shape) for o in outs),
+        out_specs=tuple(fixed(*o.shape) for o in outs[:-1]) + (HBM,),
         scratch_shapes=[
             pltpu.VMEM((rows, depth), BF16),
             pltpu.VMEM((3, rows, width), BF16),
             pltpu.VMEM((rows, 4), F32),
             pltpu.VMEM((4, rows), F32),
+            pltpu.SemaphoreType.DMA((2,)),
         ],
         compiler_params=limit(24, "arbitrary"),
         cost_estimate=cost_of(rows, depth, 4 * width),
@@ -603,7 +636,7 @@
     to_next, to_last, near_next, near_last, own = adapter_sums(
         place, image_patches.transpose(0, 2, 1), adapter
     )
-    weights, late_weights = relay_call(in_proj)
+    weights = relay_call(in_proj)
     from_left = moved(to_next, 1)
     from_right = moved(to_last, 3)
     next_sum, last_sum = pass_call(from_left, from_right, near_next, near_last)
@@ -612,7 +645,7 @@
     embed = embed_call(own, from_left, from_right, left, right)
     image_chunks = gathered(embed)
 
-    *text_parts, text_state, text_span = text_call(
+    *text_parts, text_state, text_span, late_weights = text_call(
         place, ceiling, text_chunks, gain, weights, decay
     )
     *held, states = image_state_call(

time: 114 us -> 108 us (0.947)
  Pallas kernels: 33.3 us -> 27.9 us
    pallas_call x2, Pallas kernels: 12.2 us -> 6.53 us  [the longest x1 3.71 us: relay_call(): pl.pallas_call(relay_kernel, out_shape=pltpu.VMEM((parts, depth, width),...]
  transfers between devices with their start and end apart: 19 -> 19, of which waited for: 8 -> 8; matrix products, arithmetic and copies ran while one was open for 1% -> 1% of each run, Pallas kernels for 19% -> 15%
where the time goes in v3:
time: 108 us; the launch traced here: 107 us
  Pallas kernels  27.9 us (26%)
  starting transfers between devices  27.5 us (25%)
  waiting for transfers between devices  25 us (23%)
  blocking collectives  23.9 us (22%)
  other arithmetic  1.91 us (2%)
    all_to_all x1, blocking collectives, steps(): slices = lax.all_to_all(states, SEQ, 0, 0, tiled=True)  23.9 us
    ppermute x18, starting transfers between devices, moved(): return lax.ppermute(array, 'head', [(i, (i + step) % 4) for i in range(4)])  23.8 us
    ppermute x18, waiting for transfers between devices, moved(): return lax.ppermute(array, 'head', [(i, (i + step) % 4) for i in range(4)])  21.2 us
    pallas_call x1, Pallas kernels, text_call(): pl.pallas_call(text_kernel, grid=(1,), out_shape=outs, in_specs=[SMEM, SM...  5.86 us
    pallas_call x1, Pallas kernels, image_attend_call(): pl.pallas_call(image_attend_kernel, grid=(2,), out_shape=outs, in_specs=[...  5.2 us
    pallas_call x1, Pallas kernels, image_state_call(): pl.pallas_call(image_state_kernel, out_shape=outs, in_specs=[SMEM] * 3 +...  4.15 us
    all_to_all x1, waiting for transfers between devices, steps(): lax.all_to_all(scan_call(image_start, slices), SEQ, 0, 0, tiled=True)  3.85 us
    pallas_call x1, Pallas kernels, relay_call(): pl.pallas_call(relay_kernel, out_shape=pltpu.VMEM((parts, depth, width),...  3.71 us
  transfers between devices with their start and end apart: 19, of which 8 were waited for; matrix products, arithmetic and copies ran while one was open for 1% of the time, Pallas kernels for 15%

profile of v3, /device:TPU:1, one launch (start us, length us, event | category | flops | bytes accessed | tf_op | source)
XLA Modules:
  0.0 107.2 jit_solution(6671075540094943487)
XLA Ops:
  0.6 0.1 pad_add_fusion.place_ref
  0.7 2.8 %adapter_sums.1 = (bf16[256,512]{1,0:T(8,128)(2,1)S(1)}, bf16[256,512]{1,0:T(8,128)(2,1)S(1)}, bf16[128,512]{1,0:T(8,128)(2,1)S(1)}, bf16[128,512]{1,0:T(8,128)(2,1)S(1)}, f32[256,512]{1,0:T(8,128)S(1)}) custom-call(s32[2]{0:T(128)S(1)} %pad_add_fusion.place_ref, bf16[1,288,256]{2,1,0:T(8,128)(2,1)} %bitcast.11, bf16[288,2048]{1,0:T(8,128)(2,1)} %adapter_ref.1), custom_call_target="tpu_custom_call" | custom-call | tf_op jit(solution)/shard_map/adapter_sums/pallas_call | solution.py:100
  3.5 2.1 %collective-permute-start = (bf16[256,512]{1,0:T(8,128)(2,1)S(1)}, bf16[256,512]{1,0:T(8,128)(2,1)S(1)}, u32[]{:S(2)}, u32[]{:S(2)}) collective-permute-start(bf16[256,512]{1,0:T(8,128)(2,1)S(1)} %get-tuple-element.33), channel_id=1, source_target_pairs={{0,1},{1,2},{2,3},{3,0},{4,5},{5,6},{6,7},{7,4},{8,9},{9,10},{10,1... | collective-permute-start | bytes 786440 | tf_op jit(solution)/shard_map/ppermute | solution.py:601
  5.6 1.4 %collective-permute-start.1 = (bf16[256,512]{1,0:T(8,128)(2,1)S(1)}, bf16[256,512]{1,0:T(8,128)(2,1)S(1)}, u32[]{:S(2)}, u32[]{:S(2)}) collective-permute-start(bf16[256,512]{1,0:T(8,128)(2,1)S(1)} %get-tuple-element.34), channel_id=1, source_target_pairs={{0,3},{1,0},{2,1},{3,2},{4,7},{5,4},{6,5},{7,6},{8,11},{9,8},{10,9... | collective-permute-start | bytes 786440 | tf_op jit(solution)/shard_map/ppermute | solution.py:601
  7.0 5.6 %collective-permute-done.from_left = bf16[256,512]{1,0:T(8,128)(2,1)S(1)} collective-permute-done((bf16[256,512]{1,0:T(8,128)(2,1)S(1)}, bf16[256,512]{1,0:T(8,128)(2,1)S(1)}, u32[]{:S(2)}, u32[]{:S(2)}) %collective-permute-start) | collective-permute-done | bytes 262176 | tf_op jit(solution)/shard_map/ppermute | solution.py:601
  12.6 0.1 pass_on.1
  12.6 1.3 %collective-permute-start.2 = (bf16[128,512]{1,0:T(8,128)(2,1)S(1)}, bf16[128,512]{1,0:T(8,128)(2,1)S(1)}, u32[]{:S(2)}, u32[]{:S(2)}) collective-permute-start(bf16[128,512]{1,0:T(8,128)(2,1)S(1)} %get-tuple-element.37), channel_id=1, source_target_pairs={{0,1},{1,2},{2,3},{3,0},{4,5},{5,6},{6,7},{7,4},{8,9},{9,10},{10,1... | collective-permute-start | bytes 393224 | tf_op jit(solution)/shard_map/ppermute | solution.py:601
  13.9 1.5 %collective-permute-start.3 = (bf16[128,512]{1,0:T(8,128)(2,1)S(1)}, bf16[128,512]{1,0:T(8,128)(2,1)S(1)}, u32[]{:S(2)}, u32[]{:S(2)}) collective-permute-start(bf16[128,512]{1,0:T(8,128)(2,1)S(1)} %get-tuple-element.38), channel_id=1, source_target_pairs={{0,3},{1,0},{2,1},{3,2},{4,7},{5,4},{6,5},{7,6},{8,11},{9,8},{10,9... | collective-permute-start | bytes 393224 | tf_op jit(solution)/shard_map/ppermute | solution.py:601
  15.4 1.3 %collective-permute-start.9 = (bf16[256,512]{1,0:T(8,128)(2,1)}, bf16[256,512]{1,0:T(8,128)(2,1)S(1)}, u32[]{:S(2)}, u32[]{:S(2)}) collective-permute-start(bf16[256,512]{1,0:T(8,128)(2,1)} %own.1), channel_id=1, source_target_pairs={{0,3},{1,0},{2,1},{3,2},{4,7},{5,4},{6,5},{7,6},{8,11},{9,8},{10,9... | collective-permute-start | bytes 786440 | tf_op jit(solution)/shard_map/ppermute | solution.py:601
  16.7 0.1 collective-permute-start.8
  16.8 0.9 collective-permute-done.2.left
  17.7 0.1 embed.1.own
  17.8 2.7 %collective-permute-start.5 = (bf16[256,512]{1,0:T(8,128)(2,1)S(1)}, bf16[256,512]{1,0:T(8,128)(2,1)S(1)}, u32[]{:S(2)}, u32[]{:S(2)}) collective-permute-start(bf16[256,512]{1,0:T(8,128)(2,1)S(1)} %embed.1.own), channel_id=1, source_target_pairs={{0,3},{1,0},{2,1},{3,2},{4,7},{5,4},{6,5},{7,6},{8,11},{9,8},{10,9... | collective-permute-start | bytes 786440 | tf_op jit(solution)/shard_map/ppermute | solution.py:601
  20.6 2.5 %collective-permute-done.9.right = bf16[256,512]{1,0:T(8,128)(2,1)S(1)} collective-permute-done((bf16[256,512]{1,0:T(8,128)(2,1)}, bf16[256,512]{1,0:T(8,128)(2,1)S(1)}, u32[]{:S(2)}, u32[]{:S(2)}) %collective-permute-start.9) | collective-permute-done | bytes 262176 | tf_op jit(solution)/shard_map/ppermute | solution.py:601
  23.1 2.5 %collective-permute-start.11 = (bf16[128,512]{1,0:T(8,128)(2,1)S(1)}, bf16[128,512]{1,0:T(8,128)(2,1)S(1)}, u32[]{:S(2)}, u32[]{:S(2)}) collective-permute-start(bf16[128,512]{1,0:T(8,128)(2,1)S(1)} %slice.19), channel_id=1, source_target_pairs={{0,3},{1,0},{2,1},{3,2},{4,7},{5,4},{6,5},{7,6},{8,11},{9,8},{10,9... | collective-permute-start | bytes 393224 | tf_op jit(solution)/shard_map/ppermute | solution.py:601
  25.6 0.0 copy-start.1
  25.6 0.0 copy-start.2
  25.6 0.0 copy-start.3
  25.6 0.0 copy-start.4
  25.6 0.1 collective-permute-start.10
  25.7 3.7 %relay.1.weight = bf16[4,2048,512]{2,1,0:T(8,128)(2,1)S(1)} custom-call(bf16[2048,4,512]{2,1,0:T(4,128)(2,1)} %source.1), custom_call_target="tpu_custom_call" | custom-call | bytes 8388608 | tf_op jit(solution)/shard_map/relay/pallas_call | solution.py:396
  29.4 2.7 %collective-permute-start.7 = (bf16[128,512]{1,0:T(8,128)(2,1)S(1)}, bf16[128,512]{1,0:T(8,128)(2,1)S(1)}, u32[]{:S(2)}, u32[]{:S(2)}) collective-permute-start(bf16[128,512]{1,0:T(8,128)(2,1)S(1)} %slice.17), channel_id=1, source_target_pairs={{0,3},{1,0},{2,1},{3,2},{4,7},{5,4},{6,5},{7,6},{8,11},{9,8},{10,9... | collective-permute-start | bytes 393224 | tf_op jit(solution)/shard_map/ppermute | solution.py:601
  32.2 0.3 collective-permute-start.6
  32.5 0.0 copy-start.6
  32.5 5.9 %text_unit.1 = (bf16[256,512]{1,0:T(8,128)(2,1)}, bf16[256,512]{1,0:T(8,128)(2,1)}, f32[256,512]{1,0:T(8,128)}, bf16[32,16,128]{2,1,0:T(8,128)(2,1)S(1)}, f32[4,...) custom-call(s32[2]{0:T(128)S(1)} %pad_add_fusion.place_ref, f32[4]{0:T(128)S(1)} %copy-done.4, ...), custom_call_target="tpu_custom_call" | custom-call | flops 2147483648 | bytes 8388608 | tf_op jit(solution)/shard_map/text_unit/pallas_call | solution.py:425
  38.4 4.1 %image_state.1 = (bf16[256,2048]{1,0:T(8,128)(2,1)}, bf16[2,256,512]{2,1,0:T(8,128)(2,1)}, f32[256,4]{1,0:T(8,128)S(1)}, f32[4,256]{1,0:T(4,128)S(1)}, bf16[32,40,128]{2,1,0:T(8,128)(2,1)S(1)}) custom-call(s32[2]{0:T(128)S(1)} %pad_add_fusion.place_ref, f32[4]{0:T(128)S(1)} %copy-done.4, f32[32]{0:T(128)S(1)} %copy-done.6, bf16[256,512]{1,0:T(8,128)(2,1)S(1)} %embed.1.own, ...), custom_call_target="tpu_custom_call" | custom-call | flops 1073741824 | bytes 4194304 | tf_op jit(solution)/shard_map/image_state/pallas_call | solution.py:455
  42.6 0.0 copy-start
  42.6 0.0 copy-start.5
  42.6 23.9 %all_to_all.10.states = bf16[32,40,128]{2,1,0:T(8,128)(2,1)S(1)} all-to-all(bf16[32,40,128]{2,1,0:T(8,128)(2,1)S(1)} %get-tuple-element.41), channel_id=1, replica_groups=mesh['seq_0'=4,'seq_1'=4,'seq_2'=2,'head'=4] {'seq_0','seq_1','seq_2'}, dimensions={0} | all-to-all | bytes 655360 | tf_op jit(solution)/shard_map/all_to_all | solution.py:654
  66.5 1.7 %state_scan.1 = bf16[32,32,128]{2,1,0:T(8,128)(2,1)} custom-call(s32[32]{0:T(128)S(1)} %copy-done.7, bf16[32,40,128]{2,1,0:T(8,128)(2,1)S(1)} %all_to_all.10.states), custom_call_target="tpu_custom_call" | custom-call | tf_op jit(solution)/shard_map/state_scan/pallas_call | solution.py:519
  68.2 3.7 %all-to-all-start.1 = ((bf16[32,32,128]{2,1,0:T(8,128)(2,1)}), bf16[32,32,128]{2,1,0:T(8,128)(2,1)S(1)}, u32[]{:S(2)}, u32[]{:S(2)}) async-start(bf16[32,32,128]{2,1,0:T(8,128)(2,1)} %state_scan.1), calls=%async_computation.1 | async-start | bytes 524288 | tf_op jit(solution)/shard_map/all_to_all | solution.py:658
  71.8 5.2 %image_attend.1 = (bf16[256,512]{1,0:T(8,128)(2,1)}, bf16[256,512]{1,0:T(8,128)(2,1)}, f32[256,512]{1,0:T(8,128)}) custom-call(s32[2]{0:T(128)S(1)} %pad_add_fusion.place_ref, f32[4]{0:T(128)S(1)} %copy-done.4, f32[32]{0:T(128)S(1)} %copy-done.6, bf16[256,2048]{1,0:T(8,128)(2,1)} %get-tuple-element.45.normed, ...), custom_call_target="tpu_custom_call" | custom-call | flops 1073741824 | bytes 4194304 | tf_op jit(solution)/shard_map/image_attend/pallas_call | solution.py:480
  77.0 3.8 %all-to-all-done.1.entering = bf16[32,32,128]{2,1,0:T(8,128)(2,1)S(1)} async-done(((bf16[32,32,128]{2,1,0:T(8,128)(2,1)}), bf16[32,32,128]{2,1,0:T(8,128)(2,1)S(1)}, u32[]{:S(2)}, u32[]{:S(2)}) %all-to-all-start.1) | async-done | bytes 262176 | tf_op jit(solution)/shard_map/all_to_all | solution.py:658
  80.9 2.8 %gate_far.1 = (bf16[256,512]{1,0:T(8,128)(2,1)S(1)}, bf16[256,512]{1,0:T(8,128)(2,1)S(1)}, bf16[512,512]{1,0:T(8,128)(2,1)S(1)}) custom-call(s32[2]{0:T(128)S(1)} %pad_add_fusion.place_ref, bf16[32,32,128]{2,1,0:T(8,128)(2,1)S(1)} %all-to-all-done.1.entering, f32[4,128]{1,0:T(4,128)S(1)} %copy-done.5, bf16[512,2048]{1,0:T(8,128)(2,1)S(1)} %copy-done, ...), custom_call_target="tpu_custom_call" | custom-call | tf_op jit(solution)/shard_map/gate_far/pallas_call | solution.py:565
  83.7 2.8 %collective-permute-start.13 = (bf16[256,512]{1,0:T(8,128)(2,1)S(1)}, bf16[256,512]{1,0:T(8,128)(2,1)S(1)}, u32[]{:S(2)}, u32[]{:S(2)}) collective-permute-start(bf16[256,512]{1,0:T(8,128)(2,1)S(1)} %get-tuple-element.57), channel_id=1, source_target_pairs={{0,3},{1,0},{2,1},{3,2},{4,7},{5,4},{6,5},{7,6},{8,11},{9,8},{10,9... | collective-permute-start | bytes 786440 | tf_op jit(solution)/shard_map/ppermute | solution.py:601
  86.5 1.5 %near_blocks.1 = (bf16[256,512]{1,0:T(8,128)(2,1)S(1)}, bf16[256,512]{1,0:T(8,128)(2,1)S(1)}, bf16[256,512]{1,0:T(8,128)(2,1)S(1)}, bf16[256,512]{1,0:T(8,128)(2...) custom-call(s32[2]{0:T(128)S(1)} %pad_add_fusion.place_ref, bf16[512,512]{1,0:T(8,128)(2,1)S(1)} %get-tuple-element.53.gated, ...), custom_call_target="tpu_custom_call" | custom-call | flops 805306368 | bytes 1572864 | tf_op jit(solution)/shard_map/near_blocks/pallas_call | solution.py:589
  88.0 0.1 collective-permute-start.12
  88.1 3.9 %collective-permute-done.13 = bf16[256,512]{1,0:T(8,128)(2,1)S(1)} collective-permute-done((bf16[256,512]{1,0:T(8,128)(2,1)S(1)}, bf16[256,512]{1,0:T(8,128)(2,1)S(1)}, u32[]{:S(2)}, u32[]{:S(2)}) %collective-permute-start.13) | collective-permute-done | bytes 262176 | tf_op jit(solution)/shard_map/ppermute | solution.py:601
  92.0 0.1 add_convert_fusion.3
  92.0 3.5 %collective-permute-start.14 = (bf16[256,512]{1,0:T(8,128)(2,1)S(1)}, bf16[256,512]{1,0:T(8,128)(2,1)S(1)}, u32[]{:S(2)}, u32[]{:S(2)}) collective-permute-start(bf16[256,512]{1,0:T(8,128)(2,1)S(1)} %add_convert_fusion.3), channel_id=1, source_target_pairs={{0,3},{1,0},{2,1},{3,2},{4,7},{5,4},{6,5},{7,6},{8,11},{9,8},{10,9... | collective-permute-start | bytes 786440 | tf_op jit(solution)/shard_map/ppermute | solution.py:601
  95.5 0.1 collective-permute-start.17
  95.6 0.1 add_convert_fusion.1
  95.7 1.5 %collective-permute-start.16 = (bf16[256,512]{1,0:T(8,128)(2,1)S(1)}, bf16[256,512]{1,0:T(8,128)(2,1)S(1)}, u32[]{:S(2)}, u32[]{:S(2)}) collective-permute-start(bf16[256,512]{1,0:T(8,128)(2,1)S(1)} %add_convert_fusion.1), channel_id=1, source_target_pairs={{0,1},{1,2},{2,3},{3,0},{4,5},{5,6},{6,7},{7,4},{8,9},{9,10},{10,1... | collective-permute-start | bytes 786440 | tf_op jit(solution)/shard_map/ppermute | solution.py:601
  97.1 3.6 %collective-permute-done.12 = bf16[256,512]{1,0:T(8,128)(2,1)S(1)} collective-permute-done((bf16[256,512]{1,0:T(8,128)(2,1)S(1)}, bf16[256,512]{1,0:T(8,128)(2,1)S(1)}, u32[]{:S(2)}, u32[]{:S(2)}) %collective-permute-start.12) | collective-permute-done | bytes 262176 | tf_op jit(solution)/shard_map/ppermute | solution.py:601
  100.7 0.9 fusion
  101.6 4.2 %collective-permute-done.17 = bf16[256,512]{1,0:T(8,128)(2,1)S(1)} collective-permute-done((bf16[256,512]{1,0:T(8,128)(2,1)S(1)}, bf16[256,512]{1,0:T(8,128)(2,1)S(1)}, u32[]{:S(2)}, u32[]{:S(2)}) %collective-permute-start.17) | collective-permute-done | bytes 262176 | tf_op jit(solution)/shard_map/ppermute | solution.py:601
  105.8 0.6 collective-permute-done.16
  106.3 0.9 add_convert_fusion
  (26 shorter events, 0.1 us)
Async XLA Ops:
  3.5 9.0 %collective-permute-start = (bf16[256,512]{1,0:T(8,128)(2,1)S(1)}, bf16[256,512]{1,0:T(8,128)(2,1)S(1)}, u32[]{:S(2)}, u32[]{:S(2)}) collective-permute-start(bf16[256,512]{1,0:T(8,128)(2,1)S(1)} %get-tuple-element.33), channel_id=1, source_target_pairs={{0,1},{1,2},{2,3},{3,0},{4,5},{5,6},{6,7},{7,4},{8,9},{9,10},{10,1... | collective-permute-start | bytes 786440 | tf_op jit(solution)/shard_map/ppermute | solution.py:601
  5.6 6.9 %collective-permute-start.1 = (bf16[256,512]{1,0:T(8,128)(2,1)S(1)}, bf16[256,512]{1,0:T(8,128)(2,1)S(1)}, u32[]{:S(2)}, u32[]{:S(2)}) collective-permute-start(bf16[256,512]{1,0:T(8,128)(2,1)S(1)} %get-tuple-element.34), channel_id=1, source_target_pairs={{0,3},{1,0},{2,1},{3,2},{4,7},{5,4},{6,5},{7,6},{8,11},{9,8},{10,9... | collective-permute-start | bytes 786440 | tf_op jit(solution)/shard_map/ppermute | solution.py:601
  12.6 5.1 %collective-permute-start.2 = (bf16[128,512]{1,0:T(8,128)(2,1)S(1)}, bf16[128,512]{1,0:T(8,128)(2,1)S(1)}, u32[]{:S(2)}, u32[]{:S(2)}) collective-permute-start(bf16[128,512]{1,0:T(8,128)(2,1)S(1)} %get-tuple-element.37), channel_id=1, source_target_pairs={{0,1},{1,2},{2,3},{3,0},{4,5},{5,6},{6,7},{7,4},{8,9},{9,10},{10,1... | collective-permute-start | bytes 393224 | tf_op jit(solution)/shard_map/ppermute | solution.py:601
  13.9 3.9 %collective-permute-start.3 = (bf16[128,512]{1,0:T(8,128)(2,1)S(1)}, bf16[128,512]{1,0:T(8,128)(2,1)S(1)}, u32[]{:S(2)}, u32[]{:S(2)}) collective-permute-start(bf16[128,512]{1,0:T(8,128)(2,1)S(1)} %get-tuple-element.38), channel_id=1, source_target_pairs={{0,3},{1,0},{2,1},{3,2},{4,7},{5,4},{6,5},{7,6},{8,11},{9,8},{10,9... | collective-permute-start | bytes 393224 | tf_op jit(solution)/shard_map/ppermute | solution.py:601
  15.4 7.7 %collective-permute-start.9 = (bf16[256,512]{1,0:T(8,128)(2,1)}, bf16[256,512]{1,0:T(8,128)(2,1)S(1)}, u32[]{:S(2)}, u32[]{:S(2)}) collective-permute-start(bf16[256,512]{1,0:T(8,128)(2,1)} %own.1), channel_id=1, source_target_pairs={{0,3},{1,0},{2,1},{3,2},{4,7},{5,4},{6,5},{7,6},{8,11},{9,8},{10,9... | collective-permute-start | bytes 786440 | tf_op jit(solution)/shard_map/ppermute | solution.py:601
  16.7 8.8 %collective-permute-start.8 = (bf16[256,512]{1,0:T(8,128)(2,1)}, bf16[256,512]{1,0:T(8,128)(2,1)S(1)}, u32[]{:S(2)}, u32[]{:S(2)}) collective-permute-start(bf16[256,512]{1,0:T(8,128)(2,1)} %own.1), channel_id=1, source_target_pairs={{0,1},{1,2},{2,3},{3,0},{4,5},{5,6},{6,7},{7,4},{8,9},{9,10},{10,1... | collective-permute-start | bytes 786440 | tf_op jit(solution)/shard_map/ppermute | solution.py:601
  17.8 11.6 %collective-permute-start.5 = (bf16[256,512]{1,0:T(8,128)(2,1)S(1)}, bf16[256,512]{1,0:T(8,128)(2,1)S(1)}, u32[]{:S(2)}, u32[]{:S(2)}) collective-permute-start(bf16[256,512]{1,0:T(8,128)(2,1)S(1)} %embed.1.own), channel_id=1, source_target_pairs={{0,3},{1,0},{2,1},{3,2},{4,7},{5,4},{6,5},{7,6},{8,11},{9,8},{10,9... | collective-permute-start | bytes 786440 | tf_op jit(solution)/shard_map/ppermute | solution.py:601
  20.6 11.6 %collective-permute-start.4 = (bf16[256,512]{1,0:T(8,128)(2,1)S(1)}, bf16[256,512]{1,0:T(8,128)(2,1)S(1)}, u32[]{:S(2)}, u32[]{:S(2)}) collective-permute-start(bf16[256,512]{1,0:T(8,128)(2,1)S(1)} %embed.1.own), channel_id=1, source_target_pairs={{0,1},{1,2},{2,3},{3,0},{4,5},{5,6},{6,7},{7,4},{8,9},{9,10},{10,1... | collective-permute-start | bytes 786440 | tf_op jit(solution)/shard_map/ppermute | solution.py:601
  23.1 9.4 %collective-permute-start.11 = (bf16[128,512]{1,0:T(8,128)(2,1)S(1)}, bf16[128,512]{1,0:T(8,128)(2,1)S(1)}, u32[]{:S(2)}, u32[]{:S(2)}) collective-permute-start(bf16[128,512]{1,0:T(8,128)(2,1)S(1)} %slice.19), channel_id=1, source_target_pairs={{0,3},{1,0},{2,1},{3,2},{4,7},{5,4},{6,5},{7,6},{8,11},{9,8},{10,9... | collective-permute-start | bytes 393224 | tf_op jit(solution)/shard_map/ppermute | solution.py:601
  25.6 6.9 %copy-start.1 = (bf16[256,512]{1,0:T(8,128)(2,1)S(1)}, bf16[256,512]{1,0:T(8,128)(2,1)}, u32[]{:S(2)}) copy-start(bf16[256,512]{1,0:T(8,128)(2,1)} %own.1) | copy-start | bytes 786436
  25.6 6.9 %copy-start.2 = (bf16[2048,4]{0,1:T(4,128)(2,1)S(1)}, bf16[2048,4]{0,1:T(4,128)(2,1)}, u32[]{:S(2)}) copy-start(bf16[2048,4]{0,1:T(4,128)(2,1)} %param.18) | copy-start | bytes 49156
  25.6 6.9 %copy-start.3 = (f32[2048]{0:T(1024)S(1)}, f32[2048]{0:T(1024)}, u32[]{:S(2)}) copy-start(f32[2048]{0:T(1024)} %param.16) | copy-start | bytes 24580
  25.6 6.9 %copy-start.4 = (f32[4]{0:T(128)S(1)}, f32[4]{0:T(128)}, u32[]{:S(2)}) copy-start(f32[4]{0:T(128)} %ceiling_ref.5) | copy-start | bytes 52
  25.6 6.8 %collective-permute-start.10 = (bf16[128,512]{1,0:T(8,128)(2,1)S(1)}, bf16[128,512]{1,0:T(8,128)(2,1)S(1)}, u32[]{:S(2)}, u32[]{:S(2)}) collective-permute-start(bf16[128,512]{1,0:T(8,128)(2,1)S(1)} %slice.18), channel_id=1, source_target_pairs={{0,1},{1,2},{2,3},{3,0},{4,5},{5,6},{6,7},{7,4},{8,9},{9,10},{10,1... | collective-permute-start | bytes 393224 | tf_op jit(solution)/shard_map/ppermute | solution.py:601
  29.4 8.9 %collective-permute-start.7 = (bf16[128,512]{1,0:T(8,128)(2,1)S(1)}, bf16[128,512]{1,0:T(8,128)(2,1)S(1)}, u32[]{:S(2)}, u32[]{:S(2)}) collective-permute-start(bf16[128,512]{1,0:T(8,128)(2,1)S(1)} %slice.17), channel_id=1, source_target_pairs={{0,3},{1,0},{2,1},{3,2},{4,7},{5,4},{6,5},{7,6},{8,11},{9,8},{10,9... | collective-permute-start | bytes 393224 | tf_op jit(solution)/shard_map/ppermute | solution.py:601
  32.2 6.2 %collective-permute-start.6 = (bf16[128,512]{1,0:T(8,128)(2,1)S(1)}, bf16[128,512]{1,0:T(8,128)(2,1)S(1)}, u32[]{:S(2)}, u32[]{:S(2)}) collective-permute-start(bf16[128,512]{1,0:T(8,128)(2,1)S(1)} %slice.16), channel_id=1, source_target_pairs={{0,1},{1,2},{2,3},{3,0},{4,5},{5,6},{6,7},{7,4},{8,9},{9,10},{10,1... | collective-permute-start | bytes 393224 | tf_op jit(solution)/shard_map/ppermute | solution.py:601
  32.5 5.9 %copy-start.6 = (f32[32]{0:T(128)S(1)}, f32[32]{0:T(128)}, u32[]{:S(2)}) copy-start(f32[32]{0:T(128)} %forget_ref.3) | copy-start | bytes 388
  38.4 28.0 %copy-start.7 = (s32[32]{0:T(128)S(1)}, s32[32]{0:T(128)}, u32[]{:S(2)}) copy-start(s32[32]{0:T(128)} %start_ref.1) | copy-start | bytes 388
  42.6 38.3 %copy-start = (bf16[512,2048]{1,0:T(8,128)(2,1)S(1)}, bf16[512,2048]{1,0:T(8,128)(2,1)}, u32[]{:S(2)}) copy-start(bf16[512,2048]{1,0:T(8,128)(2,1)} %out_proj.3) | copy-start | bytes 6291460
  42.6 38.3 %copy-start.5 = (f32[4,128]{1,0:T(4,128)S(1)}, f32[4,128]{1,0:T(4,128)}, u32[]{:S(2)}) copy-start(f32[4,128]{1,0:T(4,128)} %out_gain.1) | copy-start | bytes 6148
  68.2 12.7 %all-to-all-start.1 = ((bf16[32,32,128]{2,1,0:T(8,128)(2,1)}), bf16[32,32,128]{2,1,0:T(8,128)(2,1)S(1)}, u32[]{:S(2)}, u32[]{:S(2)}) async-start(bf16[32,32,128]{2,1,0:T(8,128)(2,1)} %state_scan.1), calls=%async_computation.1 | async-start | bytes 524288 | tf_op jit(solution)/shard_map/all_to_all | solution.py:658
  83.7 8.3 %collective-permute-start.13 = (bf16[256,512]{1,0:T(8,128)(2,1)S(1)}, bf16[256,512]{1,0:T(8,128)(2,1)S(1)}, u32[]{:S(2)}, u32[]{:S(2)}) collective-permute-start(bf16[256,512]{1,0:T(8,128)(2,1)S(1)} %get-tuple-element.57), channel_id=1, source_target_pairs={{0,3},{1,0},{2,1},{3,2},{4,7},{5,4},{6,5},{7,6},{8,11},{9,8},{10,9... | collective-permute-start | bytes 786440 | tf_op jit(solution)/shard_map/ppermute | solution.py:601
  86.5 9.1 %collective-permute-start.15 = (bf16[256,512]{1,0:T(8,128)(2,1)S(1)}, bf16[256,512]{1,0:T(8,128)(2,1)S(1)}, u32[]{:S(2)}, u32[]{:S(2)}) collective-permute-start(bf16[256,512]{1,0:T(8,128)(2,1)S(1)} %get-tuple-element.60), channel_id=1, source_target_pairs={{0,1},{1,2},{2,3},{3,0},{4,5},{5,6},{6,7},{7,4},{8,9},{9,10},{10,1... | collective-permute-start | bytes 786440 | tf_op jit(solution)/shard_map/ppermute | solution.py:601
  88.0 12.7 %collective-permute-start.12 = (bf16[256,512]{1,0:T(8,128)(2,1)S(1)}, bf16[256,512]{1,0:T(8,128)(2,1)S(1)}, u32[]{:S(2)}, u32[]{:S(2)}) collective-permute-start(bf16[256,512]{1,0:T(8,128)(2,1)S(1)} %get-tuple-element.55), channel_id=1, source_target_pairs={{0,1},{1,2},{2,3},{3,0},{4,5},{5,6},{6,7},{7,4},{8,9},{9,10},{10,1... | collective-permute-start | bytes 786440 | tf_op jit(solution)/shard_map/ppermute | solution.py:601
  92.0 8.7 %collective-permute-start.14 = (bf16[256,512]{1,0:T(8,128)(2,1)S(1)}, bf16[256,512]{1,0:T(8,128)(2,1)S(1)}, u32[]{:S(2)}, u32[]{:S(2)}) collective-permute-start(bf16[256,512]{1,0:T(8,128)(2,1)S(1)} %add_convert_fusion.3), channel_id=1, source_target_pairs={{0,3},{1,0},{2,1},{3,2},{4,7},{5,4},{6,5},{7,6},{8,11},{9,8},{10,9... | collective-permute-start | bytes 786440 | tf_op jit(solution)/shard_map/ppermute | solution.py:601
  95.5 10.2 %collective-permute-start.17 = (bf16[256,512]{1,0:T(8,128)(2,1)S(1)}, bf16[256,512]{1,0:T(8,128)(2,1)S(1)}, u32[]{:S(2)}, u32[]{:S(2)}) collective-permute-start(bf16[256,512]{1,0:T(8,128)(2,1)S(1)} %get-tuple-element.61), channel_id=1, source_target_pairs={{0,3},{1,0},{2,1},{3,2},{4,7},{5,4},{6,5},{7,6},{8,11},{9,8},{10,9... | collective-permute-start | bytes 786440 | tf_op jit(solution)/shard_map/ppermute | solution.py:601
  95.7 10.7 %collective-permute-start.16 = (bf16[256,512]{1,0:T(8,128)(2,1)S(1)}, bf16[256,512]{1,0:T(8,128)(2,1)S(1)}, u32[]{:S(2)}, u32[]{:S(2)}) collective-permute-start(bf16[256,512]{1,0:T(8,128)(2,1)S(1)} %add_convert_fusion.1), channel_id=1, source_target_pairs={{0,1},{1,2},{2,3},{3,0},{4,5},{5,6},{6,7},{7,4},{8,9},{9,10},{10,1... | collective-permute-start | bytes 786440 | tf_op jit(solution)/shard_map/ppermute | solution.py:601

commit v4 on v3

--- a/solution.py
+++ b/solution.py
@@ -44,72 +44,73 @@
     return pl.ds(pl.multiple_of(lax.rem(place + step, count) * width, width), width)
 
 
-def adapter_kernel(
-    place_ref,
-    patches_ref,
-    adapter_ref,
-    to_next,
-    to_last,
-    near_next,
-    near_last,
-    own,
-    patches,
-    blocks,
-    sems,
-):
-    half = near_next.shape[0]
-    width = own.shape[1]
+def adapter_blocks(place_ref, patches_ref, adapter_ref, patches, blocks, sems, steps):
     patches_copy = pltpu.make_async_copy(patches_ref.at[0], patches, sems.at[0])
     patches_copy.start()
     copies = []
-    for at, step in enumerate((2, 1, 3, 0)):
-        columns = columns_of(place_ref[0], step, 4, width)
+    for at, step in enumerate(steps):
+        columns = columns_of(place_ref[0], step, 4, blocks.shape[2])
         copies.append(
             pltpu.make_async_copy(adapter_ref.at[:, columns], blocks.at[at], sems.at[at + 1])
         )
         copies[at].start()
     patches_copy.wait()
     rows = patches[...].T
-    for at in range(4):
+    for at in range(len(steps)):
         copies[at].wait()
-        block = jnp.dot(rows, blocks[at], preferred_element_type=F32)
+        yield jnp.dot(rows, blocks[at], preferred_element_type=F32)
+
+
+def adapter_kernel(place_ref, patches_ref, adapter_ref, *refs):
+    to_next, to_last, near_next, near_last, patches, blocks, sems = refs
+    half = near_next.shape[0]
+    steps = (2, 1, 3)
+    made = adapter_blocks(place_ref, patches_ref, adapter_ref, patches, blocks, sems, steps)
+    for step, block in zip(steps, made):
         small = block.astype(BF16)
-        if at == 0:
+        if step == 2:
             to_next[:half] = small[:half]
             to_last[half:] = small[half:]
-        elif at == 1:
+        elif step == 1:
             near_next[...] = small[:half]
             to_next[half:] = small[half:]
-        elif at == 2:
+        else:
             to_last[:half] = small[:half]
             near_last[...] = small[half:]
-        else:
-            own[...] = block
-
-
-def adapter_sums(place, patches, adapter):
+
+
+def own_kernel(place_ref, patches_ref, adapter_ref, own, patches, blocks, sems):
+    for block in adapter_blocks(place_ref, patches_ref, adapter_ref, patches, blocks, sems, (0,)):
+        own[...] = block
+
+
+def adapter_call(kernel, outs, count, place, patches, adapter):
     depth, rows = patches.shape[1:]
-    width = adapter.shape[1] // 4
-    outs = (
-        shape_of(rows, width),
-        shape_of(rows, width),
-        shape_of(rows // 2, width),
-        shape_of(rows // 2, width),
-        shape_of(rows, width, dtype=F32),
-    )
-    return pl.pallas_call(
-        adapter_kernel,
+    return pl.pallas_call(
+        kernel,
         out_shape=outs,
         in_specs=[SMEM, HBM, HBM],
-        out_specs=(VMEM,) * 5,
+        out_specs=jax.tree.map(lambda _: VMEM, outs),
         scratch_shapes=[
             pltpu.VMEM((depth, rows), BF16),
-            pltpu.VMEM((4, depth, width), BF16),
-            pltpu.SemaphoreType.DMA((5,)),
+            pltpu.VMEM((count, depth, adapter.shape[1] // 4), BF16),
+            pltpu.SemaphoreType.DMA((count + 1,)),
         ],
         compiler_params=limit(8),
-        name="adapter_sums",
+        cost_estimate=cost_of(rows, depth, count * adapter.shape[1] // 4),
     )(place, *in_hbm(patches, adapter))
+
+
+def adapter_sums(*arrays):
+    rows, width = arrays[1].shape[2], arrays[2].shape[1] // 4
+    outs = (shape_of(rows, width),) * 2 + (shape_of(rows // 2, width),) * 2
+    return adapter_call(adapter_kernel, outs, 3, *arrays)
+
+
+def adapter_own(*arrays):
+    rows, width = arrays[1].shape[2], arrays[2].shape[1] // 4
+    outs = shape_of(rows, width, dtype=F32)
+    return adapter_call(own_kernel, outs, 1, *arrays)
 
 
 def pass_kernel(from_left, from_right, near_next, near_last, next_out, last_out):
@@ -170,14 +171,15 @@
     return jnp.dot(normed[...], weight, preferred_element_type=F32)
 
 
-def decay_sums(normed, decay_ref, columns, lanes):
-    rows = normed.shape[0]
-    decay = decay_ref[...].astype(F32)
-    decay = jnp.concatenate([decay] * 4, axis=0).astype(BF16)
+def decay_logits(values, decay):
+    decay = jnp.concatenate([decay.astype(F32)] * 4, axis=0).astype(BF16)
     decay = jnp.concatenate([decay, jnp.zeros((HEAD_WIDTH - 16, decay.shape[1]), BF16)], axis=0)
-    gates = jax.nn.sigmoid(
-        lax.dot_general(normed[...], decay, (((1,), (1,)), ((), ())), preferred_element_type=F32)
-    )
+    return lax.dot_general(values, decay, (((1,), (1,)), ((), ())), preferred_element_type=F32)
+
+
+def decay_sums(logits, columns, lanes):
+    rows = logits.shape[0]
+    gates = jax.nn.sigmoid(logits)
     ids = lax.broadcasted_iota(jnp.int32, gates.shape, 1)
     upper = gates.astype(BF16).astype(F32)
     middle = (gates - upper).astype(BF16).astype(F32)
@@ -254,7 +256,7 @@
     for copy in copies:
         copy.start()
     normalize(place_ref[0], (own, left, right, far_a, far_b), gain_ref, normed)
-    decay_sums(normed, decay_ref, columns, lanes)
+    decay_sums(decay_logits(normed[...], decay_ref[...]), columns, lanes)
     for part in range(3):
         parts[part] = product(normed, weight[part]).astype(BF16)
     gate_out[...] = silu_of(product(normed, weight[3]))
@@ -279,35 +281,75 @@
         copy.wait()
 
 
+def image_near_kernel(
+    place_ref, own, left, right, gain_ref, weight, decay_ref, scaled_out, total, logits, squares, scaled, sems
+):
+    copies = []
+    for at, (step, ref) in enumerate(((0, own), (3, left), (1, right))):
+        columns = columns_of(place_ref[0], step, 4, own.shape[1])
+        value = ref[...].astype(F32)
+        square = jnp.sum(value * value, axis=-1, keepdims=True)
+        small = (value * gain_ref[:, columns]).astype(BF16)
+        scaled[at] = small
+        gates = decay_logits(small, decay_ref[:, columns])
+        terms = [
+            jnp.dot(small, weight[part, columns, :], preferred_element_type=F32)
+            for part in (1, 2)
+        ]
+        copies.append(pltpu.make_async_copy(scaled.at[at], scaled_out.at[at], sems.at[at]))
+        copies[at].start()
+        if at == 0:
+            squares[...], logits[...], total[0], total[1] = square, gates, *terms
+        else:
+            squares[...] += square
+            logits[...] += gates
+            total[0] += terms[0]
+            total[1] += terms[1]
+    for copy in copies:
+        copy.wait()
+
+
 def image_state_kernel(
     place_ref,
     ceiling_ref,
     forget_ref,
-    own,
-    left,
-    right,
     far_a,
     far_b,
+    total,
+    logits,
+    squares,
     gain_ref,
     weight,
     decay_ref,
     other_state,
     other_span,
-    normed_out,
+    far_out,
     key_value_out,
+    scale_out,
     columns,
     lanes,
     state_out,
-    normed,
+    scaled,
     key_value,
     sems,
 ):
-    normalize(place_ref[0], (own, left, right, far_a, far_b), gain_ref, normed)
-    key_value[0] = product(normed, weight[1]).astype(BF16)
-    normed_copy = pltpu.make_async_copy(normed, normed_out, sems.at[0])
-    normed_copy.start()
-    key_value[1] = product(normed, weight[2]).astype(BF16)
-    decay_sums(normed, decay_ref, columns, lanes)
+    half, width = far_a.shape
+    chunk = columns_of(place_ref[0], 2, 4, width)
+    square = []
+    for at, ref in ((0, far_a), (half, far_b)):
+        value = ref[...].astype(F32)
+        square.append(jnp.sum(value * value, axis=-1, keepdims=True))
+        scaled[at : at + half] = (value * gain_ref[:, chunk]).astype(BF16)
+    square = squares[...] + jnp.concatenate(square, axis=0)
+    scale = lax.rsqrt(square / (4 * width) + EPSILON)
+    scale_out[...] = scale
+    small = scaled[...]
+    for at in range(2):
+        term = jnp.dot(small, weight[at + 1, chunk, :], preferred_element_type=F32)
+        key_value[at] = ((total[at] + term) * scale).astype(BF16)
+    far_copy = pltpu.make_async_copy(scaled, far_out, sems.at[0])
+    far_copy.start()
+    decay_sums((logits[...] + decay_logits(small, decay_ref[:, chunk])) * scale, columns, lanes)
     key_value_copy = pltpu.make_async_copy(key_value, key_value_out, sems.at[1])
     key_value_copy.start()
     state_out[:, 0:16, :] = other_state[...]
@@ -327,7 +369,7 @@
         state_out[targets, 32:40, :] = jnp.broadcast_to(
             tile.astype(BF16)[None], (8, 8, HEAD_WIDTH)
         )
-    normed_copy.wait()
+    far_copy.wait()
     key_value_copy.wait()
 
 
@@ -335,40 +377,60 @@
     place_ref,
     ceiling_ref,
     forget_ref,
-    normed,
-    key_value,
+    near_ref,
+    far_ref,
+    key_value_ref,
+    weight_ref,
+    scale_ref,
     columns,
     lanes,
-    weight,
     query_out,
     gate_out,
     inner_out,
+    scaled,
+    key_value,
+    weight,
     query,
+    sems,
 ):
-    part = pl.program_id(0)
-    block = product(normed, weight[0])
-
-    @pl.when(part == 0)
-    def _():
-        query[...] = block.astype(BF16)
-
-    @pl.when(part == 1)
-    def _():
-        gate_out[...] = silu_of(block)
-        burst = jnp.log1p(jnp.full((1, 1), -forget_ref[place_ref[1]], F32))
-        for head in range(4):
-            attend(
-                head,
-                query,
-                key_value.at[0],
-                key_value.at[1],
-                columns,
-                lanes,
-                ceiling_ref[head],
-                burst,
-                query_out,
-                inner_out,
-            )
+    width = far_ref.shape[1]
+    pieces = [
+        (near_ref.at[at], scaled.at[:, columns_of(place_ref[0], step, 4, width)])
+        for at, step in enumerate((0, 3, 1))
+    ]
+    pieces.append((far_ref, scaled.at[:, columns_of(place_ref[0], 2, 4, width)]))
+    pieces += [
+        (weight_ref.at[0], weight.at[0]),
+        (weight_ref.at[1], weight.at[1]),
+        (key_value_ref, key_value),
+    ]
+    copies = [
+        pltpu.make_async_copy(source, target, sems.at[at])
+        for at, (source, target) in enumerate(pieces)
+    ]
+    for copy in copies:
+        copy.start()
+    for copy in copies[:5]:
+        copy.wait()
+    scale = scale_ref[...]
+    query[...] = (product(scaled, weight[0]) * scale).astype(BF16)
+    copies[5].wait()
+    gate_out[...] = silu_of(product(scaled, weight[1]) * scale)
+    copies[6].wait()
+    burst = jnp.log1p(jnp.full((1, 1), -forget_ref[place_ref[1]], F32))
+    for head in range(4):
+        attend(
+            head,
+            query,
+            key_value.at[0],
+            key_value.at[1],
+            columns,
+            lanes,
+            ceiling_ref[head],
+            burst,
+            query_out,
+            inner_out,
+        )
 
 
 def cost_of(rows, depth, width):
@@ -441,55 +503,78 @@
     )(place, ceiling, *arrays)
 
 
-def image_state_call(place, ceiling, forget, chunks, gain, weights, decay, state, span):
-    rows, width = chunks[0].shape
-    depth = gain.shape[1]
+def image_near_call(place, near, gain, weights, decay):
+    rows, width = near[0].shape
     outs = (
-        hbm_of(rows, depth),
+        hbm_of(3, rows, width),
+        shape_of(2, rows, width, dtype=F32),
+        shape_of(rows, HEAD_WIDTH, dtype=F32),
+        shape_of(rows, 1, dtype=F32),
+    )
+    return pl.pallas_call(
+        image_near_kernel,
+        out_shape=outs,
+        in_specs=[SMEM] + [VMEM] * 6,
+        out_specs=(HBM,) + (VMEM,) * 3,
+        scratch_shapes=[pltpu.VMEM((3, rows, width), BF16), pltpu.SemaphoreType.DMA((3,))],
+        compiler_params=limit(16),
+        cost_estimate=cost_of(rows, 3 * width, 2 * width),
+        name="image_near",
+    )(place, *near, gain, weights, decay)
+
+
+def image_state_call(place, ceiling, forget, *arrays):
+    half, width = arrays[0].shape
+    rows = 2 * half
+    outs = (
+        hbm_of(rows, width),
         hbm_of(2, rows, width),
+        shape_of(rows, 1, dtype=F32),
         shape_of(rows, 4, dtype=F32),
         shape_of(4, rows, dtype=F32),
         shape_of(32, 40, HEAD_WIDTH),
     )
-    arrays = (*chunks, gain, weights, decay, state, span)
     return pl.pallas_call(
         image_state_kernel,
         out_shape=outs,
         in_specs=[SMEM] * 3 + [VMEM] * len(arrays),
-        out_specs=(HBM, HBM, VMEM, VMEM, VMEM),
+        out_specs=(HBM, HBM) + (VMEM,) * 4,
         scratch_shapes=[
-            pltpu.VMEM((rows, depth), BF16),
+            pltpu.VMEM((rows, width), BF16),
             pltpu.VMEM((2, rows, width), BF16),
             pltpu.SemaphoreType.DMA((2,)),
         ],
-        compiler_params=limit(24),
-        cost_estimate=cost_of(rows, depth, 2 * width),
+        compiler_params=limit(16),
+        cost_estimate=cost_of(rows, width, 2 * width),
         name="image_state",
     )(place, ceiling, forget, *arrays)
 
 
-def image_attend_call(place, ceiling, forget, weights, normed, key_value, columns, lanes):
-    rows, depth = normed.shape
-    width = key_value.shape[2]
+def image_attend_call(place, ceiling, forget, weights, near, far, key_value, *small):
+    rows, width = far.shape
+    depth = 4 * width
     outs = (
         hbm_of(rows, width),
         hbm_of(rows, width),
         hbm_of(rows, width, dtype=F32),
     )
-    held = (*in_hbm(normed, key_value), columns, lanes)
     return pl.pallas_call(
         image_attend_kernel,
-        grid=(2,),
+        grid=(1,),
         out_shape=outs,
-        in_specs=[SMEM] * 3
-        + [fixed(*h.shape) for h in held]
-        + [pl.BlockSpec((1, depth, width), lambda p: (p, 0, 0))],
+        in_specs=[SMEM] * 3 + [HBM] * 4 + [VMEM] * 3,
         out_specs=tuple(fixed(*o.shape) for o in outs),
-        scratch_shapes=[pltpu.VMEM((rows, width), BF16)],
-        compiler_params=limit(20, "arbitrary"),
+        scratch_shapes=[
+            pltpu.VMEM((rows, depth), BF16),
+            pltpu.VMEM((2, rows, width), BF16),
+            pltpu.VMEM((2, depth, width), BF16),
+            pltpu.VMEM((rows, width), BF16),
+            pltpu.SemaphoreType.DMA((7,)),
+        ],
+        compiler_params=limit(16, "arbitrary"),
         cost_estimate=cost_of(rows, depth, 2 * width),
         name="image_attend",
-    )(place, ceiling, forget, *held, *in_hbm(weights))
+    )(place, ceiling, forget, *in_hbm(near, far, key_value, weights), *small)
 
 
 def scan_kernel(start_ref, states, out, decay, image_at):
@@ -633,9 +718,9 @@
     ceiling = head_decay_ceiling
 
     text_chunks = gathered(text_embed)
-    to_next, to_last, near_next, near_last, own = adapter_sums(
-        place, image_patches.transpose(0, 2, 1), adapter
-    )
+    patches = image_patches.transpose(0, 2, 1)
+    to_next, to_last, near_next, near_last = adapter_sums(place, patches, adapter)
+    own = adapter_own(place, patches, adapter)
     weights = relay_call(in_proj)
     from_left = moved(to_next, 1)
     from_right = moved(to_last, 3)
@@ -648,12 +733,22 @@
     *text_parts, text_state, text_span, late_weights = text_call(
         place, ceiling, text_chunks, gain, weights, decay
     )
+    near, *partial = image_near_call(place, image_chunks[:3], gain, weights, decay)
     *held, states = image_state_call(
-        place, ceiling, image_forget, image_chunks, gain, weights, decay, text_state, text_span
+        place,
+        ceiling,
+        image_forget,
+        *image_chunks[3:],
+        *partial,
+        gain,
+        weights,
+        decay,
+        text_state,
+        text_span,
     )
     slices = lax.all_to_all(states, SEQ, 0, 0, tiled=True)
     image_parts = image_attend_call(
-        place, ceiling, image_forget, late_weights, *held
+        place, ceiling, image_forget, late_weights, near, *held
     )
     entering = lax.all_to_all(scan_call(image_start, slices), SEQ, 0, 0, tiled=True)
 

time: 108 us -> 109 us (level)
  Pallas kernels: 27.9 us -> 30.8 us
  waiting for transfers between devices: 25 us -> 22.9 us
    pallas_call x2 -> x4, Pallas kernels: 8.02 us -> 12.4 us  [the longest x1 5.45 us: image_attend_call(): pl.pallas_call(image_attend_kernel, grid=(1,), out_shape=outs, in_specs=[...]
    ppermute x18, waiting for transfers between devices: 21.2 us -> 19.3 us  [moved(): return lax.ppermute(array, 'head', [(i, (i + step) % 4) for i in range(4)])]
    pallas_call x1, Pallas kernels: 4.15 us -> 2.64 us  [image_state_call(): pl.pallas_call(image_state_kernel, out_shape=outs, in_specs=[SMEM] * 3 +...]
  transfers between devices with their start and end apart: 19 -> 19, of which waited for: 8 -> 7; matrix products, arithmetic and copies ran while one was open for 1% -> 1% of each run, Pallas kernels for 15% -> 20%
where the time goes in v4:
time: 109 us; the launch traced here: 108 us
  Pallas kernels  30.8 us (28%)
  starting transfers between devices  27.6 us (25%)
  blocking collectives  23.7 us (22%)
  waiting for transfers between devices  22.9 us (21%)
  other arithmetic  1.91 us (2%)
    ppermute x18, starting transfers between devices, moved(): return lax.ppermute(array, 'head', [(i, (i + step) % 4) for i in range(4)])  23.9 us
    all_to_all x1, blocking collectives, steps(): slices = lax.all_to_all(states, SEQ, 0, 0, tiled=True)  23.7 us
    ppermute x18, waiting for transfers between devices, moved(): return lax.ppermute(array, 'head', [(i, (i + step) % 4) for i in range(4)])  19.3 us
    pallas_call x1, Pallas kernels, text_call(): pl.pallas_call(text_kernel, grid=(1,), out_shape=outs, in_specs=[SMEM, SM...  5.88 us
    pallas_call x1, Pallas kernels, image_attend_call(): pl.pallas_call(image_attend_kernel, grid=(1,), out_shape=outs, in_specs=[...  5.45 us
    pallas_call x2, Pallas kernels, adapter_call(): pl.pallas_call(kernel, out_shape=outs, in_specs=[SMEM, HBM, HBM], out_spe...  4.4 us
    pallas_call x1, Pallas kernels, relay_call(): pl.pallas_call(relay_kernel, out_shape=pltpu.VMEM((parts, depth, width),...  3.71 us
    all_to_all x1, starting transfers between devices, steps(): lax.all_to_all(scan_call(image_start, slices), SEQ, 0, 0, tiled=True)  3.65 us
  transfers between devices with their start and end apart: 19, of which 7 were waited for; matrix products, arithmetic and copies ran while one was open for 1% of the time, Pallas kernels for 20%

profile of v4, /device:TPU:1, one launch (start us, length us, event | category | flops | bytes accessed | tf_op | source)
XLA Modules:
  0.0 107.9 jit_solution(4748307739610648249)
XLA Ops:
  0.6 0.1 pad_add_fusion.place_ref
  0.7 2.5 %shard_map.123 = (bf16[256,512]{1,0:T(8,128)(2,1)S(1)}, bf16[256,512]{1,0:T(8,128)(2,1)S(1)}, bf16[128,512]{1,0:T(8,128)(2,1)S(1)}, bf16[128,512]{1,0:T(8,128)(2,1)S(1)}) custom-call(s32[2]{0:T(128)S(1)} %pad_add_fusion.place_ref, bf16[1,288,256]{2,1,0:T(8,128)(2,1)} %bitcast.13, bf16[288,2048]{1,0:T(8,128)(2,1)} %adapter_ref.3), custom_call_target="tpu_custom_call" | custom-call | flops 226492416 | bytes 884736 | tf_op jit(solution)/shard_map/pallas_call | solution.py:89
  3.2 2.1 %collective-permute-start = (bf16[256,512]{1,0:T(8,128)(2,1)S(1)}, bf16[256,512]{1,0:T(8,128)(2,1)S(1)}, u32[]{:S(2)}, u32[]{:S(2)}) collective-permute-start(bf16[256,512]{1,0:T(8,128)(2,1)S(1)} %get-tuple-element.36), channel_id=1, source_target_pairs={{0,1},{1,2},{2,3},{3,0},{4,5},{5,6},{6,7},{7,4},{8,9},{9,10},{10,1... | collective-permute-start | bytes 786440 | tf_op jit(solution)/shard_map/ppermute | solution.py:686
  5.3 1.4 %collective-permute-start.1 = (bf16[256,512]{1,0:T(8,128)(2,1)S(1)}, bf16[256,512]{1,0:T(8,128)(2,1)S(1)}, u32[]{:S(2)}, u32[]{:S(2)}) collective-permute-start(bf16[256,512]{1,0:T(8,128)(2,1)S(1)} %get-tuple-element.37), channel_id=1, source_target_pairs={{0,3},{1,0},{2,1},{3,2},{4,7},{5,4},{6,5},{7,6},{8,11},{9,8},{10,9... | collective-permute-start | bytes 786440 | tf_op jit(solution)/shard_map/ppermute | solution.py:686
  6.7 5.6 %collective-permute-done.from_left = bf16[256,512]{1,0:T(8,128)(2,1)S(1)} collective-permute-done((bf16[256,512]{1,0:T(8,128)(2,1)S(1)}, bf16[256,512]{1,0:T(8,128)(2,1)S(1)}, u32[]{:S(2)}, u32[]{:S(2)}) %collective-permute-start) | collective-permute-done | bytes 262176 | tf_op jit(solution)/shard_map/ppermute | solution.py:686
  12.3 0.1 pass_on.1
  12.3 1.3 %collective-permute-start.2 = (bf16[128,512]{1,0:T(8,128)(2,1)S(1)}, bf16[128,512]{1,0:T(8,128)(2,1)S(1)}, u32[]{:S(2)}, u32[]{:S(2)}) collective-permute-start(bf16[128,512]{1,0:T(8,128)(2,1)S(1)} %get-tuple-element.40), channel_id=1, source_target_pairs={{0,1},{1,2},{2,3},{3,0},{4,5},{5,6},{6,7},{7,4},{8,9},{9,10},{10,1... | collective-permute-start | bytes 393224 | tf_op jit(solution)/shard_map/ppermute | solution.py:686
  13.6 1.5 %collective-permute-start.3 = (bf16[128,512]{1,0:T(8,128)(2,1)S(1)}, bf16[128,512]{1,0:T(8,128)(2,1)S(1)}, u32[]{:S(2)}, u32[]{:S(2)}) collective-permute-start(bf16[128,512]{1,0:T(8,128)(2,1)S(1)} %get-tuple-element.41), channel_id=1, source_target_pairs={{0,3},{1,0},{2,1},{3,2},{4,7},{5,4},{6,5},{7,6},{8,11},{9,8},{10,9... | collective-permute-start | bytes 393224 | tf_op jit(solution)/shard_map/ppermute | solution.py:686
  15.1 1.3 %collective-permute-start.9 = (bf16[256,512]{1,0:T(8,128)(2,1)}, bf16[256,512]{1,0:T(8,128)(2,1)S(1)}, u32[]{:S(2)}, u32[]{:S(2)}) collective-permute-start(bf16[256,512]{1,0:T(8,128)(2,1)} %own.1), channel_id=1, source_target_pairs={{0,3},{1,0},{2,1},{3,2},{4,7},{5,4},{6,5},{7,6},{8,11},{9,8},{10,9... | collective-permute-start | bytes 786440 | tf_op jit(solution)/shard_map/ppermute | solution.py:686
  16.4 0.1 collective-permute-start.8
  16.5 1.9 %shard_map.122.own = f32[256,512]{1,0:T(8,128)S(1)} custom-call(s32[2]{0:T(128)S(1)} %pad_add_fusion.place_ref, bf16[1,288,256]{2,1,0:T(8,128)(2,1)} %bitcast.14, bf16[288,2048]{1,0:T(8,128)(2,1)} %adapter_ref.3), custom_call_target="tpu_custom_call" | custom-call | flops 75497472 | bytes 294912 | tf_op jit(solution)/shard_map/pallas_call | solution.py:89
  18.4 0.1 embed.1.own
  18.6 2.6 %collective-permute-start.6 = (bf16[256,512]{1,0:T(8,128)(2,1)S(1)}, bf16[256,512]{1,0:T(8,128)(2,1)S(1)}, u32[]{:S(2)}, u32[]{:S(2)}) collective-permute-start(bf16[256,512]{1,0:T(8,128)(2,1)S(1)} %embed.1.own), channel_id=1, source_target_pairs={{0,3},{1,0},{2,1},{3,2},{4,7},{5,4},{6,5},{7,6},{8,11},{9,8},{10,9... | collective-permute-start | bytes 786440 | tf_op jit(solution)/shard_map/ppermute | solution.py:686
  21.2 1.6 %collective-permute-done.9.right = bf16[256,512]{1,0:T(8,128)(2,1)S(1)} collective-permute-done((bf16[256,512]{1,0:T(8,128)(2,1)}, bf16[256,512]{1,0:T(8,128)(2,1)S(1)}, u32[]{:S(2)}, u32[]{:S(2)}) %collective-permute-start.9) | collective-permute-done | bytes 262176 | tf_op jit(solution)/shard_map/ppermute | solution.py:686
  22.7 2.5 %collective-permute-start.11 = (bf16[128,512]{1,0:T(8,128)(2,1)S(1)}, bf16[128,512]{1,0:T(8,128)(2,1)S(1)}, u32[]{:S(2)}, u32[]{:S(2)}) collective-permute-start(bf16[128,512]{1,0:T(8,128)(2,1)S(1)} %slice.19), channel_id=1, source_target_pairs={{0,3},{1,0},{2,1},{3,2},{4,7},{5,4},{6,5},{7,6},{8,11},{9,8},{10,9... | collective-permute-start | bytes 393224 | tf_op jit(solution)/shard_map/ppermute | solution.py:686
  25.3 0.0 copy-start.1
  25.3 0.0 copy-start.2
  25.3 0.0 copy-start.3
  25.3 0.0 copy-start.4
  25.3 0.1 collective-permute-start.10
  25.4 3.7 %relay.1.weight = bf16[4,2048,512]{2,1,0:T(8,128)(2,1)S(1)} custom-call(bf16[2048,4,512]{2,1,0:T(4,128)(2,1)} %source.1), custom_call_target="tpu_custom_call" | custom-call | bytes 8388608 | tf_op jit(solution)/shard_map/relay/pallas_call | solution.py:458
  29.1 2.7 %collective-permute-start.7 = (bf16[128,512]{1,0:T(8,128)(2,1)S(1)}, bf16[128,512]{1,0:T(8,128)(2,1)S(1)}, u32[]{:S(2)}, u32[]{:S(2)}) collective-permute-start(bf16[128,512]{1,0:T(8,128)(2,1)S(1)} %slice.17), channel_id=1, source_target_pairs={{0,3},{1,0},{2,1},{3,2},{4,7},{5,4},{6,5},{7,6},{8,11},{9,8},{10,9... | collective-permute-start | bytes 393224 | tf_op jit(solution)/shard_map/ppermute | solution.py:686
  31.9 0.3 collective-permute-start.5
  32.2 5.9 %text_unit.1 = (bf16[256,512]{1,0:T(8,128)(2,1)}, bf16[256,512]{1,0:T(8,128)(2,1)}, f32[256,512]{1,0:T(8,128)}, bf16[32,16,128]{2,1,0:T(8,128)(2,1)S(1)}, f32[4,...) custom-call(s32[2]{0:T(128)S(1)} %pad_add_fusion.place_ref, f32[4]{0:T(128)S(1)} %copy-done.4, ...), custom_call_target="tpu_custom_call" | custom-call | flops 2147483648 | bytes 8388608 | tf_op jit(solution)/shard_map/text_unit/pallas_call | solution.py:487
  38.1 0.0 copy-start.6
  38.1 2.5 %image_near.1 = (bf16[3,256,512]{2,1,0:T(8,128)(2,1)}, f32[2,256,512]{2,1,0:T(8,128)S(1)}, f32[256,128]{1,0:T(8,128)S(1)}, f32[256,1]{1,0:T(8,128)S(1)}) custom-call(s32[2]{0:T(128)S(1)} %pad_add_fusion.place_ref, bf16[256,512]{1,0:T(8,128)(2,1)S(1)} %embed.1.own, bf16[256,512]{1,0:T(8,128)(2,1)S(1)} %collective-permute-done.4.left, ...), custom_call_target="tpu_custom_call" | custom-call | flops 805306368 | bytes 3145728 | tf_op jit(solution)/shard_map/image_near/pallas_call | solution.py:514
  40.7 0.0 copy-start.7
  40.7 2.6 %image_state.1 = (bf16[256,512]{1,0:T(8,128)(2,1)}, bf16[2,256,512]{2,1,0:T(8,128)(2,1)}, f32[256,1]{1,0:T(8,128)S(1)}, f32[256,4]{1,0:T(8,128)S(1)}, f32[4,256]...) custom-call(s32[2]{0:T(128)S(1)} %pad_add_fusion.place_ref, f32[4]{0:T(128)S(1)} %copy-done.4, f32[32]{0:T(128)S(1)} %copy-done.6, ...), custom_call_target="tpu_custom_call" | custom-call | flops 268435456 | bytes 1048576 | tf_op jit(solution)/shard_map/image_state/pallas_call | solution.py:537
  43.4 23.7 %all_to_all.10.states = bf16[32,40,128]{2,1,0:T(8,128)(2,1)S(1)} all-to-all(bf16[32,40,128]{2,1,0:T(8,128)(2,1)S(1)} %get-tuple-element.47), channel_id=1, replica_groups=mesh['seq_0'=4,'seq_1'=4,'seq_2'=2,'head'=4] {'seq_0','seq_1','seq_2'}, dimensions={0} | all-to-all | bytes 655360 | tf_op jit(solution)/shard_map/all_to_all | solution.py:749
  67.0 1.7 %state_scan.1 = bf16[32,32,128]{2,1,0:T(8,128)(2,1)} custom-call(s32[32]{0:T(128)S(1)} %copy-done.7, bf16[32,40,128]{2,1,0:T(8,128)(2,1)S(1)} %all_to_all.10.states), custom_call_target="tpu_custom_call" | custom-call | tf_op jit(solution)/shard_map/state_scan/pallas_call | solution.py:604
  68.7 3.7 %all-to-all-start.1 = ((bf16[32,32,128]{2,1,0:T(8,128)(2,1)}), bf16[32,32,128]{2,1,0:T(8,128)(2,1)S(1)}, u32[]{:S(2)}, u32[]{:S(2)}) async-start(bf16[32,32,128]{2,1,0:T(8,128)(2,1)} %state_scan.1), calls=%async_computation.1 | async-start | bytes 524288 | tf_op jit(solution)/shard_map/all_to_all | solution.py:753
  72.4 5.4 %image_attend.1 = (bf16[256,512]{1,0:T(8,128)(2,1)}, bf16[256,512]{1,0:T(8,128)(2,1)}, f32[256,512]{1,0:T(8,128)}) custom-call(s32[2]{0:T(128)S(1)} %pad_add_fusion.place_ref, f32[4]{0:T(128)S(1)} %copy-done.4, f32[32]{0:T(128)S(1)} %copy-done.6, bf16[3,256,512]{2,1,0:T(8,128)(2,1)} %get-tuple-element.51.near_ref, ...), custom_call_target="tpu_custom_call" | custom-call | flops 1073741824 | bytes 4194304 | tf_op jit(solution)/shard_map/image_attend/pallas_call | solution.py:561
  77.9 3.6 %all-to-all-done.1.entering = bf16[32,32,128]{2,1,0:T(8,128)(2,1)S(1)} async-done(((bf16[32,32,128]{2,1,0:T(8,128)(2,1)}), bf16[32,32,128]{2,1,0:T(8,128)(2,1)S(1)}, u32[]{:S(2)}, u32[]{:S(2)}) %all-to-all-start.1) | async-done | bytes 262176 | tf_op jit(solution)/shard_map/all_to_all | solution.py:753
  81.5 2.8 %gate_far.1 = (bf16[256,512]{1,0:T(8,128)(2,1)S(1)}, bf16[256,512]{1,0:T(8,128)(2,1)S(1)}, bf16[512,512]{1,0:T(8,128)(2,1)S(1)}) custom-call(s32[2]{0:T(128)S(1)} %pad_add_fusion.place_ref, bf16[32,32,128]{2,1,0:T(8,128)(2,1)S(1)} %all-to-all-done.1.entering, f32[4,128]{1,0:T(4,128)S(1)} %copy-done.5, bf16[512,2048]{1,0:T(8,128)(2,1)S(1)} %copy-done, ...), custom_call_target="tpu_custom_call" | custom-call | tf_op jit(solution)/shard_map/gate_far/pallas_call | solution.py:650
  84.2 3.0 %collective-permute-start.13 = (bf16[256,512]{1,0:T(8,128)(2,1)S(1)}, bf16[256,512]{1,0:T(8,128)(2,1)S(1)}, u32[]{:S(2)}, u32[]{:S(2)}) collective-permute-start(bf16[256,512]{1,0:T(8,128)(2,1)S(1)} %get-tuple-element.65), channel_id=1, source_target_pairs={{0,3},{1,0},{2,1},{3,2},{4,7},{5,4},{6,5},{7,6},{8,11},{9,8},{10,9... | collective-permute-start | bytes 786440 | tf_op jit(solution)/shard_map/ppermute | solution.py:686
  87.2 1.5 %near_blocks.1 = (bf16[256,512]{1,0:T(8,128)(2,1)S(1)}, bf16[256,512]{1,0:T(8,128)(2,1)S(1)}, bf16[256,512]{1,0:T(8,128)(2,1)S(1)}, bf16[256,512]{1,0:T(8,128)(2...) custom-call(s32[2]{0:T(128)S(1)} %pad_add_fusion.place_ref, bf16[512,512]{1,0:T(8,128)(2,1)S(1)} %get-tuple-element.61.gated, ...), custom_call_target="tpu_custom_call" | custom-call | flops 805306368 | bytes 1572864 | tf_op jit(solution)/shard_map/near_blocks/pallas_call | solution.py:674
  88.8 0.1 collective-permute-start.12
  88.9 3.8 %collective-permute-done.13 = bf16[256,512]{1,0:T(8,128)(2,1)S(1)} collective-permute-done((bf16[256,512]{1,0:T(8,128)(2,1)S(1)}, bf16[256,512]{1,0:T(8,128)(2,1)S(1)}, u32[]{:S(2)}, u32[]{:S(2)}) %collective-permute-start.13) | collective-permute-done | bytes 262176 | tf_op jit(solution)/shard_map/ppermute | solution.py:686
  92.7 0.1 add_convert_fusion.3
  92.8 3.5 %collective-permute-start.14 = (bf16[256,512]{1,0:T(8,128)(2,1)S(1)}, bf16[256,512]{1,0:T(8,128)(2,1)S(1)}, u32[]{:S(2)}, u32[]{:S(2)}) collective-permute-start(bf16[256,512]{1,0:T(8,128)(2,1)S(1)} %add_convert_fusion.3), channel_id=1, source_target_pairs={{0,3},{1,0},{2,1},{3,2},{4,7},{5,4},{6,5},{7,6},{8,11},{9,8},{10,9... | collective-permute-start | bytes 786440 | tf_op jit(solution)/shard_map/ppermute | solution.py:686
  96.3 0.1 collective-permute-start.17
  96.3 0.1 add_convert_fusion.1
  96.4 1.5 %collective-permute-start.16 = (bf16[256,512]{1,0:T(8,128)(2,1)S(1)}, bf16[256,512]{1,0:T(8,128)(2,1)S(1)}, u32[]{:S(2)}, u32[]{:S(2)}) collective-permute-start(bf16[256,512]{1,0:T(8,128)(2,1)S(1)} %add_convert_fusion.1), channel_id=1, source_target_pairs={{0,1},{1,2},{2,3},{3,0},{4,5},{5,6},{6,7},{7,4},{8,9},{9,10},{10,1... | collective-permute-start | bytes 786440 | tf_op jit(solution)/shard_map/ppermute | solution.py:686
  97.9 3.6 %collective-permute-done.12 = bf16[256,512]{1,0:T(8,128)(2,1)S(1)} collective-permute-done((bf16[256,512]{1,0:T(8,128)(2,1)S(1)}, bf16[256,512]{1,0:T(8,128)(2,1)S(1)}, u32[]{:S(2)}, u32[]{:S(2)}) %collective-permute-start.12) | collective-permute-done | bytes 262176 | tf_op jit(solution)/shard_map/ppermute | solution.py:686
  101.5 0.9 fusion
  102.3 4.2 %collective-permute-done.17 = bf16[256,512]{1,0:T(8,128)(2,1)S(1)} collective-permute-done((bf16[256,512]{1,0:T(8,128)(2,1)S(1)}, bf16[256,512]{1,0:T(8,128)(2,1)S(1)}, u32[]{:S(2)}, u32[]{:S(2)}) %collective-permute-start.17) | collective-permute-done | bytes 262176 | tf_op jit(solution)/shard_map/ppermute | solution.py:686
  106.5 0.6 collective-permute-done.16
  107.1 0.9 add_convert_fusion
  (28 shorter events, 0.1 us)
Async XLA Ops:
  3.2 9.0 %collective-permute-start = (bf16[256,512]{1,0:T(8,128)(2,1)S(1)}, bf16[256,512]{1,0:T(8,128)(2,1)S(1)}, u32[]{:S(2)}, u32[]{:S(2)}) collective-permute-start(bf16[256,512]{1,0:T(8,128)(2,1)S(1)} %get-tuple-element.36), channel_id=1, source_target_pairs={{0,1},{1,2},{2,3},{3,0},{4,5},{5,6},{6,7},{7,4},{8,9},{9,10},{10,1... | collective-permute-start | bytes 786440 | tf_op jit(solution)/shard_map/ppermute | solution.py:686
  5.3 6.9 %collective-permute-start.1 = (bf16[256,512]{1,0:T(8,128)(2,1)S(1)}, bf16[256,512]{1,0:T(8,128)(2,1)S(1)}, u32[]{:S(2)}, u32[]{:S(2)}) collective-permute-start(bf16[256,512]{1,0:T(8,128)(2,1)S(1)} %get-tuple-element.37), channel_id=1, source_target_pairs={{0,3},{1,0},{2,1},{3,2},{4,7},{5,4},{6,5},{7,6},{8,11},{9,8},{10,9... | collective-permute-start | bytes 786440 | tf_op jit(solution)/shard_map/ppermute | solution.py:686
  12.3 6.1 %collective-permute-start.2 = (bf16[128,512]{1,0:T(8,128)(2,1)S(1)}, bf16[128,512]{1,0:T(8,128)(2,1)S(1)}, u32[]{:S(2)}, u32[]{:S(2)}) collective-permute-start(bf16[128,512]{1,0:T(8,128)(2,1)S(1)} %get-tuple-element.40), channel_id=1, source_target_pairs={{0,1},{1,2},{2,3},{3,0},{4,5},{5,6},{6,7},{7,4},{8,9},{9,10},{10,1... | collective-permute-start | bytes 393224 | tf_op jit(solution)/shard_map/ppermute | solution.py:686
  13.6 4.9 %collective-permute-start.3 = (bf16[128,512]{1,0:T(8,128)(2,1)S(1)}, bf16[128,512]{1,0:T(8,128)(2,1)S(1)}, u32[]{:S(2)}, u32[]{:S(2)}) collective-permute-start(bf16[128,512]{1,0:T(8,128)(2,1)S(1)} %get-tuple-element.41), channel_id=1, source_target_pairs={{0,3},{1,0},{2,1},{3,2},{4,7},{5,4},{6,5},{7,6},{8,11},{9,8},{10,9... | collective-permute-start | bytes 393224 | tf_op jit(solution)/shard_map/ppermute | solution.py:686
  15.1 7.7 %collective-permute-start.9 = (bf16[256,512]{1,0:T(8,128)(2,1)}, bf16[256,512]{1,0:T(8,128)(2,1)S(1)}, u32[]{:S(2)}, u32[]{:S(2)}) collective-permute-start(bf16[256,512]{1,0:T(8,128)(2,1)} %own.1), channel_id=1, source_target_pairs={{0,3},{1,0},{2,1},{3,2},{4,7},{5,4},{6,5},{7,6},{8,11},{9,8},{10,9... | collective-permute-start | bytes 786440 | tf_op jit(solution)/shard_map/ppermute | solution.py:686
  16.4 8.8 %collective-permute-start.8 = (bf16[256,512]{1,0:T(8,128)(2,1)}, bf16[256,512]{1,0:T(8,128)(2,1)S(1)}, u32[]{:S(2)}, u32[]{:S(2)}) collective-permute-start(bf16[256,512]{1,0:T(8,128)(2,1)} %own.1), channel_id=1, source_target_pairs={{0,1},{1,2},{2,3},{3,0},{4,5},{5,6},{6,7},{7,4},{8,9},{9,10},{10,1... | collective-permute-start | bytes 786440 | tf_op jit(solution)/shard_map/ppermute | solution.py:686
  18.6 10.6 %collective-permute-start.6 = (bf16[256,512]{1,0:T(8,128)(2,1)S(1)}, bf16[256,512]{1,0:T(8,128)(2,1)S(1)}, u32[]{:S(2)}, u32[]{:S(2)}) collective-permute-start(bf16[256,512]{1,0:T(8,128)(2,1)S(1)} %embed.1.own), channel_id=1, source_target_pairs={{0,3},{1,0},{2,1},{3,2},{4,7},{5,4},{6,5},{7,6},{8,11},{9,8},{10,9... | collective-permute-start | bytes 786440 | tf_op jit(solution)/shard_map/ppermute | solution.py:686
  21.2 10.7 %collective-permute-start.4 = (bf16[256,512]{1,0:T(8,128)(2,1)S(1)}, bf16[256,512]{1,0:T(8,128)(2,1)S(1)}, u32[]{:S(2)}, u32[]{:S(2)}) collective-permute-start(bf16[256,512]{1,0:T(8,128)(2,1)S(1)} %embed.1.own), channel_id=1, source_target_pairs={{0,1},{1,2},{2,3},{3,0},{4,5},{5,6},{6,7},{7,4},{8,9},{9,10},{10,1... | collective-permute-start | bytes 786440 | tf_op jit(solution)/shard_map/ppermute | solution.py:686
  22.7 9.4 %collective-permute-start.11 = (bf16[128,512]{1,0:T(8,128)(2,1)S(1)}, bf16[128,512]{1,0:T(8,128)(2,1)S(1)}, u32[]{:S(2)}, u32[]{:S(2)}) collective-permute-start(bf16[128,512]{1,0:T(8,128)(2,1)S(1)} %slice.19), channel_id=1, source_target_pairs={{0,3},{1,0},{2,1},{3,2},{4,7},{5,4},{6,5},{7,6},{8,11},{9,8},{10,9... | collective-permute-start | bytes 393224 | tf_op jit(solution)/shard_map/ppermute | solution.py:686
  25.3 6.9 %copy-start.1 = (bf16[256,512]{1,0:T(8,128)(2,1)S(1)}, bf16[256,512]{1,0:T(8,128)(2,1)}, u32[]{:S(2)}) copy-start(bf16[256,512]{1,0:T(8,128)(2,1)} %own.1) | copy-start | bytes 786436
  25.3 6.9 %copy-start.2 = (bf16[2048,4]{0,1:T(4,128)(2,1)S(1)}, bf16[2048,4]{0,1:T(4,128)(2,1)}, u32[]{:S(2)}) copy-start(bf16[2048,4]{0,1:T(4,128)(2,1)} %param.18) | copy-start | bytes 49156
  25.3 6.9 %copy-start.3 = (f32[2048]{0:T(1024)S(1)}, f32[2048]{0:T(1024)}, u32[]{:S(2)}) copy-start(f32[2048]{0:T(1024)} %param.16) | copy-start | bytes 24580
  25.3 6.9 %copy-start.4 = (f32[4]{0:T(128)S(1)}, f32[4]{0:T(128)}, u32[]{:S(2)}) copy-start(f32[4]{0:T(128)} %ceiling_ref.5) | copy-start | bytes 52
  25.3 6.8 %collective-permute-start.10 = (bf16[128,512]{1,0:T(8,128)(2,1)S(1)}, bf16[128,512]{1,0:T(8,128)(2,1)S(1)}, u32[]{:S(2)}, u32[]{:S(2)}) collective-permute-start(bf16[128,512]{1,0:T(8,128)(2,1)S(1)} %slice.18), channel_id=1, source_target_pairs={{0,1},{1,2},{2,3},{3,0},{4,5},{5,6},{6,7},{7,4},{8,9},{9,10},{10,1... | collective-permute-start | bytes 393224 | tf_op jit(solution)/shard_map/ppermute | solution.py:686
  29.1 11.5 %collective-permute-start.7 = (bf16[128,512]{1,0:T(8,128)(2,1)S(1)}, bf16[128,512]{1,0:T(8,128)(2,1)S(1)}, u32[]{:S(2)}, u32[]{:S(2)}) collective-permute-start(bf16[128,512]{1,0:T(8,128)(2,1)S(1)} %slice.17), channel_id=1, source_target_pairs={{0,3},{1,0},{2,1},{3,2},{4,7},{5,4},{6,5},{7,6},{8,11},{9,8},{10,9... | collective-permute-start | bytes 393224 | tf_op jit(solution)/shard_map/ppermute | solution.py:686
  31.9 8.8 %collective-permute-start.5 = (bf16[128,512]{1,0:T(8,128)(2,1)S(1)}, bf16[128,512]{1,0:T(8,128)(2,1)S(1)}, u32[]{:S(2)}, u32[]{:S(2)}) collective-permute-start(bf16[128,512]{1,0:T(8,128)(2,1)S(1)} %slice.16), channel_id=1, source_target_pairs={{0,1},{1,2},{2,3},{3,0},{4,5},{5,6},{6,7},{7,4},{8,9},{9,10},{10,1... | collective-permute-start | bytes 393224 | tf_op jit(solution)/shard_map/ppermute | solution.py:686
  38.1 2.6 %copy-start.6 = (f32[32]{0:T(128)S(1)}, f32[32]{0:T(128)}, u32[]{:S(2)}) copy-start(f32[32]{0:T(128)} %forget_ref.3) | copy-start | bytes 388
  40.7 26.4 %copy-start.7 = (s32[32]{0:T(128)S(1)}, s32[32]{0:T(128)}, u32[]{:S(2)}) copy-start(s32[32]{0:T(128)} %start_ref.1) | copy-start | bytes 388
  43.3 38.1 %copy-start = (bf16[512,2048]{1,0:T(8,128)(2,1)S(1)}, bf16[512,2048]{1,0:T(8,128)(2,1)}, u32[]{:S(2)}) copy-start(bf16[512,2048]{1,0:T(8,128)(2,1)} %out_proj.3) | copy-start | bytes 6291460
  43.4 38.1 %copy-start.5 = (f32[4,128]{1,0:T(4,128)S(1)}, f32[4,128]{1,0:T(4,128)}, u32[]{:S(2)}) copy-start(f32[4,128]{1,0:T(4,128)} %out_gain.1) | copy-start | bytes 6148
  68.7 12.7 %all-to-all-start.1 = ((bf16[32,32,128]{2,1,0:T(8,128)(2,1)}), bf16[32,32,128]{2,1,0:T(8,128)(2,1)S(1)}, u32[]{:S(2)}, u32[]{:S(2)}) async-start(bf16[32,32,128]{2,1,0:T(8,128)(2,1)} %state_scan.1), calls=%async_computation.1 | async-start | bytes 524288 | tf_op jit(solution)/shard_map/all_to_all | solution.py:753
  84.2 8.5 %collective-permute-start.13 = (bf16[256,512]{1,0:T(8,128)(2,1)S(1)}, bf16[256,512]{1,0:T(8,128)(2,1)S(1)}, u32[]{:S(2)}, u32[]{:S(2)}) collective-permute-start(bf16[256,512]{1,0:T(8,128)(2,1)S(1)} %get-tuple-element.65), channel_id=1, source_target_pairs={{0,3},{1,0},{2,1},{3,2},{4,7},{5,4},{6,5},{7,6},{8,11},{9,8},{10,9... | collective-permute-start | bytes 786440 | tf_op jit(solution)/shard_map/ppermute | solution.py:686
  87.2 9.1 %collective-permute-start.15 = (bf16[256,512]{1,0:T(8,128)(2,1)S(1)}, bf16[256,512]{1,0:T(8,128)(2,1)S(1)}, u32[]{:S(2)}, u32[]{:S(2)}) collective-permute-start(bf16[256,512]{1,0:T(8,128)(2,1)S(1)} %get-tuple-element.68), channel_id=1, source_target_pairs={{0,1},{1,2},{2,3},{3,0},{4,5},{5,6},{6,7},{7,4},{8,9},{9,10},{10,1... | collective-permute-start | bytes 786440 | tf_op jit(solution)/shard_map/ppermute | solution.py:686
  88.8 12.7 %collective-permute-start.12 = (bf16[256,512]{1,0:T(8,128)(2,1)S(1)}, bf16[256,512]{1,0:T(8,128)(2,1)S(1)}, u32[]{:S(2)}, u32[]{:S(2)}) collective-permute-start(bf16[256,512]{1,0:T(8,128)(2,1)S(1)} %get-tuple-element.63), channel_id=1, source_target_pairs={{0,1},{1,2},{2,3},{3,0},{4,5},{5,6},{6,7},{7,4},{8,9},{9,10},{10,1... | collective-permute-start | bytes 786440 | tf_op jit(solution)/shard_map/ppermute | solution.py:686
  92.8 8.7 %collective-permute-start.14 = (bf16[256,512]{1,0:T(8,128)(2,1)S(1)}, bf16[256,512]{1,0:T(8,128)(2,1)S(1)}, u32[]{:S(2)}, u32[]{:S(2)}) collective-permute-start(bf16[256,512]{1,0:T(8,128)(2,1)S(1)} %add_convert_fusion.3), channel_id=1, source_target_pairs={{0,3},{1,0},{2,1},{3,2},{4,7},{5,4},{6,5},{7,6},{8,11},{9,8},{10,9... | collective-permute-start | bytes 786440 | tf_op jit(solution)/shard_map/ppermute | solution.py:686
  96.3 10.2 %collective-permute-start.17 = (bf16[256,512]{1,0:T(8,128)(2,1)S(1)}, bf16[256,512]{1,0:T(8,128)(2,1)S(1)}, u32[]{:S(2)}, u32[]{:S(2)}) collective-permute-start(bf16[256,512]{1,0:T(8,128)(2,1)S(1)} %get-tuple-element.69), channel_id=1, source_target_pairs={{0,3},{1,0},{2,1},{3,2},{4,7},{5,4},{6,5},{7,6},{8,11},{9,8},{10,9... | collective-permute-start | bytes 786440 | tf_op jit(solution)/shard_map/ppermute | solution.py:686
  96.4 10.7 %collective-permute-start.16 = (bf16[256,512]{1,0:T(8,128)(2,1)S(1)}, bf16[256,512]{1,0:T(8,128)(2,1)S(1)}, u32[]{:S(2)}, u32[]{:S(2)}) collective-permute-start(bf16[256,512]{1,0:T(8,128)(2,1)S(1)} %add_convert_fusion.1), channel_id=1, source_target_pairs={{0,1},{1,2},{2,3},{3,0},{4,5},{5,6},{6,7},{7,4},{8,9},{9,10},{10,1... | collective-permute-start | bytes 786440 | tf_op jit(solution)/shard_map/ppermute | solution.py:686

commit v5 on v4

--- a/solution.py
+++ b/solution.py
@@ -40,48 +40,36 @@
     return pl.BlockSpec(dims, lambda *_: (0,) * len(dims))
 
 
-def columns_of(place, step, count, width):
-    return pl.ds(pl.multiple_of(lax.rem(place + step, count) * width, width), width)
-
-
-def adapter_blocks(place_ref, patches_ref, adapter_ref, patches, blocks, sems, steps):
+def columns_of(place_ref, slot, width):
+    return pl.ds(pl.multiple_of(place_ref[slot] * width, width), width)
+
+
+def adapter_blocks(place_ref, patches_ref, adapter_ref, patches, blocks, sems, slots):
     patches_copy = pltpu.make_async_copy(patches_ref.at[0], patches, sems.at[0])
     patches_copy.start()
     copies = []
-    for at, step in enumerate(steps):
-        columns = columns_of(place_ref[0], step, 4, blocks.shape[2])
+    for at, slot in enumerate(slots):
+        columns = columns_of(place_ref, slot, blocks.shape[2])
         copies.append(
             pltpu.make_async_copy(adapter_ref.at[:, columns], blocks.at[at], sems.at[at + 1])
         )
         copies[at].start()
     patches_copy.wait()
     rows = patches[...].T
-    for at in range(len(steps)):
+    for at in range(len(slots)):
         copies[at].wait()
         yield jnp.dot(rows, blocks[at], preferred_element_type=F32)
 
 
-def adapter_kernel(place_ref, patches_ref, adapter_ref, *refs):
-    to_next, to_last, near_next, near_last, patches, blocks, sems = refs
-    half = near_next.shape[0]
-    steps = (2, 1, 3)
-    made = adapter_blocks(place_ref, patches_ref, adapter_ref, patches, blocks, sems, steps)
-    for step, block in zip(steps, made):
-        small = block.astype(BF16)
-        if step == 2:
-            to_next[:half] = small[:half]
-            to_last[half:] = small[half:]
-        elif step == 1:
-            near_next[...] = small[:half]
-            to_next[half:] = small[half:]
-        else:
-            to_last[:half] = small[:half]
-            near_last[...] = small[half:]
-
-
-def own_kernel(place_ref, patches_ref, adapter_ref, own, patches, blocks, sems):
-    for block in adapter_blocks(place_ref, patches_ref, adapter_ref, patches, blocks, sems, (0,)):
-        own[...] = block
+def leave_kernel(place_ref, patches_ref, adapter_ref, out, *scratch):
+    rows = out.shape[0] // 2
+    for at, block in enumerate(adapter_blocks(place_ref, patches_ref, adapter_ref, *scratch, (1, 3))):
+        out[at * rows : (at + 1) * rows] = block.astype(BF16)
+
+
+def stay_kernel(place_ref, patches_ref, adapter_ref, out, *scratch):
+    for at, block in enumerate(adapter_blocks(place_ref, patches_ref, adapter_ref, *scratch, (2, 0))):
+        out[at] = block
 
 
 def adapter_call(kernel, outs, count, place, patches, adapter):
@@ -101,70 +89,55 @@
     )(place, *in_hbm(patches, adapter))
 
 
-def adapter_sums(*arrays):
+def adapter_leave(*arrays):
     rows, width = arrays[1].shape[2], arrays[2].shape[1] // 4
-    outs = (shape_of(rows, width),) * 2 + (shape_of(rows // 2, width),) * 2
-    return adapter_call(adapter_kernel, outs, 3, *arrays)
-
-
-def adapter_own(*arrays):
+    return adapter_call(leave_kernel, shape_of(2 * rows, width), 2, *arrays)
+
+
+def adapter_stay(*arrays):
     rows, width = arrays[1].shape[2], arrays[2].shape[1] // 4
-    outs = shape_of(rows, width, dtype=F32)
-    return adapter_call(own_kernel, outs, 1, *arrays)
-
-
-def pass_kernel(from_left, from_right, near_next, near_last, next_out, last_out):
-    half = near_next.shape[0]
-    next_out[...] = (near_next[...].astype(F32) + from_left[:half].astype(F32)).astype(BF16)
-    last_out[...] = (near_last[...].astype(F32) + from_right[half:].astype(F32)).astype(BF16)
-
-
-def pass_call(*arrays):
-    half = shape_of(*arrays[2].shape)
-    return pl.pallas_call(
-        pass_kernel,
-        out_shape=(half, half),
-        in_specs=[VMEM] * 4,
-        out_specs=(VMEM, VMEM),
-        compiler_params=limit(4),
-        name="pass_on",
-    )(*arrays)
-
-
-def embed_kernel(own, from_left, from_right, left, right, out):
-    half = left.shape[0]
-    first = own[:half] + left[...].astype(F32) + from_right[:half].astype(F32)
-    second = own[half:] + from_left[half:].astype(F32) + right[...].astype(F32)
-    out[:half] = first.astype(BF16)
-    out[half:] = second.astype(BF16)
-
-
-def embed_call(own, *arrays):
-    return pl.pallas_call(
-        embed_kernel,
-        out_shape=shape_of(*own.shape),
-        in_specs=[VMEM] * 5,
+    outs = shape_of(2, rows, width, dtype=F32)
+    return adapter_call(stay_kernel, outs, 2, *arrays)
+
+
+def small_call(kernel, out, *arrays):
+    return pl.pallas_call(
+        kernel,
+        out_shape=out,
+        in_specs=[VMEM] * len(arrays),
         out_specs=VMEM,
         compiler_params=limit(4),
-        name="embed",
-    )(own, *arrays)
-
-
-def normalize(place, chunks, gain_ref, normed):
-    own, left, right, far_a, far_b = chunks
+    )(*arrays)
+
+
+def pass_kernel(stay, arrived, out):
+    rows = out.shape[0]
+    out[...] = (stay[0] + arrived[rows:].astype(F32)).astype(BF16)
+
+
+def embed_kernel(stay, arrived, last, out):
+    rows = out.shape[0]
+    out[...] = (stay[1] + arrived[:rows].astype(F32) + last[...].astype(F32)).astype(BF16)
+
+
+def join_kernel(one, two, out):
+    rows = one.shape[0]
+    out[:rows] = one[...]
+    out[rows:] = two[...]
+
+
+def normalize(place_ref, chunks, gain_ref, normed):
+    own, first, others = chunks
     rows, width = own.shape
-    half = rows // 2
-    for at, far in ((0, far_a), (half, far_b)):
-        span = slice(at, at + half)
-        values = ((0, own[span]), (3, left[span]), (1, right[span]), (2, far[...]))
-        total = 0.0
-        for _, value in values:
-            value = value.astype(F32)
-            total += jnp.sum(value * value, axis=-1, keepdims=True)
-        scale = lax.rsqrt(total / (4 * width) + EPSILON)
-        for step, value in values:
-            columns = columns_of(place, step, 4, width)
-            normed[span, columns] = (value.astype(F32) * scale * gain_ref[:, columns]).astype(BF16)
+    values = (own[...], first[...], others[:rows], others[rows:])
+    total = 0.0
+    for value in values:
+        value = value.astype(F32)
+        total += jnp.sum(value * value, axis=-1, keepdims=True)
+    scale = lax.rsqrt(total / (4 * width) + EPSILON)
+    for slot, value in enumerate(values):
+        columns = columns_of(place_ref, slot, width)
+        normed[:, columns] = (value.astype(F32) * scale * gain_ref[:, columns]).astype(BF16)
 
 
 def product(normed, weight):
@@ -231,10 +204,8 @@
     place_ref,
     ceiling_ref,
     own,
-    left,
-    right,
-    far_a,
-    far_b,
+    first,
+    others,
     gain_ref,
     weight,
     decay_ref,
@@ -255,7 +226,7 @@
     ]
     for copy in copies:
         copy.start()
-    normalize(place_ref[0], (own, left, right, far_a, far_b), gain_ref, normed)
+    normalize(place_ref, (own, first, others), gain_ref, normed)
     decay_sums(decay_logits(normed[...], decay_ref[...]), columns, lanes)
     for part in range(3):
         parts[part] = product(normed, weight[part]).astype(BF16)
@@ -282,11 +253,11 @@
 
 
 def image_near_kernel(
-    place_ref, own, left, right, gain_ref, weight, decay_ref, scaled_out, total, logits, squares, scaled, sems
+    place_ref, own, first, gain_ref, weight, decay_ref, scaled_out, total, logits, squares, scaled, sems
 ):
     copies = []
-    for at, (step, ref) in enumerate(((0, own), (3, left), (1, right))):
-        columns = columns_of(place_ref[0], step, 4, own.shape[1])
+    for at, ref in enumerate((own, first)):
+        columns = columns_of(place_ref, at, own.shape[1])
         value = ref[...].astype(F32)
         square = jnp.sum(value * value, axis=-1, keepdims=True)
         small = (value * gain_ref[:, columns]).astype(BF16)
@@ -313,8 +284,7 @@
     place_ref,
     ceiling_ref,
     forget_ref,
-    far_a,
-    far_b,
+    others,
     total,
     logits,
     squares,
@@ -333,27 +303,31 @@
     key_value,
     sems,
 ):
-    half, width = far_a.shape
-    chunk = columns_of(place_ref[0], 2, 4, width)
-    square = []
-    for at, ref in ((0, far_a), (half, far_b)):
-        value = ref[...].astype(F32)
-        square.append(jnp.sum(value * value, axis=-1, keepdims=True))
-        scaled[at : at + half] = (value * gain_ref[:, chunk]).astype(BF16)
-    square = squares[...] + jnp.concatenate(square, axis=0)
+    rows, width = others.shape[0] // 2, others.shape[1]
+    square = squares[...]
+    chunks = []
+    for at in range(2):
+        chunks.append(columns_of(place_ref, at + 2, width))
+        value = others[at * rows : (at + 1) * rows].astype(F32)
+        square += jnp.sum(value * value, axis=-1, keepdims=True)
+        scaled[at] = (value * gain_ref[:, chunks[at]]).astype(BF16)
     scale = lax.rsqrt(square / (4 * width) + EPSILON)
     scale_out[...] = scale
-    small = scaled[...]
     for at in range(2):
-        term = jnp.dot(small, weight[at + 1, chunk, :], preferred_element_type=F32)
-        key_value[at] = ((total[at] + term) * scale).astype(BF16)
+        term = total[at]
+        for place, chunk in enumerate(chunks):
+            term += jnp.dot(scaled[place], weight[at + 1, chunk, :], preferred_element_type=F32)
+        key_value[at] = (term * scale).astype(BF16)
     far_copy = pltpu.make_async_copy(scaled, far_out, sems.at[0])
     far_copy.start()
-    decay_sums((logits[...] + decay_logits(small, decay_ref[:, chunk])) * scale, columns, lanes)
+    gates = logits[...]
+    for place, chunk in enumerate(chunks):
+        gates += decay_logits(scaled[place], decay_ref[:, chunk])
+    decay_sums(gates * scale, columns, lanes)
     key_value_copy = pltpu.make_async_copy(key_value, key_value_out, sems.at[1])
     key_value_copy.start()
     state_out[:, 0:16, :] = other_state[...]
-    burst = jnp.log1p(jnp.full((1, 1), -forget_ref[place_ref[1]], F32))
+    burst = jnp.log1p(jnp.full((1, 1), -forget_ref[place_ref[4]], F32))
     ids = lax.broadcasted_iota(jnp.int32, (8, HEAD_WIDTH), 0)
     for head in range(4):
         state, span = chunk_state(
@@ -393,12 +367,11 @@
     query,
     sems,
 ):
-    width = far_ref.shape[1]
-    pieces = [
-        (near_ref.at[at], scaled.at[:, columns_of(place_ref[0], step, 4, width)])
-        for at, step in enumerate((0, 3, 1))
-    ]
-    pieces.append((far_ref, scaled.at[:, columns_of(place_ref[0], 2, 4, width)]))
+    width = far_ref.shape[2]
+    pieces = []
+    for slot in range(4):
+        ref = (near_ref, far_ref)[slot // 2]
+        pieces.append((ref.at[slot % 2], scaled.at[:, columns_of(place_ref, slot, width)]))
     pieces += [
         (weight_ref.at[0], weight.at[0]),
         (weight_ref.at[1], weight.at[1]),
@@ -417,7 +390,7 @@
     copies[5].wait()
     gate_out[...] = silu_of(product(scaled, weight[1]) * scale)
     copies[6].wait()
-    burst = jnp.log1p(jnp.full((1, 1), -forget_ref[place_ref[1]], F32))
+    burst = jnp.log1p(jnp.full((1, 1), -forget_ref[place_ref[4]], F32))
     for head in range(4):
         attend(
             head,
@@ -506,7 +479,7 @@
 def image_near_call(place, near, gain, weights, decay):
     rows, width = near[0].shape
     outs = (
-        hbm_of(3, rows, width),
+        hbm_of(2, rows, width),
         shape_of(2, rows, width, dtype=F32),
         shape_of(rows, HEAD_WIDTH, dtype=F32),
         shape_of(rows, 1, dtype=F32),
@@ -514,20 +487,19 @@
     return pl.pallas_call(
         image_near_kernel,
         out_shape=outs,
-        in_specs=[SMEM] + [VMEM] * 6,
+        in_specs=[SMEM] + [VMEM] * 5,
         out_specs=(HBM,) + (VMEM,) * 3,
-        scratch_shapes=[pltpu.VMEM((3, rows, width), BF16), pltpu.SemaphoreType.DMA((3,))],
+        scratch_shapes=[pltpu.VMEM((2, rows, width), BF16), pltpu.SemaphoreType.DMA((2,))],
         compiler_params=limit(16),
-        cost_estimate=cost_of(rows, 3 * width, 2 * width),
+        cost_estimate=cost_of(rows, 2 * width, 2 * width),
         name="image_near",
     )(place, *near, gain, weights, decay)
 
 
 def image_state_call(place, ceiling, forget, *arrays):
-    half, width = arrays[0].shape
-    rows = 2 * half
+    rows, width = arrays[0].shape[0] // 2, arrays[0].shape[1]
     outs = (
-        hbm_of(rows, width),
+        hbm_of(2, rows, width),
         hbm_of(2, rows, width),
         shape_of(rows, 1, dtype=F32),
         shape_of(rows, 4, dtype=F32),
@@ -540,7 +512,7 @@
         in_specs=[SMEM] * 3 + [VMEM] * len(arrays),
         out_specs=(HBM, HBM) + (VMEM,) * 4,
         scratch_shapes=[
-            pltpu.VMEM((rows, width), BF16),
+            pltpu.VMEM((2, rows, width), BF16),
             pltpu.VMEM((2, rows, width), BF16),
             pltpu.SemaphoreType.DMA((2,)),
         ],
@@ -551,7 +523,7 @@
 
 
 def image_attend_call(place, ceiling, forget, weights, near, far, key_value, *small):
-    rows, width = far.shape
+    rows, width = far.shape[1:]
     depth = 4 * width
     outs = (
         hbm_of(rows, width),
@@ -616,14 +588,14 @@
 
 
 def gate_kernel(place_ref, entering, out_gain, out_proj, *refs):
-    sources, (far_text, far_image, gated), buffers, sems = refs[:6], refs[6:9], refs[9:15], refs[15]
+    sources, (leave_t, leave_i, gated), buffers, sems = refs[:6], refs[6:9], refs[9:15], refs[15]
     copies = [
         pltpu.make_async_copy(source, buffer, sems.at[at])
         for at, (source, buffer) in enumerate(zip(sources, buffers))
     ]
     for copy in copies:
         copy.start()
-    rows, width = far_text.shape
+    rows, width = leave_t.shape[0] // 2, leave_t.shape[1]
     for kind in range(2):
         for copy in copies[3 * kind : 3 * kind + 3]:
             copy.wait()
@@ -637,15 +609,16 @@
             scale = lax.rsqrt(jnp.mean(attended * attended, axis=-1, keepdims=True) + EPSILON)
             value = attended * scale * out_gain[head : head + 1, :] * gate[:, lanes].astype(F32)
             gated[kind * rows : (kind + 1) * rows, lanes] = value.astype(BF16)
-    weight = out_proj[:, columns_of(place_ref[0], 2, 4, width)]
-    block = jnp.dot(gated[...], weight, preferred_element_type=F32).astype(BF16)
-    far_text[...] = block[:rows]
-    far_image[...] = block[rows:]
+    for at, slot in enumerate((1, 3)):
+        weight = out_proj[:, columns_of(place_ref, slot, width)]
+        block = jnp.dot(gated[...], weight, preferred_element_type=F32).astype(BF16)
+        leave_t[at * rows : (at + 1) * rows] = block[:rows]
+        leave_i[at * rows : (at + 1) * rows] = block[rows:]
 
 
 def gate_call(place, entering, out_gain, out_proj, text_parts, image_parts):
     rows, width = text_parts[0].shape
-    outs = (shape_of(rows, width), shape_of(rows, width), shape_of(2 * rows, width))
+    outs = (shape_of(2 * rows, width),) * 3
     parts = in_hbm(*text_parts, *image_parts)
     return pl.pallas_call(
         gate_kernel,
@@ -655,44 +628,45 @@
         scratch_shapes=[pltpu.VMEM(p.shape, p.dtype) for p in parts]
         + [pltpu.SemaphoreType.DMA((6,))],
         compiler_params=limit(16),
-        name="gate_far",
+        name="gate_leave",
     )(place, entering, out_gain, out_proj, *parts)
 
 
-def near_kernel(place_ref, gated, out_proj, next_t, next_i, last_t, last_i, own_t, own_i):
-    rows, width = next_t.shape
-    for step, text, image in ((1, next_t, next_i), (3, last_t, last_i), (0, own_t, own_i)):
-        weight = out_proj[:, columns_of(place_ref[0], step, 4, width)]
+def stay_blocks_kernel(place_ref, gated, out_proj, pass_t, pass_i, own_t, own_i):
+    rows, width = own_t.shape
+    for slot, text, image in ((2, pass_t, pass_i), (0, own_t, own_i)):
+        weight = out_proj[:, columns_of(place_ref, slot, width)]
         block = jnp.dot(gated[...], weight, preferred_element_type=F32)
-        text[...] = block[:rows].astype(text.dtype)
-        image[...] = block[rows:].astype(image.dtype)
-
-
-def near_call(place, gated, out_proj):
+        text[...] = block[:rows]
+        image[...] = block[rows:]
+
+
+def stay_call(place, gated, out_proj):
     rows, width = gated.shape[0] // 2, gated.shape[1]
-    outs = (shape_of(rows, width),) * 4 + (shape_of(rows, width, dtype=F32),) * 2
-    return pl.pallas_call(
-        near_kernel,
-        out_shape=outs,
+    return pl.pallas_call(
+        stay_blocks_kernel,
+        out_shape=(shape_of(rows, width, dtype=F32),) * 4,
         in_specs=[SMEM, VMEM, VMEM],
-        out_specs=(VMEM,) * 6,
+        out_specs=(VMEM,) * 4,
         compiler_params=limit(16),
-        cost_estimate=cost_of(2 * rows, width, 3 * width),
-        name="near_blocks",
+        cost_estimate=cost_of(2 * rows, width, 2 * width),
+        name="stay_blocks",
     )(place, gated, out_proj)
 
 
-def moved(array, step):
-    return lax.ppermute(array, "head", [(i, (i + step) % 4) for i in range(4)])
+def moved(array, turn):
+    pairs = []
+    for core in range(2):
+        for x in range(4):
+            partner = x ^ 1 if (core + turn) % 2 == 0 else 3 - x
+            pairs.append((4 * core + x, 4 * core + partner))
+    return lax.ppermute(array, ("seq_2", "head"), pairs)
 
 
 def gathered(rows):
-    half = rows.shape[0] // 2
-    left = moved(rows, 1)
-    right = moved(rows, 3)
-    far_a = moved(left[:half], 1)
-    far_b = moved(right[half:], 3)
-    return (rows, left, right, far_a, far_b)
+    first = moved(rows, 0)
+    joined = small_call(join_kernel, shape_of(2 * rows.shape[0], rows.shape[1]), rows, first)
+    return (rows, first, moved(joined, 1))
 
 
 def added(one, two):
@@ -712,33 +686,34 @@
     out_gain,
     out_proj,
 ):
-    place = jnp.stack([lax.axis_index("head"), lax.axis_index(SEQ)]).astype(jnp.int32)
+    x = lax.axis_index("head")
+    even = lax.axis_index("seq_2") == 0
+    first, second = jnp.where(even, x ^ 1, 3 - x), jnp.where(even, 3 - x, x ^ 1)
+    place = jnp.stack([x, first, second, x ^ 2, lax.axis_index(SEQ)]).astype(jnp.int32)
     decay = decay_proj.T
     gain = norm_gain[None]
     ceiling = head_decay_ceiling
 
     text_chunks = gathered(text_embed)
     patches = image_patches.transpose(0, 2, 1)
-    to_next, to_last, near_next, near_last = adapter_sums(place, patches, adapter)
-    own = adapter_own(place, patches, adapter)
+    leaving = adapter_leave(place, patches, adapter)
+    stay = adapter_stay(place, patches, adapter)
     weights = relay_call(in_proj)
-    from_left = moved(to_next, 1)
-    from_right = moved(to_last, 3)
-    next_sum, last_sum = pass_call(from_left, from_right, near_next, near_last)
-    left = moved(next_sum, 1)
-    right = moved(last_sum, 3)
-    embed = embed_call(own, from_left, from_right, left, right)
+    block = shape_of(*text_embed.shape)
+    arrived = moved(leaving, 0)
+    last = moved(small_call(pass_kernel, block, stay, arrived), 1)
+    embed = small_call(embed_kernel, block, stay, arrived, last)
     image_chunks = gathered(embed)
 
     *text_parts, text_state, text_span, late_weights = text_call(
         place, ceiling, text_chunks, gain, weights, decay
     )
-    near, *partial = image_near_call(place, image_chunks[:3], gain, weights, decay)
+    near, *partial = image_near_call(place, image_chunks[:2], gain, weights, decay)
     *held, states = image_state_call(
         place,
         ceiling,
         image_forget,
-        *image_chunks[3:],
+        image_chunks[2],
         *partial,
         gain,
         weights,
@@ -752,18 +727,17 @@
     )
     entering = lax.all_to_all(scan_call(image_start, slices), SEQ, 0, 0, tiled=True)
 
-    far_t, far_i, gated = gate_call(
+    leave_t, leave_i, gated = gate_call(
         place, entering, out_gain, out_proj, text_parts, image_parts
     )
-    next_t, next_i, last_t, last_i, own_t, own_i = near_call(place, gated, out_proj)
-    far_from_left = moved(far_t, 1)
-    far_from_right = moved(far_i, 3)
-    left_i = moved(next_i, 1)
-    right_t = moved(last_t, 3)
-    left_t = moved(added(next_t, far_from_left), 1)
-    right_i = moved(added(last_i, far_from_right), 3)
-    text_out = text_embed.astype(F32) + (own_t + left_t.astype(F32) + right_t.astype(F32))
-    image_out = embed.astype(F32) + (own_i + left_i.astype(F32) + right_i.astype(F32))
+    pass_t, pass_i, own_t, own_i = stay_call(place, gated, out_proj)
+    rows = own_t.shape[0]
+    arrived_t = moved(leave_t, 0)
+    arrived_i = moved(leave_i, 0)
+    last_t = moved(added(pass_t, arrived_t[rows:]), 1)
+    last_i = moved(added(pass_i, arrived_i[rows:]), 1)
+    text_out = text_embed.astype(F32) + (own_t + arrived_t[:rows].astype(F32) + last_t.astype(F32))
+    image_out = embed.astype(F32) + (own_i + arrived_i[:rows].astype(F32) + last_i.astype(F32))
     return (image_out.astype(BF16)[None], text_out.astype(BF16))
 
 

time: 109 us -> 111 us (1.018); the launches traced: 108 us -> 109 us
  waiting for transfers between devices: 22.9 us -> 34.5 us
  starting transfers between devices: 27.6 us -> 17.5 us
    ppermute x18 -> x10, waiting for transfers between devices: 19.3 us -> 31 us  [moved(): return lax.ppermute(array, ('seq_2', 'head'), pairs)]
    ppermute x18 -> x10, starting transfers between devices: 23.9 us -> 13.7 us  [moved(): return lax.ppermute(array, ('seq_2', 'head'), pairs)]
  transfers between devices with their start and end apart: 19 -> 11, of which waited for: 7 -> 9; matrix products, arithmetic and copies ran while one was open for 1% -> 1% of each run, Pallas kernels for 20% -> 19%
where the time goes in v5:
time: 111 us; the launch traced here: 109 us
  waiting for transfers between devices  34.5 us (31%)
  Pallas kernels  30.8 us (28%)
  blocking collectives  22.9 us (21%)
  starting transfers between devices  17.5 us (16%)
  other arithmetic  1.9 us (2%)
    ppermute x10, waiting for transfers between devices, moved(): return lax.ppermute(array, ('seq_2', 'head'), pairs)  31 us
    all_to_all x1, blocking collectives, steps(): slices = lax.all_to_all(states, SEQ, 0, 0, tiled=True)  22.9 us
    ppermute x10, starting transfers between devices, moved(): return lax.ppermute(array, ('seq_2', 'head'), pairs)  13.7 us
    pallas_call x1, Pallas kernels, text_call(): pl.pallas_call(text_kernel, grid=(1,), out_shape=outs, in_specs=[SMEM, SM...  6.06 us
    pallas_call x1, Pallas kernels, image_attend_call(): pl.pallas_call(image_attend_kernel, grid=(1,), out_shape=outs, in_specs=[...  5.4 us
    pallas_call x2, Pallas kernels, adapter_call(): pl.pallas_call(kernel, out_shape=outs, in_specs=[SMEM, HBM, HBM], out_spe...  4.39 us
    all_to_all x1, starting transfers between devices, steps(): lax.all_to_all(scan_call(image_start, slices), SEQ, 0, 0, tiled=True)  3.84 us
    pallas_call x1, Pallas kernels, relay_call(): pl.pallas_call(relay_kernel, out_shape=pltpu.VMEM((parts, depth, width),...  3.71 us
  transfers between devices with their start and end apart: 11, of which 9 were waited for; matrix products, arithmetic and copies ran while one was open for 1% of the time, Pallas kernels for 19%

profile of v5, /device:TPU:1, one launch (start us, length us, event | category | flops | bytes accessed | tf_op | source)
XLA Modules:
  0.0 108.6 jit_solution(11602911945665657116)
XLA Ops:
  0.7 0.1 stack.23.place_ref
  0.7 2.2 %shard_map.123 = bf16[512,512]{1,0:T(8,128)(2,1)S(1)} custom-call(s32[5]{0:T(128)S(1)} %stack.23.place_ref, bf16[1,288,256]{2,1,0:T(8,128)(2,1)} %bitcast.16, bf16[288,2048]{1,0:T(8,128)(2,1)} %adapter_ref.3), custom_call_target="tpu_custom_call" | custom-call | flops 150994944 | bytes 589824 | tf_op jit(solution)/shard_map/pallas_call | solution.py:77
  2.9 3.4 %collective-permute-start = (bf16[512,512]{1,0:T(8,128)(2,1)S(1)}, bf16[512,512]{1,0:T(8,128)(2,1)S(1)}, u32[]{:S(2)}, u32[]{:S(2)}) collective-permute-start(bf16[512,512]{1,0:T(8,128)(2,1)S(1)} %shard_map.123), channel_id=1, source_target_pairs={{0,1},{1,0},{2,3},{3,2},{4,7},{5,6},{6,5},{7,4},{8,9},{9,8},{10,11... | collective-permute-start | bytes 1572872 | tf_op jit(solution)/shard_map/ppermute | solution.py:663
  6.3 2.2 %shard_map.122.stay = f32[2,256,512]{2,1,0:T(8,128)S(1)} custom-call(s32[5]{0:T(128)S(1)} %stack.23.place_ref, bf16[1,288,256]{2,1,0:T(8,128)(2,1)} %bitcast.17, bf16[288,2048]{1,0:T(8,128)(2,1)} %adapter_ref.3), custom_call_target="tpu_custom_call" | custom-call | flops 150994944 | bytes 589824 | tf_op jit(solution)/shard_map/pallas_call | solution.py:77
  8.5 4.4 %collective-permute-done.arrived = bf16[512,512]{1,0:T(8,128)(2,1)S(1)} collective-permute-done((bf16[512,512]{1,0:T(8,128)(2,1)S(1)}, bf16[512,512]{1,0:T(8,128)(2,1)S(1)}, u32[]{:S(2)}, u32[]{:S(2)}) %collective-permute-start) | collective-permute-done | bytes 524320 | tf_op jit(solution)/shard_map/ppermute | solution.py:663
  12.9 0.6 collective-permute-start.1
  13.5 0.0 copy-done.1
  13.5 2.3 %collective-permute-start.4 = (bf16[256,512]{1,0:T(8,128)(2,1)S(1)}, bf16[256,512]{1,0:T(8,128)(2,1)S(1)}, u32[]{:S(2)}, u32[]{:S(2)}) collective-permute-start(bf16[256,512]{1,0:T(8,128)(2,1)S(1)} %copy-done.1), channel_id=1, source_target_pairs={{0,1},{1,0},{2,3},{3,2},{4,7},{5,6},{6,5},{7,4},{8,9},{9,8},{10,11... | collective-permute-start | bytes 786440 | tf_op jit(solution)/shard_map/ppermute | solution.py:663
  15.8 2.7 %collective-permute-done.1.last = bf16[256,512]{1,0:T(8,128)(2,1)S(1)} collective-permute-done((bf16[256,512]{1,0:T(8,128)(2,1)S(1)}, bf16[256,512]{1,0:T(8,128)(2,1)S(1)}, u32[]{:S(2)}, u32[]{:S(2)}) %collective-permute-start.1) | collective-permute-done | bytes 262176 | tf_op jit(solution)/shard_map/ppermute | solution.py:663
  18.5 0.1 shard_map.125.one.own
  18.6 4.1 %collective-permute-start.2 = (bf16[256,512]{1,0:T(8,128)(2,1)S(1)}, bf16[256,512]{1,0:T(8,128)(2,1)S(1)}, u32[]{:S(2)}, u32[]{:S(2)}) collective-permute-start(bf16[256,512]{1,0:T(8,128)(2,1)S(1)} %shard_map.125.one.own), channel_id=1, source_target_pairs={{0,1},{1,0},{2,3},{3,2},{4,7},{5,6},{6,5},{7,4},{8,9},{9,8},{10,11... | collective-permute-start | bytes 786440 | tf_op jit(solution)/shard_map/ppermute | solution.py:663
  22.7 0.0 collective-permute-done.4.two.first
  22.8 0.3 collective-permute-start.5
  23.1 3.4 %collective-permute-done.2.two.first = bf16[256,512]{1,0:T(8,128)(2,1)S(1)} collective-permute-done((bf16[256,512]{1,0:T(8,128)(2,1)S(1)}, bf16[256,512]{1,0:T(8,128)(2,1)S(1)}, u32[]{:S(2)}, u32[]{:S(2)}) %collective-permute-start.2) | collective-permute-done | bytes 262176 | tf_op jit(solution)/shard_map/ppermute | solution.py:663
  26.5 0.0 copy-start.2
  26.5 0.0 copy-start.3
  26.6 0.0 copy-start.4
  26.6 0.1 collective-permute-start.3
  26.7 3.7 %relay.1.weight = bf16[4,2048,512]{2,1,0:T(8,128)(2,1)S(1)} custom-call(bf16[2048,4,512]{2,1,0:T(4,128)(2,1)} %source.1), custom_call_target="tpu_custom_call" | custom-call | bytes 8388608 | tf_op jit(solution)/shard_map/relay/pallas_call | solution.py:431
  30.4 3.6 %collective-permute-done.5.others = bf16[512,512]{1,0:T(8,128)(2,1)S(1)} collective-permute-done((bf16[512,512]{1,0:T(8,128)(2,1)S(1)}, bf16[512,512]{1,0:T(8,128)(2,1)S(1)}, u32[]{:S(2)}, u32[]{:S(2)}) %collective-permute-start.5) | collective-permute-done | bytes 524320 | tf_op jit(solution)/shard_map/ppermute | solution.py:663
  34.0 0.0 copy-done.3
  34.0 6.1 %text_unit.1 = (bf16[256,512]{1,0:T(8,128)(2,1)}, bf16[256,512]{1,0:T(8,128)(2,1)}, f32[256,512]{1,0:T(8,128)}, bf16[32,16,128]{2,1,0:T(8,128)(2,1)S(1)}, f32[4,...) custom-call(s32[5]{0:T(128)S(1)} %stack.23.place_ref, f32[4]{0:T(128)S(1)} %copy-done.4, bf16[256,512]{1,0:T(8,128)(2,1)S(1)} %copy-done.1, ...), custom_call_target="tpu_custom_call" | custom-call | flops 2147483648 | bytes 8388608 | tf_op jit(solution)/shard_map/text_unit/pallas_call | solution.py:460
  40.1 0.0 copy-start.6
  40.1 2.1 %image_near.1 = (bf16[2,256,512]{2,1,0:T(8,128)(2,1)}, f32[2,256,512]{2,1,0:T(8,128)S(1)}, f32[256,128]{1,0:T(8,128)S(1)}, f32[256,1]{1,0:T(8,128)S(1)}) custom-call(s32[5]{0:T(128)S(1)} %stack.23.place_ref, bf16[256,512]{1,0:T(8,128)(2,1)S(1)} %shard_map.125.one.own, bf16[256,512]{1,0:T(8,128)(2,1)S(1)} %collective-permute-done.2.two.first, ...), custom_call_target="tpu_custom_call" | custom-call | flops 536870912 | bytes 2097152 | tf_op jit(solution)/shard_map/image_near/pallas_call | solution.py:487
  42.2 0.0 collective-permute-done.3.others
  42.2 0.0 copy-start.7
  42.2 2.9 %image_state.1 = (bf16[2,256,512]{2,1,0:T(8,128)(2,1)}, bf16[2,256,512]{2,1,0:T(8,128)(2,1)}, f32[256,1]{1,0:T(8,128)S(1)}, f32[256,4]{1,0:T(8,128)S(1)}, f32[4,...) custom-call(s32[5]{0:T(128)S(1)} %stack.23.place_ref, f32[4]{0:T(128)S(1)} %copy-done.4, f32[32]{0:T(128)S(1)} %copy-done.6, ...), custom_call_target="tpu_custom_call" | custom-call | flops 268435456 | bytes 1048576 | tf_op jit(solution)/shard_map/image_state/pallas_call | solution.py:509
  45.1 0.0 copy-start
  45.2 0.0 copy-start.5
  45.2 22.9 %all_to_all.10.states = bf16[32,40,128]{2,1,0:T(8,128)(2,1)S(1)} all-to-all(bf16[32,40,128]{2,1,0:T(8,128)(2,1)S(1)} %get-tuple-element.33), channel_id=1, replica_groups=mesh['seq_0'=4,'seq_1'=4,'seq_2'=2,'head'=4] {'seq_0','seq_1','seq_2'}, dimensions={0} | all-to-all | bytes 655360 | tf_op jit(solution)/shard_map/all_to_all | solution.py:724
  68.1 1.7 %state_scan.1 = bf16[32,32,128]{2,1,0:T(8,128)(2,1)} custom-call(s32[32]{0:T(128)S(1)} %copy-done.7, bf16[32,40,128]{2,1,0:T(8,128)(2,1)S(1)} %all_to_all.10.states), custom_call_target="tpu_custom_call" | custom-call | tf_op jit(solution)/shard_map/state_scan/pallas_call | solution.py:576
  69.7 3.8 %all-to-all-start.1 = ((bf16[32,32,128]{2,1,0:T(8,128)(2,1)}), bf16[32,32,128]{2,1,0:T(8,128)(2,1)S(1)}, u32[]{:S(2)}, u32[]{:S(2)}) async-start(bf16[32,32,128]{2,1,0:T(8,128)(2,1)} %state_scan.1), calls=%async_computation.1 | async-start | bytes 524288 | tf_op jit(solution)/shard_map/all_to_all | solution.py:728
  73.6 5.4 %image_attend.1 = (bf16[256,512]{1,0:T(8,128)(2,1)}, bf16[256,512]{1,0:T(8,128)(2,1)}, f32[256,512]{1,0:T(8,128)}) custom-call(s32[5]{0:T(128)S(1)} %stack.23.place_ref, f32[4]{0:T(128)S(1)} %copy-done.4, f32[32]{0:T(128)S(1)} %copy-done.6, bf16[2,256,512]{2,1,0:T(8,128)(2,1)} %get-tuple-element.37.near_ref, bf16[2,256,512]{2,1,0:T(8,128)(2,1)} %get-tuple-element.38.far_ref, ...), custom_call_target="tpu_custom_call" | custom-call | flops 1073741824 | bytes 4194304 | tf_op jit(solution)/shard_map/image_attend/pallas_call | solution.py:533
  79.0 3.5 %all-to-all-done.1.entering = bf16[32,32,128]{2,1,0:T(8,128)(2,1)S(1)} async-done(((bf16[32,32,128]{2,1,0:T(8,128)(2,1)}), bf16[32,32,128]{2,1,0:T(8,128)(2,1)S(1)}, u32[]{:S(2)}, u32[]{:S(2)}) %all-to-all-start.1) | async-done | bytes 262176 | tf_op jit(solution)/shard_map/all_to_all | solution.py:728
  82.5 3.1 %gate_leave.1 = (bf16[512,512]{1,0:T(8,128)(2,1)S(1)}, bf16[512,512]{1,0:T(8,128)(2,1)S(1)}, bf16[512,512]{1,0:T(8,128)(2,1)S(1)}) custom-call(s32[5]{0:T(128)S(1)} %stack.23.place_ref, bf16[32,32,128]{2,1,0:T(8,128)(2,1)S(1)} %all-to-all-done.1.entering, f32[4,128]{1,0:T(4,128)S(1)} %copy-done.5, bf16[512,2048]{1,0:T(8,128)(2,1)S(1)} %copy-done, ...), custom_call_target="tpu_custom_call" | custom-call | tf_op jit(solution)/shard_map/gate_leave/pallas_call | solution.py:623
  85.5 0.5 collective-permute-start.8
  86.0 2.3 %collective-permute-start.6 = (bf16[512,512]{1,0:T(8,128)(2,1)S(1)}, bf16[512,512]{1,0:T(8,128)(2,1)S(1)}, u32[]{:S(2)}, u32[]{:S(2)}) collective-permute-start(bf16[512,512]{1,0:T(8,128)(2,1)S(1)} %get-tuple-element.49), channel_id=1, source_target_pairs={{0,1},{1,0},{2,3},{3,2},{4,7},{5,6},{6,5},{7,4},{8,9},{9,8},{10,11... | collective-permute-start | bytes 1572872 | tf_op jit(solution)/shard_map/ppermute | solution.py:663
  88.3 1.3 %stay_blocks.1 = (f32[256,512]{1,0:T(8,128)S(1)}, f32[256,512]{1,0:T(8,128)S(1)}, f32[256,512]{1,0:T(8,128)S(1)}, f32[256,512]{1,0:T(8,128)S(1)}) custom-call(s32[5]{0:T(128)S(1)} %stack.23.place_ref, bf16[512,512]{1,0:T(8,128)(2,1)S(1)} %get-tuple-element.47.gated, bf16[512,2048]{1,0:T(8,128)(2,1)S(1)} %copy-done), custom_call_target="tpu_custom_call" | custom-call | flops 536870912 | bytes 1048576 | tf_op jit(solution)/shard_map/stay_blocks/pallas_call | solution.py:646
  89.5 5.3 %collective-permute-done.8 = bf16[512,512]{1,0:T(8,128)(2,1)S(1)} collective-permute-done((bf16[512,512]{1,0:T(8,128)(2,1)S(1)}, bf16[512,512]{1,0:T(8,128)(2,1)S(1)}, u32[]{:S(2)}, u32[]{:S(2)}) %collective-permute-start.8) | collective-permute-done | bytes 524320 | tf_op jit(solution)/shard_map/ppermute | solution.py:663
  94.9 0.1 add_convert_fusion.1
  94.9 0.1 collective-permute-start.9
  95.0 7.0 %collective-permute-done.6 = bf16[512,512]{1,0:T(8,128)(2,1)S(1)} collective-permute-done((bf16[512,512]{1,0:T(8,128)(2,1)S(1)}, bf16[512,512]{1,0:T(8,128)(2,1)S(1)}, u32[]{:S(2)}, u32[]{:S(2)}) %collective-permute-start.6) | collective-permute-done | bytes 524320 | tf_op jit(solution)/shard_map/ppermute | solution.py:663
  102.0 0.1 add_convert_fusion.3
  102.1 0.1 collective-permute-start.7
  102.2 0.8 collective-permute-done.9
  103.0 0.9 add_convert_fusion
  103.9 3.8 %collective-permute-done.7 = bf16[256,512]{1,0:T(8,128)(2,1)S(1)} collective-permute-done((bf16[256,512]{1,0:T(8,128)(2,1)S(1)}, bf16[256,512]{1,0:T(8,128)(2,1)S(1)}, u32[]{:S(2)}, u32[]{:S(2)}) %collective-permute-start.7) | collective-permute-done | bytes 262176 | tf_op jit(solution)/shard_map/ppermute | solution.py:663
  107.7 0.9 fusion
  (10 shorter events, 0.1 us)
Async XLA Ops:
  0.6 12.9 %copy-start.1 = (bf16[256,512]{1,0:T(8,128)(2,1)S(1)}, bf16[256,512]{1,0:T(8,128)(2,1)}, u32[]{:S(2)}) copy-start(bf16[256,512]{1,0:T(8,128)(2,1)} %own.1) | copy-start | bytes 786436
  2.9 9.9 %collective-permute-start = (bf16[512,512]{1,0:T(8,128)(2,1)S(1)}, bf16[512,512]{1,0:T(8,128)(2,1)S(1)}, u32[]{:S(2)}, u32[]{:S(2)}) collective-permute-start(bf16[512,512]{1,0:T(8,128)(2,1)S(1)} %shard_map.123), channel_id=1, source_target_pairs={{0,1},{1,0},{2,3},{3,2},{4,7},{5,6},{6,5},{7,4},{8,9},{9,8},{10,11... | collective-permute-start | bytes 1572872 | tf_op jit(solution)/shard_map/ppermute | solution.py:663
  12.9 5.6 %collective-permute-start.1 = (bf16[256,512]{1,0:T(8,128)(2,1)S(1)}, bf16[256,512]{1,0:T(8,128)(2,1)S(1)}, u32[]{:S(2)}, u32[]{:S(2)}) collective-permute-start(bf16[256,512]{1,0:T(8,128)(2,1)S(1)} %shard_map.124), channel_id=1, source_target_pairs={{0,3},{1,2},{2,1},{3,0},{4,5},{5,4},{6,7},{7,6},{8,11},{9,10},{10,... | collective-permute-start | bytes 786440 | tf_op jit(solution)/shard_map/ppermute | solution.py:663
  13.5 9.2 %collective-permute-start.4 = (bf16[256,512]{1,0:T(8,128)(2,1)S(1)}, bf16[256,512]{1,0:T(8,128)(2,1)S(1)}, u32[]{:S(2)}, u32[]{:S(2)}) collective-permute-start(bf16[256,512]{1,0:T(8,128)(2,1)S(1)} %copy-done.1), channel_id=1, source_target_pairs={{0,1},{1,0},{2,3},{3,2},{4,7},{5,6},{6,5},{7,4},{8,9},{9,8},{10,11... | collective-permute-start | bytes 786440 | tf_op jit(solution)/shard_map/ppermute | solution.py:663
  18.6 7.9 %collective-permute-start.2 = (bf16[256,512]{1,0:T(8,128)(2,1)S(1)}, bf16[256,512]{1,0:T(8,128)(2,1)S(1)}, u32[]{:S(2)}, u32[]{:S(2)}) collective-permute-start(bf16[256,512]{1,0:T(8,128)(2,1)S(1)} %shard_map.125.one.own), channel_id=1, source_target_pairs={{0,1},{1,0},{2,3},{3,2},{4,7},{5,6},{6,5},{7,4},{8,9},{9,8},{10,11... | collective-permute-start | bytes 786440 | tf_op jit(solution)/shard_map/ppermute | solution.py:663
  22.8 11.2 %collective-permute-start.5 = (bf16[512,512]{1,0:T(8,128)(2,1)S(1)}, bf16[512,512]{1,0:T(8,128)(2,1)S(1)}, u32[]{:S(2)}, u32[]{:S(2)}) collective-permute-start(bf16[512,512]{1,0:T(8,128)(2,1)S(1)} %shard_map.127), channel_id=1, source_target_pairs={{0,3},{1,2},{2,1},{3,0},{4,5},{5,4},{6,7},{7,6},{8,11},{9,10},{10,... | collective-permute-start | bytes 1572872 | tf_op jit(solution)/shard_map/ppermute | solution.py:663
  26.5 7.5 %copy-start.2 = (bf16[2048,4]{0,1:T(4,128)(2,1)S(1)}, bf16[2048,4]{0,1:T(4,128)(2,1)}, u32[]{:S(2)}) copy-start(bf16[2048,4]{0,1:T(4,128)(2,1)} %param.18) | copy-start | bytes 49156
  26.5 7.4 %copy-start.3 = (f32[2048]{0:T(1024)S(1)}, f32[2048]{0:T(1024)}, u32[]{:S(2)}) copy-start(f32[2048]{0:T(1024)} %param.16) | copy-start | bytes 24580
  26.6 7.4 %copy-start.4 = (f32[4]{0:T(128)S(1)}, f32[4]{0:T(128)}, u32[]{:S(2)}) copy-start(f32[4]{0:T(128)} %ceiling_ref.5) | copy-start | bytes 52
  26.6 15.6 %collective-permute-start.3 = (bf16[512,512]{1,0:T(8,128)(2,1)S(1)}, bf16[512,512]{1,0:T(8,128)(2,1)S(1)}, u32[]{:S(2)}, u32[]{:S(2)}) collective-permute-start(bf16[512,512]{1,0:T(8,128)(2,1)S(1)} %shard_map.126), channel_id=1, source_target_pairs={{0,3},{1,2},{2,1},{3,0},{4,5},{5,4},{6,7},{7,6},{8,11},{9,10},{10,... | collective-permute-start | bytes 1572872 | tf_op jit(solution)/shard_map/ppermute | solution.py:663
  40.1 2.1 %copy-start.6 = (f32[32]{0:T(128)S(1)}, f32[32]{0:T(128)}, u32[]{:S(2)}) copy-start(f32[32]{0:T(128)} %forget_ref.3) | copy-start | bytes 388
  42.2 25.9 %copy-start.7 = (s32[32]{0:T(128)S(1)}, s32[32]{0:T(128)}, u32[]{:S(2)}) copy-start(s32[32]{0:T(128)} %start_ref.1) | copy-start | bytes 388
  45.1 37.3 %copy-start = (bf16[512,2048]{1,0:T(8,128)(2,1)S(1)}, bf16[512,2048]{1,0:T(8,128)(2,1)}, u32[]{:S(2)}) copy-start(bf16[512,2048]{1,0:T(8,128)(2,1)} %out_proj.3) | copy-start | bytes 6291460
  45.2 37.3 %copy-start.5 = (f32[4,128]{1,0:T(4,128)S(1)}, f32[4,128]{1,0:T(4,128)}, u32[]{:S(2)}) copy-start(f32[4,128]{1,0:T(4,128)} %out_gain.1) | copy-start | bytes 6148
  69.7 12.7 %all-to-all-start.1 = ((bf16[32,32,128]{2,1,0:T(8,128)(2,1)}), bf16[32,32,128]{2,1,0:T(8,128)(2,1)S(1)}, u32[]{:S(2)}, u32[]{:S(2)}) async-start(bf16[32,32,128]{2,1,0:T(8,128)(2,1)} %state_scan.1), calls=%async_computation.1 | async-start | bytes 524288 | tf_op jit(solution)/shard_map/all_to_all | solution.py:728
  85.5 9.3 %collective-permute-start.8 = (bf16[512,512]{1,0:T(8,128)(2,1)S(1)}, bf16[512,512]{1,0:T(8,128)(2,1)S(1)}, u32[]{:S(2)}, u32[]{:S(2)}) collective-permute-start(bf16[512,512]{1,0:T(8,128)(2,1)S(1)} %get-tuple-element.52), channel_id=1, source_target_pairs={{0,1},{1,0},{2,3},{3,2},{4,7},{5,6},{6,5},{7,4},{8,9},{9,8},{10,11... | collective-permute-start | bytes 1572872 | tf_op jit(solution)/shard_map/ppermute | solution.py:663
  86.0 16.0 %collective-permute-start.6 = (bf16[512,512]{1,0:T(8,128)(2,1)S(1)}, bf16[512,512]{1,0:T(8,128)(2,1)S(1)}, u32[]{:S(2)}, u32[]{:S(2)}) collective-permute-start(bf16[512,512]{1,0:T(8,128)(2,1)S(1)} %get-tuple-element.49), channel_id=1, source_target_pairs={{0,1},{1,0},{2,3},{3,2},{4,7},{5,6},{6,5},{7,4},{8,9},{9,8},{10,11... | collective-permute-start | bytes 1572872 | tf_op jit(solution)/shard_map/ppermute | solution.py:663
  94.9 8.1 %collective-permute-start.9 = (bf16[256,512]{1,0:T(8,128)(2,1)S(1)}, bf16[256,512]{1,0:T(8,128)(2,1)S(1)}, u32[]{:S(2)}, u32[]{:S(2)}) collective-permute-start(bf16[256,512]{1,0:T(8,128)(2,1)S(1)} %add_convert_fusion.1), channel_id=1, source_target_pairs={{0,3},{1,2},{2,1},{3,0},{4,5},{5,4},{6,7},{7,6},{8,11},{9,10},{10,... | collective-permute-start | bytes 786440 | tf_op jit(solution)/shard_map/ppermute | solution.py:663
  102.1 5.6 %collective-permute-start.7 = (bf16[256,512]{1,0:T(8,128)(2,1)S(1)}, bf16[256,512]{1,0:T(8,128)(2,1)S(1)}, u32[]{:S(2)}, u32[]{:S(2)}) collective-permute-start(bf16[256,512]{1,0:T(8,128)(2,1)S(1)} %add_convert_fusion.3), channel_id=1, source_target_pairs={{0,3},{1,2},{2,1},{3,0},{4,5},{5,4},{6,7},{7,6},{8,11},{9,10},{10,... | collective-permute-start | bytes 786440 | tf_op jit(solution)/shard_map/ppermute | solution.py:663

commit v6 on v5

--- a/solution.py
+++ b/solution.py
@@ -42,6 +42,10 @@
 
 def columns_of(place_ref, slot, width):
     return pl.ds(pl.multiple_of(place_ref[slot] * width, width), width)
+
+
+def ring_columns(place_ref, step, width):
+    return pl.ds(pl.multiple_of(lax.rem(place_ref[0] + step, 4) * width, width), width)
 
 
 def adapter_blocks(place_ref, patches_ref, adapter_ref, patches, blocks, sems, slots):
@@ -588,14 +592,14 @@
 
 
 def gate_kernel(place_ref, entering, out_gain, out_proj, *refs):
-    sources, (leave_t, leave_i, gated), buffers, sems = refs[:6], refs[6:9], refs[9:15], refs[15]
+    sources, (far_text, far_image, gated), buffers, sems = refs[:6], refs[6:9], refs[9:15], refs[15]
     copies = [
         pltpu.make_async_copy(source, buffer, sems.at[at])
         for at, (source, buffer) in enumerate(zip(sources, buffers))
     ]
     for copy in copies:
         copy.start()
-    rows, width = leave_t.shape[0] // 2, leave_t.shape[1]
+    rows, width = far_text.shape
     for kind in range(2):
         for copy in copies[3 * kind : 3 * kind + 3]:
             copy.wait()
@@ -609,16 +613,15 @@
             scale = lax.rsqrt(jnp.mean(attended * attended, axis=-1, keepdims=True) + EPSILON)
             value = attended * scale * out_gain[head : head + 1, :] * gate[:, lanes].astype(F32)
             gated[kind * rows : (kind + 1) * rows, lanes] = value.astype(BF16)
-    for at, slot in enumerate((1, 3)):
-        weight = out_proj[:, columns_of(place_ref, slot, width)]
-        block = jnp.dot(gated[...], weight, preferred_element_type=F32).astype(BF16)
-        leave_t[at * rows : (at + 1) * rows] = block[:rows]
-        leave_i[at * rows : (at + 1) * rows] = block[rows:]
+    weight = out_proj[:, ring_columns(place_ref, 2, width)]
+    block = jnp.dot(gated[...], weight, preferred_element_type=F32).astype(BF16)
+    far_text[...] = block[:rows]
+    far_image[...] = block[rows:]
 
 
 def gate_call(place, entering, out_gain, out_proj, text_parts, image_parts):
     rows, width = text_parts[0].shape
-    outs = (shape_of(2 * rows, width),) * 3
+    outs = (shape_of(rows, width), shape_of(rows, width), shape_of(2 * rows, width))
     parts = in_hbm(*text_parts, *image_parts)
     return pl.pallas_call(
         gate_kernel,
@@ -628,29 +631,30 @@
         scratch_shapes=[pltpu.VMEM(p.shape, p.dtype) for p in parts]
         + [pltpu.SemaphoreType.DMA((6,))],
         compiler_params=limit(16),
-        name="gate_leave",
+        name="gate_far",
     )(place, entering, out_gain, out_proj, *parts)
 
 
-def stay_blocks_kernel(place_ref, gated, out_proj, pass_t, pass_i, own_t, own_i):
-    rows, width = own_t.shape
-    for slot, text, image in ((2, pass_t, pass_i), (0, own_t, own_i)):
-        weight = out_proj[:, columns_of(place_ref, slot, width)]
+def near_kernel(place_ref, gated, out_proj, next_t, next_i, last_t, last_i, own_t, own_i):
+    rows, width = next_t.shape
+    for step, text, image in ((1, next_t, next_i), (3, last_t, last_i), (0, own_t, own_i)):
+        weight = out_proj[:, ring_columns(place_ref, step, width)]
         block = jnp.dot(gated[...], weight, preferred_element_type=F32)
-        text[...] = block[:rows]
-        image[...] = block[rows:]
-
-
-def stay_call(place, gated, out_proj):
+        text[...] = block[:rows].astype(text.dtype)
+        image[...] = block[rows:].astype(image.dtype)
+
+
+def near_call(place, gated, out_proj):
     rows, width = gated.shape[0] // 2, gated.shape[1]
-    return pl.pallas_call(
-        stay_blocks_kernel,
-        out_shape=(shape_of(rows, width, dtype=F32),) * 4,
+    outs = (shape_of(rows, width),) * 4 + (shape_of(rows, width, dtype=F32),) * 2
+    return pl.pallas_call(
+        near_kernel,
+        out_shape=outs,
         in_specs=[SMEM, VMEM, VMEM],
-        out_specs=(VMEM,) * 4,
+        out_specs=(VMEM,) * 6,
         compiler_params=limit(16),
-        cost_estimate=cost_of(2 * rows, width, 2 * width),
-        name="stay_blocks",
+        cost_estimate=cost_of(2 * rows, width, 3 * width),
+        name="near_blocks",
     )(place, gated, out_proj)
 
 
@@ -661,6 +665,10 @@
             partner = x ^ 1 if (core + turn) % 2 == 0 else 3 - x
             pairs.append((4 * core + x, 4 * core + partner))
     return lax.ppermute(array, ("seq_2", "head"), pairs)
+
+
+def passed(array, step):
+    return lax.ppermute(array, "head", [(i, (i + step) % 4) for i in range(4)])
 
 
 def gathered(rows):
@@ -727,17 +735,18 @@
     )
     entering = lax.all_to_all(scan_call(image_start, slices), SEQ, 0, 0, tiled=True)
 
-    leave_t, leave_i, gated = gate_call(
+    far_t, far_i, gated = gate_call(
         place, entering, out_gain, out_proj, text_parts, image_parts
     )
-    pass_t, pass_i, own_t, own_i = stay_call(place, gated, out_proj)
-    rows = own_t.shape[0]
-    arrived_t = moved(leave_t, 0)
-    arrived_i = moved(leave_i, 0)
-    last_t = moved(added(pass_t, arrived_t[rows:]), 1)
-    last_i = moved(added(pass_i, arrived_i[rows:]), 1)
-    text_out = text_embed.astype(F32) + (own_t + arrived_t[:rows].astype(F32) + last_t.astype(F32))
-    image_out = embed.astype(F32) + (own_i + arrived_i[:rows].astype(F32) + last_i.astype(F32))
+    next_t, next_i, last_t, last_i, own_t, own_i = near_call(place, gated, out_proj)
+    far_from_left = passed(far_t, 1)
+    far_from_right = passed(far_i, 3)
+    left_i = passed(next_i, 1)
+    right_t = passed(last_t, 3)
+    left_t = passed(added(next_t, far_from_left), 1)
+    right_i = passed(added(last_i, far_from_right), 3)
+    text_out = text_embed.astype(F32) + (own_t + left_t.astype(F32) + right_t.astype(F32))
+    image_out = embed.astype(F32) + (own_i + left_i.astype(F32) + right_i.astype(F32))
     return (image_out.astype(BF16)[None], text_out.astype(BF16))
 
 

time: 111 us -> 108 us (0.973)
  waiting for transfers between devices: 34.5 us -> 30.5 us
  starting transfers between devices: 17.5 us -> 19.4 us
    ppermute x10 -> x6, waiting for transfers between devices: 31 us -> 14.1 us  [moved(): return lax.ppermute(array, ('seq_2', 'head'), pairs)]
    ppermute x0 -> x6, waiting for transfers between devices: none -> 13 us  [passed(): return lax.ppermute(array, 'head', [(i, (i + step) % 4) for i in range(4)])]
    ppermute x0 -> x6, starting transfers between devices: none -> 4.82 us  [passed(): return lax.ppermute(array, 'head', [(i, (i + step) % 4) for i in range(4)])]
    ppermute x10 -> x6, starting transfers between devices: 13.7 us -> 10.8 us  [moved(): return lax.ppermute(array, ('seq_2', 'head'), pairs)]
  transfers between devices with their start and end apart: 11 -> 13, of which waited for: 9 -> 8; matrix products, arithmetic and copies ran while one was open for 1% -> 1% of each run, Pallas kernels for 19% -> 20%
where the time goes in v6:
time: 108 us; the launch traced here: 106 us
  Pallas kernels  30.8 us (29%)
  waiting for transfers between devices  30.5 us (28%)
  blocking collectives  22.9 us (21%)
  starting transfers between devices  19.4 us (18%)
  other arithmetic  1.84 us (2%)
    all_to_all x1, blocking collectives, steps(): slices = lax.all_to_all(states, SEQ, 0, 0, tiled=True)  22.9 us
    ppermute x6, waiting for transfers between devices, moved(): return lax.ppermute(array, ('seq_2', 'head'), pairs)  14.1 us
    ppermute x6, waiting for transfers between devices, passed(): return lax.ppermute(array, 'head', [(i, (i + step) % 4) for i in range(4)])  13 us
    ppermute x6, starting transfers between devices, moved(): return lax.ppermute(array, ('seq_2', 'head'), pairs)  10.8 us
    pallas_call x1, Pallas kernels, text_call(): pl.pallas_call(text_kernel, grid=(1,), out_shape=outs, in_specs=[SMEM, SM...  6.06 us
    pallas_call x1, Pallas kernels, image_attend_call(): pl.pallas_call(image_attend_kernel, grid=(1,), out_shape=outs, in_specs=[...  5.41 us
    ppermute x6, starting transfers between devices, passed(): return lax.ppermute(array, 'head', [(i, (i + step) % 4) for i in range(4)])  4.82 us
    pallas_call x2, Pallas kernels, adapter_call(): pl.pallas_call(kernel, out_shape=outs, in_specs=[SMEM, HBM, HBM], out_spe...  4.39 us
  transfers between devices with their start and end apart: 13, of which 8 were waited for; matrix products, arithmetic and copies ran while one was open for 1% of the time, Pallas kernels for 20%

profile of v6, /device:TPU:1, one launch (start us, length us, event | category | flops | bytes accessed | tf_op | source)
XLA Modules:
  0.0 106.5 jit_solution(14495751243859011417)
XLA Ops:
  0.7 0.1 stack.23.place_ref
  0.7 2.2 %shard_map.123 = bf16[512,512]{1,0:T(8,128)(2,1)S(1)} custom-call(s32[5]{0:T(128)S(1)} %stack.23.place_ref, bf16[1,288,256]{2,1,0:T(8,128)(2,1)} %bitcast.16, bf16[288,2048]{1,0:T(8,128)(2,1)} %adapter_ref.3), custom_call_target="tpu_custom_call" | custom-call | flops 150994944 | bytes 589824 | tf_op jit(solution)/shard_map/pallas_call | solution.py:81
  2.9 3.4 %collective-permute-start = (bf16[512,512]{1,0:T(8,128)(2,1)S(1)}, bf16[512,512]{1,0:T(8,128)(2,1)S(1)}, u32[]{:S(2)}, u32[]{:S(2)}) collective-permute-start(bf16[512,512]{1,0:T(8,128)(2,1)S(1)} %shard_map.123), channel_id=1, source_target_pairs={{0,1},{1,0},{2,3},{3,2},{4,7},{5,6},{6,5},{7,4},{8,9},{9,8},{10,11... | collective-permute-start | bytes 1572872 | tf_op jit(solution)/shard_map/ppermute | solution.py:667
  6.3 2.2 %shard_map.122.stay = f32[2,256,512]{2,1,0:T(8,128)S(1)} custom-call(s32[5]{0:T(128)S(1)} %stack.23.place_ref, bf16[1,288,256]{2,1,0:T(8,128)(2,1)} %bitcast.17, bf16[288,2048]{1,0:T(8,128)(2,1)} %adapter_ref.3), custom_call_target="tpu_custom_call" | custom-call | flops 150994944 | bytes 589824 | tf_op jit(solution)/shard_map/pallas_call | solution.py:81
  8.5 4.4 %collective-permute-done.arrived = bf16[512,512]{1,0:T(8,128)(2,1)S(1)} collective-permute-done((bf16[512,512]{1,0:T(8,128)(2,1)S(1)}, bf16[512,512]{1,0:T(8,128)(2,1)S(1)}, u32[]{:S(2)}, u32[]{:S(2)}) %collective-permute-start) | collective-permute-done | bytes 524320 | tf_op jit(solution)/shard_map/ppermute | solution.py:667
  12.9 0.6 collective-permute-start.1
  13.5 2.3 %collective-permute-start.4 = (bf16[256,512]{1,0:T(8,128)(2,1)S(1)}, bf16[256,512]{1,0:T(8,128)(2,1)S(1)}, u32[]{:S(2)}, u32[]{:S(2)}) collective-permute-start(bf16[256,512]{1,0:T(8,128)(2,1)S(1)} %copy-done), channel_id=1, source_target_pairs={{0,1},{1,0},{2,3},{3,2},{4,7},{5,6},{6,5},{7,4},{8,9},{9,8},{10,11... | collective-permute-start | bytes 786440 | tf_op jit(solution)/shard_map/ppermute | solution.py:667
  15.8 2.7 %collective-permute-done.1.last = bf16[256,512]{1,0:T(8,128)(2,1)S(1)} collective-permute-done((bf16[256,512]{1,0:T(8,128)(2,1)S(1)}, bf16[256,512]{1,0:T(8,128)(2,1)S(1)}, u32[]{:S(2)}, u32[]{:S(2)}) %collective-permute-start.1) | collective-permute-done | bytes 262176 | tf_op jit(solution)/shard_map/ppermute | solution.py:667
  18.5 0.1 shard_map.125.one.own
  18.6 4.1 %collective-permute-start.2 = (bf16[256,512]{1,0:T(8,128)(2,1)S(1)}, bf16[256,512]{1,0:T(8,128)(2,1)S(1)}, u32[]{:S(2)}, u32[]{:S(2)}) collective-permute-start(bf16[256,512]{1,0:T(8,128)(2,1)S(1)} %shard_map.125.one.own), channel_id=1, source_target_pairs={{0,1},{1,0},{2,3},{3,2},{4,7},{5,6},{6,5},{7,4},{8,9},{9,8},{10,11... | collective-permute-start | bytes 786440 | tf_op jit(solution)/shard_map/ppermute | solution.py:667
  22.7 0.0 collective-permute-done.4.two.first
  22.8 0.3 collective-permute-start.5
  23.1 3.4 %collective-permute-done.2.two.first = bf16[256,512]{1,0:T(8,128)(2,1)S(1)} collective-permute-done((bf16[256,512]{1,0:T(8,128)(2,1)S(1)}, bf16[256,512]{1,0:T(8,128)(2,1)S(1)}, u32[]{:S(2)}, u32[]{:S(2)}) %collective-permute-start.2) | collective-permute-done | bytes 262176 | tf_op jit(solution)/shard_map/ppermute | solution.py:667
  26.5 0.0 copy-start.2
  26.5 0.0 copy-start.3
  26.6 0.0 copy-start.4
  26.6 0.1 collective-permute-start.3
  26.7 3.7 %relay.1.weight = bf16[4,2048,512]{2,1,0:T(8,128)(2,1)S(1)} custom-call(bf16[2048,4,512]{2,1,0:T(4,128)(2,1)} %source.1), custom_call_target="tpu_custom_call" | custom-call | bytes 8388608 | tf_op jit(solution)/shard_map/relay/pallas_call | solution.py:435
  30.4 3.6 %collective-permute-done.5.others = bf16[512,512]{1,0:T(8,128)(2,1)S(1)} collective-permute-done((bf16[512,512]{1,0:T(8,128)(2,1)S(1)}, bf16[512,512]{1,0:T(8,128)(2,1)S(1)}, u32[]{:S(2)}, u32[]{:S(2)}) %collective-permute-start.5) | collective-permute-done | bytes 524320 | tf_op jit(solution)/shard_map/ppermute | solution.py:667
  34.0 6.1 %text_unit.1 = (bf16[256,512]{1,0:T(8,128)(2,1)}, bf16[256,512]{1,0:T(8,128)(2,1)}, f32[256,512]{1,0:T(8,128)}, bf16[32,16,128]{2,1,0:T(8,128)(2,1)S(1)}, f32[4,...) custom-call(s32[5]{0:T(128)S(1)} %stack.23.place_ref, f32[4]{0:T(128)S(1)} %copy-done.4, bf16[256,512]{1,0:T(8,128)(2,1)S(1)} %copy-done, ...), custom_call_target="tpu_custom_call" | custom-call | flops 2147483648 | bytes 8388608 | tf_op jit(solution)/shard_map/text_unit/pallas_call | solution.py:464
  40.1 0.0 copy-start.6
  40.1 2.1 %image_near.1 = (bf16[2,256,512]{2,1,0:T(8,128)(2,1)}, f32[2,256,512]{2,1,0:T(8,128)S(1)}, f32[256,128]{1,0:T(8,128)S(1)}, f32[256,1]{1,0:T(8,128)S(1)}) custom-call(s32[5]{0:T(128)S(1)} %stack.23.place_ref, bf16[256,512]{1,0:T(8,128)(2,1)S(1)} %shard_map.125.one.own, bf16[256,512]{1,0:T(8,128)(2,1)S(1)} %collective-permute-done.2.two.first, ...), custom_call_target="tpu_custom_call" | custom-call | flops 536870912 | bytes 2097152 | tf_op jit(solution)/shard_map/image_near/pallas_call | solution.py:491
  42.2 0.0 collective-permute-done.3.others
  42.2 0.0 copy-start.7
  42.2 2.9 %image_state.1 = (bf16[2,256,512]{2,1,0:T(8,128)(2,1)}, bf16[2,256,512]{2,1,0:T(8,128)(2,1)}, f32[256,1]{1,0:T(8,128)S(1)}, f32[256,4]{1,0:T(8,128)S(1)}, f32[4,...) custom-call(s32[5]{0:T(128)S(1)} %stack.23.place_ref, f32[4]{0:T(128)S(1)} %copy-done.4, f32[32]{0:T(128)S(1)} %copy-done.6, ...), custom_call_target="tpu_custom_call" | custom-call | flops 268435456 | bytes 1048576 | tf_op jit(solution)/shard_map/image_state/pallas_call | solution.py:513
  45.1 0.0 copy-start.1
  45.2 0.0 copy-start.5
  45.2 22.9 %all_to_all.10.states = bf16[32,40,128]{2,1,0:T(8,128)(2,1)S(1)} all-to-all(bf16[32,40,128]{2,1,0:T(8,128)(2,1)S(1)} %get-tuple-element.35), channel_id=1, replica_groups=mesh['seq_0'=4,'seq_1'=4,'seq_2'=2,'head'=4] {'seq_0','seq_1','seq_2'}, dimensions={0} | all-to-all | bytes 655360 | tf_op jit(solution)/shard_map/all_to_all | solution.py:732
  68.1 1.7 %state_scan.1 = bf16[32,32,128]{2,1,0:T(8,128)(2,1)} custom-call(s32[32]{0:T(128)S(1)} %copy-done.7, bf16[32,40,128]{2,1,0:T(8,128)(2,1)S(1)} %all_to_all.10.states), custom_call_target="tpu_custom_call" | custom-call | tf_op jit(solution)/shard_map/state_scan/pallas_call | solution.py:580
  69.8 3.8 %all-to-all-start.1 = ((bf16[32,32,128]{2,1,0:T(8,128)(2,1)}), bf16[32,32,128]{2,1,0:T(8,128)(2,1)S(1)}, u32[]{:S(2)}, u32[]{:S(2)}) async-start(bf16[32,32,128]{2,1,0:T(8,128)(2,1)} %state_scan.1), calls=%async_computation.1 | async-start | bytes 524288 | tf_op jit(solution)/shard_map/all_to_all | solution.py:736
  73.6 5.4 %image_attend.1 = (bf16[256,512]{1,0:T(8,128)(2,1)}, bf16[256,512]{1,0:T(8,128)(2,1)}, f32[256,512]{1,0:T(8,128)}) custom-call(s32[5]{0:T(128)S(1)} %stack.23.place_ref, f32[4]{0:T(128)S(1)} %copy-done.4, f32[32]{0:T(128)S(1)} %copy-done.6, bf16[2,256,512]{2,1,0:T(8,128)(2,1)} %get-tuple-element.39.near_ref, bf16[2,256,512]{2,1,0:T(8,128)(2,1)} %get-tuple-element.40.far_ref, ...), custom_call_target="tpu_custom_call" | custom-call | flops 1073741824 | bytes 4194304 | tf_op jit(solution)/shard_map/image_attend/pallas_call | solution.py:537
  79.0 3.5 %all-to-all-done.1.entering = bf16[32,32,128]{2,1,0:T(8,128)(2,1)S(1)} async-done(((bf16[32,32,128]{2,1,0:T(8,128)(2,1)}), bf16[32,32,128]{2,1,0:T(8,128)(2,1)S(1)}, u32[]{:S(2)}, u32[]{:S(2)}) %all-to-all-start.1) | async-done | bytes 262176 | tf_op jit(solution)/shard_map/all_to_all | solution.py:736
  82.5 2.8 %gate_far.1 = (bf16[256,512]{1,0:T(8,128)(2,1)S(1)}, bf16[256,512]{1,0:T(8,128)(2,1)S(1)}, bf16[512,512]{1,0:T(8,128)(2,1)S(1)}) custom-call(s32[5]{0:T(128)S(1)} %stack.23.place_ref, bf16[32,32,128]{2,1,0:T(8,128)(2,1)S(1)} %all-to-all-done.1.entering, f32[4,128]{1,0:T(4,128)S(1)} %copy-done.5, bf16[512,2048]{1,0:T(8,128)(2,1)S(1)} %copy-done.1, ...), custom_call_target="tpu_custom_call" | custom-call | tf_op jit(solution)/shard_map/gate_far/pallas_call | solution.py:626
  85.3 0.5 collective-permute-start.7
  85.8 1.1 collective-permute-start.9
  86.8 1.5 %near_blocks.1 = (bf16[256,512]{1,0:T(8,128)(2,1)S(1)}, bf16[256,512]{1,0:T(8,128)(2,1)S(1)}, bf16[256,512]{1,0:T(8,128)(2,1)S(1)}, bf16[256,512]{1,0:T(8,128)(2...) custom-call(s32[5]{0:T(128)S(1)} %stack.23.place_ref, bf16[512,512]{1,0:T(8,128)(2,1)S(1)} %get-tuple-element.49.gated, ...), custom_call_target="tpu_custom_call" | custom-call | flops 805306368 | bytes 1572864 | tf_op jit(solution)/shard_map/near_blocks/pallas_call | solution.py:650
  88.3 0.1 collective-permute-start.6
  88.4 4.6 %collective-permute-done.7 = bf16[256,512]{1,0:T(8,128)(2,1)S(1)} collective-permute-done((bf16[256,512]{1,0:T(8,128)(2,1)S(1)}, bf16[256,512]{1,0:T(8,128)(2,1)S(1)}, u32[]{:S(2)}, u32[]{:S(2)}) %collective-permute-start.7) | collective-permute-done | bytes 262176 | tf_op jit(solution)/shard_map/ppermute | solution.py:671
  93.0 0.1 add_convert_fusion.3
  93.1 1.7 %collective-permute-start.8 = (bf16[256,512]{1,0:T(8,128)(2,1)S(1)}, bf16[256,512]{1,0:T(8,128)(2,1)S(1)}, u32[]{:S(2)}, u32[]{:S(2)}) collective-permute-start(bf16[256,512]{1,0:T(8,128)(2,1)S(1)} %add_convert_fusion.3), channel_id=1, source_target_pairs={{0,3},{1,0},{2,1},{3,2},{4,7},{5,4},{6,5},{7,6},{8,11},{9,8},{10,9... | collective-permute-start | bytes 786440 | tf_op jit(solution)/shard_map/ppermute | solution.py:671
  94.8 0.1 collective-permute-start.11
  94.9 0.1 add_convert_fusion.1
  94.9 1.5 %collective-permute-start.10 = (bf16[256,512]{1,0:T(8,128)(2,1)S(1)}, bf16[256,512]{1,0:T(8,128)(2,1)S(1)}, u32[]{:S(2)}, u32[]{:S(2)}) collective-permute-start(bf16[256,512]{1,0:T(8,128)(2,1)S(1)} %add_convert_fusion.1), channel_id=1, source_target_pairs={{0,1},{1,2},{2,3},{3,0},{4,5},{5,6},{6,7},{7,4},{8,9},{9,10},{10,1... | collective-permute-start | bytes 786440 | tf_op jit(solution)/shard_map/ppermute | solution.py:671
  96.4 3.6 %collective-permute-done.6 = bf16[256,512]{1,0:T(8,128)(2,1)S(1)} collective-permute-done((bf16[256,512]{1,0:T(8,128)(2,1)S(1)}, bf16[256,512]{1,0:T(8,128)(2,1)S(1)}, u32[]{:S(2)}, u32[]{:S(2)}) %collective-permute-start.6) | collective-permute-done | bytes 262176 | tf_op jit(solution)/shard_map/ppermute | solution.py:671
  100.0 0.0 collective-permute-done.8
  100.0 0.9 fusion
  100.8 4.8 %collective-permute-done.11 = bf16[256,512]{1,0:T(8,128)(2,1)S(1)} collective-permute-done((bf16[256,512]{1,0:T(8,128)(2,1)S(1)}, bf16[256,512]{1,0:T(8,128)(2,1)S(1)}, u32[]{:S(2)}, u32[]{:S(2)}) %collective-permute-start.11) | collective-permute-done | bytes 262176 | tf_op jit(solution)/shard_map/ppermute | solution.py:671
  105.6 0.9 add_convert_fusion
  (14 shorter events, 0.1 us)
Async XLA Ops:
  0.6 12.9 %copy-start = (bf16[256,512]{1,0:T(8,128)(2,1)S(1)}, bf16[256,512]{1,0:T(8,128)(2,1)}, u32[]{:S(2)}) copy-start(bf16[256,512]{1,0:T(8,128)(2,1)} %own.1) | copy-start | bytes 786436
  2.9 9.9 %collective-permute-start = (bf16[512,512]{1,0:T(8,128)(2,1)S(1)}, bf16[512,512]{1,0:T(8,128)(2,1)S(1)}, u32[]{:S(2)}, u32[]{:S(2)}) collective-permute-start(bf16[512,512]{1,0:T(8,128)(2,1)S(1)} %shard_map.123), channel_id=1, source_target_pairs={{0,1},{1,0},{2,3},{3,2},{4,7},{5,6},{6,5},{7,4},{8,9},{9,8},{10,11... | collective-permute-start | bytes 1572872 | tf_op jit(solution)/shard_map/ppermute | solution.py:667
  12.9 5.6 %collective-permute-start.1 = (bf16[256,512]{1,0:T(8,128)(2,1)S(1)}, bf16[256,512]{1,0:T(8,128)(2,1)S(1)}, u32[]{:S(2)}, u32[]{:S(2)}) collective-permute-start(bf16[256,512]{1,0:T(8,128)(2,1)S(1)} %shard_map.124), channel_id=1, source_target_pairs={{0,3},{1,2},{2,1},{3,0},{4,5},{5,4},{6,7},{7,6},{8,11},{9,10},{10,... | collective-permute-start | bytes 786440 | tf_op jit(solution)/shard_map/ppermute | solution.py:667
  13.5 9.2 %collective-permute-start.4 = (bf16[256,512]{1,0:T(8,128)(2,1)S(1)}, bf16[256,512]{1,0:T(8,128)(2,1)S(1)}, u32[]{:S(2)}, u32[]{:S(2)}) collective-permute-start(bf16[256,512]{1,0:T(8,128)(2,1)S(1)} %copy-done), channel_id=1, source_target_pairs={{0,1},{1,0},{2,3},{3,2},{4,7},{5,6},{6,5},{7,4},{8,9},{9,8},{10,11... | collective-permute-start | bytes 786440 | tf_op jit(solution)/shard_map/ppermute | solution.py:667
  18.6 7.9 %collective-permute-start.2 = (bf16[256,512]{1,0:T(8,128)(2,1)S(1)}, bf16[256,512]{1,0:T(8,128)(2,1)S(1)}, u32[]{:S(2)}, u32[]{:S(2)}) collective-permute-start(bf16[256,512]{1,0:T(8,128)(2,1)S(1)} %shard_map.125.one.own), channel_id=1, source_target_pairs={{0,1},{1,0},{2,3},{3,2},{4,7},{5,6},{6,5},{7,4},{8,9},{9,8},{10,11... | collective-permute-start | bytes 786440 | tf_op jit(solution)/shard_map/ppermute | solution.py:667
  22.8 11.2 %collective-permute-start.5 = (bf16[512,512]{1,0:T(8,128)(2,1)S(1)}, bf16[512,512]{1,0:T(8,128)(2,1)S(1)}, u32[]{:S(2)}, u32[]{:S(2)}) collective-permute-start(bf16[512,512]{1,0:T(8,128)(2,1)S(1)} %shard_map.127), channel_id=1, source_target_pairs={{0,3},{1,2},{2,1},{3,0},{4,5},{5,4},{6,7},{7,6},{8,11},{9,10},{10,... | collective-permute-start | bytes 1572872 | tf_op jit(solution)/shard_map/ppermute | solution.py:667
  26.5 7.5 %copy-start.2 = (bf16[2048,4]{0,1:T(4,128)(2,1)S(1)}, bf16[2048,4]{0,1:T(4,128)(2,1)}, u32[]{:S(2)}) copy-start(bf16[2048,4]{0,1:T(4,128)(2,1)} %param.18) | copy-start | bytes 49156
  26.5 7.4 %copy-start.3 = (f32[2048]{0:T(1024)S(1)}, f32[2048]{0:T(1024)}, u32[]{:S(2)}) copy-start(f32[2048]{0:T(1024)} %param.16) | copy-start | bytes 24580
  26.6 7.4 %copy-start.4 = (f32[4]{0:T(128)S(1)}, f32[4]{0:T(128)}, u32[]{:S(2)}) copy-start(f32[4]{0:T(128)} %ceiling_ref.5) | copy-start | bytes 52
  26.6 15.6 %collective-permute-start.3 = (bf16[512,512]{1,0:T(8,128)(2,1)S(1)}, bf16[512,512]{1,0:T(8,128)(2,1)S(1)}, u32[]{:S(2)}, u32[]{:S(2)}) collective-permute-start(bf16[512,512]{1,0:T(8,128)(2,1)S(1)} %shard_map.126), channel_id=1, source_target_pairs={{0,3},{1,2},{2,1},{3,0},{4,5},{5,4},{6,7},{7,6},{8,11},{9,10},{10,... | collective-permute-start | bytes 1572872 | tf_op jit(solution)/shard_map/ppermute | solution.py:667
  40.1 2.1 %copy-start.6 = (f32[32]{0:T(128)S(1)}, f32[32]{0:T(128)}, u32[]{:S(2)}) copy-start(f32[32]{0:T(128)} %forget_ref.3) | copy-start | bytes 388
  42.2 25.9 %copy-start.7 = (s32[32]{0:T(128)S(1)}, s32[32]{0:T(128)}, u32[]{:S(2)}) copy-start(s32[32]{0:T(128)} %start_ref.1) | copy-start | bytes 388
  45.1 37.3 %copy-start.1 = (bf16[512,2048]{1,0:T(8,128)(2,1)S(1)}, bf16[512,2048]{1,0:T(8,128)(2,1)}, u32[]{:S(2)}) copy-start(bf16[512,2048]{1,0:T(8,128)(2,1)} %out_proj.3) | copy-start | bytes 6291460
  45.2 37.3 %copy-start.5 = (f32[4,128]{1,0:T(4,128)S(1)}, f32[4,128]{1,0:T(4,128)}, u32[]{:S(2)}) copy-start(f32[4,128]{1,0:T(4,128)} %out_gain.1) | copy-start | bytes 6148
  69.8 12.7 %all-to-all-start.1 = ((bf16[32,32,128]{2,1,0:T(8,128)(2,1)}), bf16[32,32,128]{2,1,0:T(8,128)(2,1)S(1)}, u32[]{:S(2)}, u32[]{:S(2)}) async-start(bf16[32,32,128]{2,1,0:T(8,128)(2,1)} %state_scan.1), calls=%async_computation.1 | async-start | bytes 524288 | tf_op jit(solution)/shard_map/all_to_all | solution.py:736
  85.3 7.7 %collective-permute-start.7 = (bf16[256,512]{1,0:T(8,128)(2,1)S(1)}, bf16[256,512]{1,0:T(8,128)(2,1)S(1)}, u32[]{:S(2)}, u32[]{:S(2)}) collective-permute-start(bf16[256,512]{1,0:T(8,128)(2,1)S(1)} %get-tuple-element.53), channel_id=1, source_target_pairs={{0,3},{1,0},{2,1},{3,2},{4,7},{5,4},{6,5},{7,6},{8,11},{9,8},{10,9... | collective-permute-start | bytes 786440 | tf_op jit(solution)/shard_map/ppermute | solution.py:671
  85.8 9.1 %collective-permute-start.9 = (bf16[256,512]{1,0:T(8,128)(2,1)S(1)}, bf16[256,512]{1,0:T(8,128)(2,1)S(1)}, u32[]{:S(2)}, u32[]{:S(2)}) collective-permute-start(bf16[256,512]{1,0:T(8,128)(2,1)S(1)} %get-tuple-element.56), channel_id=1, source_target_pairs={{0,1},{1,2},{2,3},{3,0},{4,5},{5,6},{6,7},{7,4},{8,9},{9,10},{10,1... | collective-permute-start | bytes 786440 | tf_op jit(solution)/shard_map/ppermute | solution.py:671
  88.3 11.6 %collective-permute-start.6 = (bf16[256,512]{1,0:T(8,128)(2,1)S(1)}, bf16[256,512]{1,0:T(8,128)(2,1)S(1)}, u32[]{:S(2)}, u32[]{:S(2)}) collective-permute-start(bf16[256,512]{1,0:T(8,128)(2,1)S(1)} %get-tuple-element.51), channel_id=1, source_target_pairs={{0,1},{1,2},{2,3},{3,0},{4,5},{5,6},{6,7},{7,4},{8,9},{9,10},{10,1... | collective-permute-start | bytes 786440 | tf_op jit(solution)/shard_map/ppermute | solution.py:671
  93.1 6.9 %collective-permute-start.8 = (bf16[256,512]{1,0:T(8,128)(2,1)S(1)}, bf16[256,512]{1,0:T(8,128)(2,1)S(1)}, u32[]{:S(2)}, u32[]{:S(2)}) collective-permute-start(bf16[256,512]{1,0:T(8,128)(2,1)S(1)} %add_convert_fusion.3), channel_id=1, source_target_pairs={{0,3},{1,0},{2,1},{3,2},{4,7},{5,4},{6,5},{7,6},{8,11},{9,8},{10,9... | collective-permute-start | bytes 786440 | tf_op jit(solution)/shard_map/ppermute | solution.py:671
  94.8 10.8 %collective-permute-start.11 = (bf16[256,512]{1,0:T(8,128)(2,1)S(1)}, bf16[256,512]{1,0:T(8,128)(2,1)S(1)}, u32[]{:S(2)}, u32[]{:S(2)}) collective-permute-start(bf16[256,512]{1,0:T(8,128)(2,1)S(1)} %get-tuple-element.57), channel_id=1, source_target_pairs={{0,3},{1,0},{2,1},{3,2},{4,7},{5,4},{6,5},{7,6},{8,11},{9,8},{10,9... | collective-permute-start | bytes 786440 | tf_op jit(solution)/shard_map/ppermute | solution.py:671
  94.9 10.7 %collective-permute-start.10 = (bf16[256,512]{1,0:T(8,128)(2,1)S(1)}, bf16[256,512]{1,0:T(8,128)(2,1)S(1)}, u32[]{:S(2)}, u32[]{:S(2)}) collective-permute-start(bf16[256,512]{1,0:T(8,128)(2,1)S(1)} %add_convert_fusion.1), channel_id=1, source_target_pairs={{0,1},{1,2},{2,3},{3,0},{4,5},{5,6},{6,7},{7,4},{8,9},{9,10},{10,1... | collective-permute-start | bytes 786440 | tf_op jit(solution)/shard_map/ppermute | solution.py:671

commit v7 on v6

--- a/solution.py
+++ b/solution.py
@@ -555,15 +555,15 @@
 
 def scan_kernel(start_ref, states, out, decay, image_at):
     count = start_ref.shape[0]
-    for kind in range(2):
-        spans = states[:, 32:40, :].astype(F32)
-        span = spans[:, 2 * kind : 2 * kind + 1, :] + spans[:, 2 * kind + 1 : 2 * kind + 2, :]
-        decay[:, kind] = jnp.broadcast_to(jnp.exp(span), (count, 16, HEAD_WIDTH))
     for position in range(2 * count):
         image_at[position] = -1
     for image in range(count):
         image_at[lax.shift_right_logical(start_ref[image], 1)] = image
-    carry = jnp.zeros((16, HEAD_WIDTH), F32)
+    spans = states[:, 32:40, :].astype(F32)
+    for kind in range(2):
+        span = spans[:, 2 * kind : 2 * kind + 1, :] + spans[:, 2 * kind + 1 : 2 * kind + 2, :]
+        decay[:, kind] = jnp.broadcast_to(jnp.exp(span), (count, 8, HEAD_WIDTH))
+    upper = lower = jnp.zeros((8, HEAD_WIDTH), F32)
     texts = jnp.int32(0)
     for position in range(2 * count):
         found = image_at[position]
@@ -571,8 +571,11 @@
         source = jnp.where(found >= 0, found, jnp.minimum(texts, count - 1))
         texts += 1 - kind
         rows = pl.ds(pl.multiple_of(kind * 16, 16), 16)
-        out[source, rows, :] = carry.astype(BF16)
-        carry = decay[source, kind] * carry + states[source, rows, :].astype(F32)
+        out[source, rows, :] = jnp.concatenate([upper, lower], axis=0).astype(BF16)
+        state = states[source, rows, :].astype(F32)
+        factor = decay[source, kind]
+        upper = factor * upper + state[:8]
+        lower = factor * lower + state[8:]
 
 
 def scan_call(starts, states):
@@ -583,7 +586,7 @@
         in_specs=[SMEM, VMEM],
         out_specs=VMEM,
         scratch_shapes=[
-            pltpu.VMEM((count, 2, 16, HEAD_WIDTH), F32),
+            pltpu.VMEM((count, 2, 8, HEAD_WIDTH), F32),
             pltpu.SMEM((2 * count,), jnp.int32),
         ],
         compiler_params=limit(6),

time: 108 us -> 108 us (level)
  no operation moved by 1% of the time
where the time goes in v7:
time: 108 us; the launch traced here: 106 us
  Pallas kernels  30.8 us (29%)
  waiting for transfers between devices  30.5 us (28%)
  blocking collectives  22.9 us (21%)
  starting transfers between devices  19.4 us (18%)
  other arithmetic  1.84 us (2%)
    all_to_all x1, blocking collectives, steps(): slices = lax.all_to_all(states, SEQ, 0, 0, tiled=True)  22.9 us
    ppermute x6, waiting for transfers between devices, moved(): return lax.ppermute(array, ('seq_2', 'head'), pairs)  14.1 us
    ppermute x6, waiting for transfers between devices, passed(): return lax.ppermute(array, 'head', [(i, (i + step) % 4) for i in range(4)])  12.9 us
    ppermute x6, starting transfers between devices, moved(): return lax.ppermute(array, ('seq_2', 'head'), pairs)  10.8 us
    pallas_call x1, Pallas kernels, text_call(): pl.pallas_call(text_kernel, grid=(1,), out_shape=outs, in_specs=[SMEM, SM...  6.06 us
    pallas_call x1, Pallas kernels, image_attend_call(): pl.pallas_call(image_attend_kernel, grid=(1,), out_shape=outs, in_specs=[...  5.41 us
    ppermute x6, starting transfers between devices, passed(): return lax.ppermute(array, 'head', [(i, (i + step) % 4) for i in range(4)])  4.85 us
    pallas_call x2, Pallas kernels, adapter_call(): pl.pallas_call(kernel, out_shape=outs, in_specs=[SMEM, HBM, HBM], out_spe...  4.39 us
  transfers between devices with their start and end apart: 13, of which 8 were waited for; matrix products, arithmetic and copies ran while one was open for 1% of the time, Pallas kernels for 20%

profile of v7, /device:TPU:1, one launch (start us, length us, event | category | flops | bytes accessed | tf_op | source)
XLA Modules:
  0.0 106.5 jit_solution(12437141697132906219)
XLA Ops:
  0.7 0.1 stack.23.place_ref
  0.7 2.2 %shard_map.123 = bf16[512,512]{1,0:T(8,128)(2,1)S(1)} custom-call(s32[5]{0:T(128)S(1)} %stack.23.place_ref, bf16[1,288,256]{2,1,0:T(8,128)(2,1)} %bitcast.16, bf16[288,2048]{1,0:T(8,128)(2,1)} %adapter_ref.3), custom_call_target="tpu_custom_call" | custom-call | flops 150994944 | bytes 589824 | tf_op jit(solution)/shard_map/pallas_call | solution.py:81
  2.9 3.4 %collective-permute-start = (bf16[512,512]{1,0:T(8,128)(2,1)S(1)}, bf16[512,512]{1,0:T(8,128)(2,1)S(1)}, u32[]{:S(2)}, u32[]{:S(2)}) collective-permute-start(bf16[512,512]{1,0:T(8,128)(2,1)S(1)} %shard_map.123), channel_id=1, source_target_pairs={{0,1},{1,0},{2,3},{3,2},{4,7},{5,6},{6,5},{7,4},{8,9},{9,8},{10,11... | collective-permute-start | bytes 1572872 | tf_op jit(solution)/shard_map/ppermute | solution.py:670
  6.3 2.2 %shard_map.122.stay = f32[2,256,512]{2,1,0:T(8,128)S(1)} custom-call(s32[5]{0:T(128)S(1)} %stack.23.place_ref, bf16[1,288,256]{2,1,0:T(8,128)(2,1)} %bitcast.17, bf16[288,2048]{1,0:T(8,128)(2,1)} %adapter_ref.3), custom_call_target="tpu_custom_call" | custom-call | flops 150994944 | bytes 589824 | tf_op jit(solution)/shard_map/pallas_call | solution.py:81
  8.5 4.4 %collective-permute-done.arrived = bf16[512,512]{1,0:T(8,128)(2,1)S(1)} collective-permute-done((bf16[512,512]{1,0:T(8,128)(2,1)S(1)}, bf16[512,512]{1,0:T(8,128)(2,1)S(1)}, u32[]{:S(2)}, u32[]{:S(2)}) %collective-permute-start) | collective-permute-done | bytes 524320 | tf_op jit(solution)/shard_map/ppermute | solution.py:670
  12.9 0.6 collective-permute-start.1
  13.5 2.3 %collective-permute-start.4 = (bf16[256,512]{1,0:T(8,128)(2,1)S(1)}, bf16[256,512]{1,0:T(8,128)(2,1)S(1)}, u32[]{:S(2)}, u32[]{:S(2)}) collective-permute-start(bf16[256,512]{1,0:T(8,128)(2,1)S(1)} %copy-done), channel_id=1, source_target_pairs={{0,1},{1,0},{2,3},{3,2},{4,7},{5,6},{6,5},{7,4},{8,9},{9,8},{10,11... | collective-permute-start | bytes 786440 | tf_op jit(solution)/shard_map/ppermute | solution.py:670
  15.8 2.7 %collective-permute-done.1.last = bf16[256,512]{1,0:T(8,128)(2,1)S(1)} collective-permute-done((bf16[256,512]{1,0:T(8,128)(2,1)S(1)}, bf16[256,512]{1,0:T(8,128)(2,1)S(1)}, u32[]{:S(2)}, u32[]{:S(2)}) %collective-permute-start.1) | collective-permute-done | bytes 262176 | tf_op jit(solution)/shard_map/ppermute | solution.py:670
  18.5 0.1 shard_map.125.one.own
  18.6 4.1 %collective-permute-start.2 = (bf16[256,512]{1,0:T(8,128)(2,1)S(1)}, bf16[256,512]{1,0:T(8,128)(2,1)S(1)}, u32[]{:S(2)}, u32[]{:S(2)}) collective-permute-start(bf16[256,512]{1,0:T(8,128)(2,1)S(1)} %shard_map.125.one.own), channel_id=1, source_target_pairs={{0,1},{1,0},{2,3},{3,2},{4,7},{5,6},{6,5},{7,4},{8,9},{9,8},{10,11... | collective-permute-start | bytes 786440 | tf_op jit(solution)/shard_map/ppermute | solution.py:670
  22.7 0.0 collective-permute-done.4.two.first
  22.8 0.3 collective-permute-start.5
  23.1 3.4 %collective-permute-done.2.two.first = bf16[256,512]{1,0:T(8,128)(2,1)S(1)} collective-permute-done((bf16[256,512]{1,0:T(8,128)(2,1)S(1)}, bf16[256,512]{1,0:T(8,128)(2,1)S(1)}, u32[]{:S(2)}, u32[]{:S(2)}) %collective-permute-start.2) | collective-permute-done | bytes 262176 | tf_op jit(solution)/shard_map/ppermute | solution.py:670
  26.5 0.0 copy-start.2
  26.5 0.0 copy-start.3
  26.6 0.0 copy-start.4
  26.6 0.1 collective-permute-start.3
  26.7 3.7 %relay.1.weight = bf16[4,2048,512]{2,1,0:T(8,128)(2,1)S(1)} custom-call(bf16[2048,4,512]{2,1,0:T(4,128)(2,1)} %source.1), custom_call_target="tpu_custom_call" | custom-call | bytes 8388608 | tf_op jit(solution)/shard_map/relay/pallas_call | solution.py:435
  30.4 3.6 %collective-permute-done.5.others = bf16[512,512]{1,0:T(8,128)(2,1)S(1)} collective-permute-done((bf16[512,512]{1,0:T(8,128)(2,1)S(1)}, bf16[512,512]{1,0:T(8,128)(2,1)S(1)}, u32[]{:S(2)}, u32[]{:S(2)}) %collective-permute-start.5) | collective-permute-done | bytes 524320 | tf_op jit(solution)/shard_map/ppermute | solution.py:670
  34.0 6.1 %text_unit.1 = (bf16[256,512]{1,0:T(8,128)(2,1)}, bf16[256,512]{1,0:T(8,128)(2,1)}, f32[256,512]{1,0:T(8,128)}, bf16[32,16,128]{2,1,0:T(8,128)(2,1)S(1)}, f32[4,...) custom-call(s32[5]{0:T(128)S(1)} %stack.23.place_ref, f32[4]{0:T(128)S(1)} %copy-done.4, bf16[256,512]{1,0:T(8,128)(2,1)S(1)} %copy-done, ...), custom_call_target="tpu_custom_call" | custom-call | flops 2147483648 | bytes 8388608 | tf_op jit(solution)/shard_map/text_unit/pallas_call | solution.py:464
  40.1 0.0 copy-start.6
  40.1 2.1 %image_near.1 = (bf16[2,256,512]{2,1,0:T(8,128)(2,1)}, f32[2,256,512]{2,1,0:T(8,128)S(1)}, f32[256,128]{1,0:T(8,128)S(1)}, f32[256,1]{1,0:T(8,128)S(1)}) custom-call(s32[5]{0:T(128)S(1)} %stack.23.place_ref, bf16[256,512]{1,0:T(8,128)(2,1)S(1)} %shard_map.125.one.own, bf16[256,512]{1,0:T(8,128)(2,1)S(1)} %collective-permute-done.2.two.first, ...), custom_call_target="tpu_custom_call" | custom-call | flops 536870912 | bytes 2097152 | tf_op jit(solution)/shard_map/image_near/pallas_call | solution.py:491
  42.2 0.0 collective-permute-done.3.others
  42.2 0.0 copy-start.7
  42.2 2.9 %image_state.1 = (bf16[2,256,512]{2,1,0:T(8,128)(2,1)}, bf16[2,256,512]{2,1,0:T(8,128)(2,1)}, f32[256,1]{1,0:T(8,128)S(1)}, f32[256,4]{1,0:T(8,128)S(1)}, f32[4,...) custom-call(s32[5]{0:T(128)S(1)} %stack.23.place_ref, f32[4]{0:T(128)S(1)} %copy-done.4, f32[32]{0:T(128)S(1)} %copy-done.6, ...), custom_call_target="tpu_custom_call" | custom-call | flops 268435456 | bytes 1048576 | tf_op jit(solution)/shard_map/image_state/pallas_call | solution.py:513
  45.1 0.0 copy-start.1
  45.2 0.0 copy-start.5
  45.2 22.9 %all_to_all.10.states = bf16[32,40,128]{2,1,0:T(8,128)(2,1)S(1)} all-to-all(bf16[32,40,128]{2,1,0:T(8,128)(2,1)S(1)} %get-tuple-element.35), channel_id=1, replica_groups=mesh['seq_0'=4,'seq_1'=4,'seq_2'=2,'head'=4] {'seq_0','seq_1','seq_2'}, dimensions={0} | all-to-all | bytes 655360 | tf_op jit(solution)/shard_map/all_to_all | solution.py:735
  68.1 1.7 %state_scan.1 = bf16[32,32,128]{2,1,0:T(8,128)(2,1)} custom-call(s32[32]{0:T(128)S(1)} %copy-done.7, bf16[32,40,128]{2,1,0:T(8,128)(2,1)S(1)} %all_to_all.10.states), custom_call_target="tpu_custom_call" | custom-call | tf_op jit(solution)/shard_map/state_scan/pallas_call | solution.py:583
  69.8 3.8 %all-to-all-start.1 = ((bf16[32,32,128]{2,1,0:T(8,128)(2,1)}), bf16[32,32,128]{2,1,0:T(8,128)(2,1)S(1)}, u32[]{:S(2)}, u32[]{:S(2)}) async-start(bf16[32,32,128]{2,1,0:T(8,128)(2,1)} %state_scan.1), calls=%async_computation.1 | async-start | bytes 524288 | tf_op jit(solution)/shard_map/all_to_all | solution.py:739
  73.6 5.4 %image_attend.1 = (bf16[256,512]{1,0:T(8,128)(2,1)}, bf16[256,512]{1,0:T(8,128)(2,1)}, f32[256,512]{1,0:T(8,128)}) custom-call(s32[5]{0:T(128)S(1)} %stack.23.place_ref, f32[4]{0:T(128)S(1)} %copy-done.4, f32[32]{0:T(128)S(1)} %copy-done.6, bf16[2,256,512]{2,1,0:T(8,128)(2,1)} %get-tuple-element.39.near_ref, bf16[2,256,512]{2,1,0:T(8,128)(2,1)} %get-tuple-element.40.far_ref, ...), custom_call_target="tpu_custom_call" | custom-call | flops 1073741824 | bytes 4194304 | tf_op jit(solution)/shard_map/image_attend/pallas_call | solution.py:537
  79.0 3.5 %all-to-all-done.1.entering = bf16[32,32,128]{2,1,0:T(8,128)(2,1)S(1)} async-done(((bf16[32,32,128]{2,1,0:T(8,128)(2,1)}), bf16[32,32,128]{2,1,0:T(8,128)(2,1)S(1)}, u32[]{:S(2)}, u32[]{:S(2)}) %all-to-all-start.1) | async-done | bytes 262176 | tf_op jit(solution)/shard_map/all_to_all | solution.py:739
  82.5 2.8 %gate_far.1 = (bf16[256,512]{1,0:T(8,128)(2,1)S(1)}, bf16[256,512]{1,0:T(8,128)(2,1)S(1)}, bf16[512,512]{1,0:T(8,128)(2,1)S(1)}) custom-call(s32[5]{0:T(128)S(1)} %stack.23.place_ref, bf16[32,32,128]{2,1,0:T(8,128)(2,1)S(1)} %all-to-all-done.1.entering, f32[4,128]{1,0:T(4,128)S(1)} %copy-done.5, bf16[512,2048]{1,0:T(8,128)(2,1)S(1)} %copy-done.1, ...), custom_call_target="tpu_custom_call" | custom-call | tf_op jit(solution)/shard_map/gate_far/pallas_call | solution.py:629
  85.3 0.5 collective-permute-start.7
  85.8 1.0 collective-permute-start.9
  86.8 1.5 %near_blocks.1 = (bf16[256,512]{1,0:T(8,128)(2,1)S(1)}, bf16[256,512]{1,0:T(8,128)(2,1)S(1)}, bf16[256,512]{1,0:T(8,128)(2,1)S(1)}, bf16[256,512]{1,0:T(8,128)(2...) custom-call(s32[5]{0:T(128)S(1)} %stack.23.place_ref, bf16[512,512]{1,0:T(8,128)(2,1)S(1)} %get-tuple-element.49.gated, ...), custom_call_target="tpu_custom_call" | custom-call | flops 805306368 | bytes 1572864 | tf_op jit(solution)/shard_map/near_blocks/pallas_call | solution.py:653
  88.4 0.1 collective-permute-start.6
  88.4 4.6 %collective-permute-done.7 = bf16[256,512]{1,0:T(8,128)(2,1)S(1)} collective-permute-done((bf16[256,512]{1,0:T(8,128)(2,1)S(1)}, bf16[256,512]{1,0:T(8,128)(2,1)S(1)}, u32[]{:S(2)}, u32[]{:S(2)}) %collective-permute-start.7) | collective-permute-done | bytes 262176 | tf_op jit(solution)/shard_map/ppermute | solution.py:674
  93.0 0.1 add_convert_fusion.3
  93.1 1.7 %collective-permute-start.8 = (bf16[256,512]{1,0:T(8,128)(2,1)S(1)}, bf16[256,512]{1,0:T(8,128)(2,1)S(1)}, u32[]{:S(2)}, u32[]{:S(2)}) collective-permute-start(bf16[256,512]{1,0:T(8,128)(2,1)S(1)} %add_convert_fusion.3), channel_id=1, source_target_pairs={{0,3},{1,0},{2,1},{3,2},{4,7},{5,4},{6,5},{7,6},{8,11},{9,8},{10,9... | collective-permute-start | bytes 786440 | tf_op jit(solution)/shard_map/ppermute | solution.py:674
  94.8 0.1 collective-permute-start.11
  94.9 0.1 add_convert_fusion.1
  95.0 1.5 %collective-permute-start.10 = (bf16[256,512]{1,0:T(8,128)(2,1)S(1)}, bf16[256,512]{1,0:T(8,128)(2,1)S(1)}, u32[]{:S(2)}, u32[]{:S(2)}) collective-permute-start(bf16[256,512]{1,0:T(8,128)(2,1)S(1)} %add_convert_fusion.1), channel_id=1, source_target_pairs={{0,1},{1,2},{2,3},{3,0},{4,5},{5,6},{6,7},{7,4},{8,9},{9,10},{10,1... | collective-permute-start | bytes 786440 | tf_op jit(solution)/shard_map/ppermute | solution.py:674
  96.4 3.6 %collective-permute-done.6 = bf16[256,512]{1,0:T(8,128)(2,1)S(1)} collective-permute-done((bf16[256,512]{1,0:T(8,128)(2,1)S(1)}, bf16[256,512]{1,0:T(8,128)(2,1)S(1)}, u32[]{:S(2)}, u32[]{:S(2)}) %collective-permute-start.6) | collective-permute-done | bytes 262176 | tf_op jit(solution)/shard_map/ppermute | solution.py:674
  100.0 0.9 fusion
  100.9 4.7 %collective-permute-done.11 = bf16[256,512]{1,0:T(8,128)(2,1)S(1)} collective-permute-done((bf16[256,512]{1,0:T(8,128)(2,1)S(1)}, bf16[256,512]{1,0:T(8,128)(2,1)S(1)}, u32[]{:S(2)}, u32[]{:S(2)}) %collective-permute-start.11) | collective-permute-done | bytes 262176 | tf_op jit(solution)/shard_map/ppermute | solution.py:674
  105.6 0.0 collective-permute-done.10
  105.6 0.9 add_convert_fusion
  (14 shorter events, 0.1 us)
Async XLA Ops:
  0.6 12.9 %copy-start = (bf16[256,512]{1,0:T(8,128)(2,1)S(1)}, bf16[256,512]{1,0:T(8,128)(2,1)}, u32[]{:S(2)}) copy-start(bf16[256,512]{1,0:T(8,128)(2,1)} %own.1) | copy-start | bytes 786436
  2.9 9.9 %collective-permute-start = (bf16[512,512]{1,0:T(8,128)(2,1)S(1)}, bf16[512,512]{1,0:T(8,128)(2,1)S(1)}, u32[]{:S(2)}, u32[]{:S(2)}) collective-permute-start(bf16[512,512]{1,0:T(8,128)(2,1)S(1)} %shard_map.123), channel_id=1, source_target_pairs={{0,1},{1,0},{2,3},{3,2},{4,7},{5,6},{6,5},{7,4},{8,9},{9,8},{10,11... | collective-permute-start | bytes 1572872 | tf_op jit(solution)/shard_map/ppermute | solution.py:670
  12.9 5.6 %collective-permute-start.1 = (bf16[256,512]{1,0:T(8,128)(2,1)S(1)}, bf16[256,512]{1,0:T(8,128)(2,1)S(1)}, u32[]{:S(2)}, u32[]{:S(2)}) collective-permute-start(bf16[256,512]{1,0:T(8,128)(2,1)S(1)} %shard_map.124), channel_id=1, source_target_pairs={{0,3},{1,2},{2,1},{3,0},{4,5},{5,4},{6,7},{7,6},{8,11},{9,10},{10,... | collective-permute-start | bytes 786440 | tf_op jit(solution)/shard_map/ppermute | solution.py:670
  13.5 9.2 %collective-permute-start.4 = (bf16[256,512]{1,0:T(8,128)(2,1)S(1)}, bf16[256,512]{1,0:T(8,128)(2,1)S(1)}, u32[]{:S(2)}, u32[]{:S(2)}) collective-permute-start(bf16[256,512]{1,0:T(8,128)(2,1)S(1)} %copy-done), channel_id=1, source_target_pairs={{0,1},{1,0},{2,3},{3,2},{4,7},{5,6},{6,5},{7,4},{8,9},{9,8},{10,11... | collective-permute-start | bytes 786440 | tf_op jit(solution)/shard_map/ppermute | solution.py:670
  18.6 7.9 %collective-permute-start.2 = (bf16[256,512]{1,0:T(8,128)(2,1)S(1)}, bf16[256,512]{1,0:T(8,128)(2,1)S(1)}, u32[]{:S(2)}, u32[]{:S(2)}) collective-permute-start(bf16[256,512]{1,0:T(8,128)(2,1)S(1)} %shard_map.125.one.own), channel_id=1, source_target_pairs={{0,1},{1,0},{2,3},{3,2},{4,7},{5,6},{6,5},{7,4},{8,9},{9,8},{10,11... | collective-permute-start | bytes 786440 | tf_op jit(solution)/shard_map/ppermute | solution.py:670
  22.8 11.2 %collective-permute-start.5 = (bf16[512,512]{1,0:T(8,128)(2,1)S(1)}, bf16[512,512]{1,0:T(8,128)(2,1)S(1)}, u32[]{:S(2)}, u32[]{:S(2)}) collective-permute-start(bf16[512,512]{1,0:T(8,128)(2,1)S(1)} %shard_map.127), channel_id=1, source_target_pairs={{0,3},{1,2},{2,1},{3,0},{4,5},{5,4},{6,7},{7,6},{8,11},{9,10},{10,... | collective-permute-start | bytes 1572872 | tf_op jit(solution)/shard_map/ppermute | solution.py:670
  26.5 7.5 %copy-start.2 = (bf16[2048,4]{0,1:T(4,128)(2,1)S(1)}, bf16[2048,4]{0,1:T(4,128)(2,1)}, u32[]{:S(2)}) copy-start(bf16[2048,4]{0,1:T(4,128)(2,1)} %param.18) | copy-start | bytes 49156
  26.5 7.4 %copy-start.3 = (f32[2048]{0:T(1024)S(1)}, f32[2048]{0:T(1024)}, u32[]{:S(2)}) copy-start(f32[2048]{0:T(1024)} %param.16) | copy-start | bytes 24580
  26.6 7.4 %copy-start.4 = (f32[4]{0:T(128)S(1)}, f32[4]{0:T(128)}, u32[]{:S(2)}) copy-start(f32[4]{0:T(128)} %ceiling_ref.5) | copy-start | bytes 52
  26.6 15.6 %collective-permute-start.3 = (bf16[512,512]{1,0:T(8,128)(2,1)S(1)}, bf16[512,512]{1,0:T(8,128)(2,1)S(1)}, u32[]{:S(2)}, u32[]{:S(2)}) collective-permute-start(bf16[512,512]{1,0:T(8,128)(2,1)S(1)} %shard_map.126), channel_id=1, source_target_pairs={{0,3},{1,2},{2,1},{3,0},{4,5},{5,4},{6,7},{7,6},{8,11},{9,10},{10,... | collective-permute-start | bytes 1572872 | tf_op jit(solution)/shard_map/ppermute | solution.py:670
  40.1 2.1 %copy-start.6 = (f32[32]{0:T(128)S(1)}, f32[32]{0:T(128)}, u32[]{:S(2)}) copy-start(f32[32]{0:T(128)} %forget_ref.3) | copy-start | bytes 388
  42.2 25.9 %copy-start.7 = (s32[32]{0:T(128)S(1)}, s32[32]{0:T(128)}, u32[]{:S(2)}) copy-start(s32[32]{0:T(128)} %start_ref.1) | copy-start | bytes 388
  45.1 37.3 %copy-start.1 = (bf16[512,2048]{1,0:T(8,128)(2,1)S(1)}, bf16[512,2048]{1,0:T(8,128)(2,1)}, u32[]{:S(2)}) copy-start(bf16[512,2048]{1,0:T(8,128)(2,1)} %out_proj.3) | copy-start | bytes 6291460
  45.2 37.3 %copy-start.5 = (f32[4,128]{1,0:T(4,128)S(1)}, f32[4,128]{1,0:T(4,128)}, u32[]{:S(2)}) copy-start(f32[4,128]{1,0:T(4,128)} %out_gain.1) | copy-start | bytes 6148
  69.8 12.7 %all-to-all-start.1 = ((bf16[32,32,128]{2,1,0:T(8,128)(2,1)}), bf16[32,32,128]{2,1,0:T(8,128)(2,1)S(1)}, u32[]{:S(2)}, u32[]{:S(2)}) async-start(bf16[32,32,128]{2,1,0:T(8,128)(2,1)} %state_scan.1), calls=%async_computation.1 | async-start | bytes 524288 | tf_op jit(solution)/shard_map/all_to_all | solution.py:739
  85.3 7.7 %collective-permute-start.7 = (bf16[256,512]{1,0:T(8,128)(2,1)S(1)}, bf16[256,512]{1,0:T(8,128)(2,1)S(1)}, u32[]{:S(2)}, u32[]{:S(2)}) collective-permute-start(bf16[256,512]{1,0:T(8,128)(2,1)S(1)} %get-tuple-element.53), channel_id=1, source_target_pairs={{0,3},{1,0},{2,1},{3,2},{4,7},{5,4},{6,5},{7,6},{8,11},{9,8},{10,9... | collective-permute-start | bytes 786440 | tf_op jit(solution)/shard_map/ppermute | solution.py:674
  85.8 9.1 %collective-permute-start.9 = (bf16[256,512]{1,0:T(8,128)(2,1)S(1)}, bf16[256,512]{1,0:T(8,128)(2,1)S(1)}, u32[]{:S(2)}, u32[]{:S(2)}) collective-permute-start(bf16[256,512]{1,0:T(8,128)(2,1)S(1)} %get-tuple-element.56), channel_id=1, source_target_pairs={{0,1},{1,2},{2,3},{3,0},{4,5},{5,6},{6,7},{7,4},{8,9},{9,10},{10,1... | collective-permute-start | bytes 786440 | tf_op jit(solution)/shard_map/ppermute | solution.py:674
  88.4 11.6 %collective-permute-start.6 = (bf16[256,512]{1,0:T(8,128)(2,1)S(1)}, bf16[256,512]{1,0:T(8,128)(2,1)S(1)}, u32[]{:S(2)}, u32[]{:S(2)}) collective-permute-start(bf16[256,512]{1,0:T(8,128)(2,1)S(1)} %get-tuple-element.51), channel_id=1, source_target_pairs={{0,1},{1,2},{2,3},{3,0},{4,5},{5,6},{6,7},{7,4},{8,9},{9,10},{10,1... | collective-permute-start | bytes 786440 | tf_op jit(solution)/shard_map/ppermute | solution.py:674
  93.1 6.9 %collective-permute-start.8 = (bf16[256,512]{1,0:T(8,128)(2,1)S(1)}, bf16[256,512]{1,0:T(8,128)(2,1)S(1)}, u32[]{:S(2)}, u32[]{:S(2)}) collective-permute-start(bf16[256,512]{1,0:T(8,128)(2,1)S(1)} %add_convert_fusion.3), channel_id=1, source_target_pairs={{0,3},{1,0},{2,1},{3,2},{4,7},{5,4},{6,5},{7,6},{8,11},{9,8},{10,9... | collective-permute-start | bytes 786440 | tf_op jit(solution)/shard_map/ppermute | solution.py:674
  94.8 10.8 %collective-permute-start.11 = (bf16[256,512]{1,0:T(8,128)(2,1)S(1)}, bf16[256,512]{1,0:T(8,128)(2,1)S(1)}, u32[]{:S(2)}, u32[]{:S(2)}) collective-permute-start(bf16[256,512]{1,0:T(8,128)(2,1)S(1)} %get-tuple-element.57), channel_id=1, source_target_pairs={{0,3},{1,0},{2,1},{3,2},{4,7},{5,4},{6,5},{7,6},{8,11},{9,8},{10,9... | collective-permute-start | bytes 786440 | tf_op jit(solution)/shard_map/ppermute | solution.py:674
  95.0 10.7 %collective-permute-start.10 = (bf16[256,512]{1,0:T(8,128)(2,1)S(1)}, bf16[256,512]{1,0:T(8,128)(2,1)S(1)}, u32[]{:S(2)}, u32[]{:S(2)}) collective-permute-start(bf16[256,512]{1,0:T(8,128)(2,1)S(1)} %add_convert_fusion.1), channel_id=1, source_target_pairs={{0,1},{1,2},{2,3},{3,0},{4,5},{5,6},{6,7},{7,4},{8,9},{9,10},{10,1... | collective-permute-start | bytes 786440 | tf_op jit(solution)/shard_map/ppermute | solution.py:674
